TPU v7x, 32 devices: a whole 2x2x4 slice. The times are simulated.
32 devices in a mesh: dp: 2 (over x), seq: 4 (over z), tensor: 4 (over y, core).
Axes of the slice: x: 2, y: 2, z: 4, core: 2. Of those that a mesh axis runs over, the one named last changes fastest.
Arguments:
- tokens: bfloat16 [4, 2048, 768], P('dp', 'seq'), may hold values from -6 to 6
- cotangent: bfloat16 [4, 2048, 768], P('dp', 'seq'), may hold values from -6 to 6
- segments: int32 [4, 2048], P('dp'), may hold values from 0 to 12, as said below
- parents: int32 [4, 13], P('dp'), may hold values from 0 to 4, as said below
- routes: int32 [4, 2048, 2], P('dp', 'seq'), may hold values from 0 to 7, all different within a row; in each aligned block of 512 rows (0 to 511, 512 to 1023, ..., all dimensions but the last counted through in order) at most 192 rows name the same one
- norm_gains: bfloat16 [2, 768], P(None, ('dp', 'seq')), may hold values from 0.5 to 1.5
- project: bfloat16 [3, 768, 768], P(None, ('dp', 'seq'), 'tensor'), may hold values from -0.21875 to 0.21875
- mixing: bfloat16 [768, 768], P('tensor', ('dp', 'seq')), may hold values from -1.5 to 1.5
- router: bfloat16 [768, 8], P(('dp', 'seq')), may hold values from -0.21875 to 0.21875
- expander: bfloat16 [8, 2, 768, 2048], P(None, None, ('dp', 'seq'), 'tensor'), may hold values from -0.21875 to 0.21875
- reducer: bfloat16 [8, 2048, 768], P(None, 'tensor', ('dp', 'seq')), may hold values from -1 to 1
- spreader: bfloat16 [2, 768, 2048], P(None, ('dp', 'seq'), 'tensor'), may hold values from -0.21875 to 0.21875
- collector: bfloat16 [2048, 768], P('tensor', ('dp', 'seq')), may hold values from -0.25 to 0.25
Outputs:
- output: bfloat16 [4, 2048, 768], P('dp', 'seq')
- input_grad: bfloat16 [4, 2048, 768], P('dp', 'seq')
- gain_grad: float32 [2, 768], P(None, ('dp', 'seq'))
- project_grad: float32 [3, 768, 768], P(None, ('dp', 'seq'), 'tensor')
- mixing_grad: float32 [768, 768], P('tensor', ('dp', 'seq'))
- router_grad: float32 [768, 8], P(('dp', 'seq'))
- expander_grad: float32 [8, 2, 768, 2048], P(None, None, ('dp', 'seq'), 'tensor')
- reducer_grad: float32 [8, 2048, 768], P(None, 'tensor', ('dp', 'seq'))
- spreader_grad: float32 [2, 768, 2048], P(None, ('dp', 'seq'), 'tensor')
- collector_grad: float32 [2048, 768], P('tensor', ('dp', 'seq'))
Inputs may be any that keep to these rules, and one draw needn't show every extreme that they name: `segments`: along each tree the segment numbers never fall; segment 0, the trunk, holds the first quarter to half of the tree's 2048 tokens; any other segment may be empty. `parents`: segments 0 to 4 have parent 0 (the trunk is its own parent; 1 to 4 are branches); segments 5 to 12 are leaves whose parent is one of the branches 1 to 4. `routes`: the 2 experts of a token differ; among the 512 tokens that one device holds of one tree, no expert is named more than 192 times, and in some such block one expert is named exactly 192 times.
All inputs are finite; a program needn't handle non-finite values.
Results may differ from a plain program's by a relative error of at most 0.025.
Values may be sent and summed in bfloat16 or wider, within the bound.
No kernel may reach another device: no remote copies, remote signals or barrier semaphores. Data moves between devices by JAX's collectives and lax.ppermute only.
A program may use at most 320 MiB of HBM per device.

v0:
```python
import math

import jax
import jax.numpy as jnp
from jax import lax
from jax.sharding import PartitionSpec as P

HEAD_DIM = 64
EXPERTS = 8
CAP = 192
QB = 512


epsilon = 1e-05
theta = 10000.0
highest = lax.Precision.HIGHEST


def ancestry(parents):
    labels = jnp.arange(parents.shape[0], dtype=jnp.int32)
    grandparent = jnp.take(parents, parents)
    itself = labels[:, None] == labels[None, :]
    return (
        itself | (parents[:, None] == labels[None, :]) | (grandparent[:, None] == labels[None, :])
    )


def positions(segments, table):
    labels = jnp.arange(table.shape[0], dtype=jnp.int32)
    member = (segments[:, None] == labels[None, :]).astype(jnp.int32)
    lengths = jnp.sum(member, 0)
    offsets = jnp.cumsum(lengths) - lengths
    ancestral = jnp.sum(table.astype(jnp.int32) * lengths[None, :], 1) - lengths
    moving = ancestral - offsets
    return jnp.arange(segments.shape[0], dtype=jnp.int32) + jnp.sum(member * moving[None, :], 1)


def visible(row_segments, row_index, key_segments, key_index, table):
    labels = jnp.arange(table.shape[0], dtype=jnp.int32)
    member_rows = (row_segments[:, None] == labels[None, :]).astype(jnp.bfloat16)
    member_keys = (key_segments[:, None] == labels[None, :]).astype(jnp.bfloat16)
    reach = jnp.dot(member_rows, table.astype(jnp.bfloat16), preferred_element_type=jnp.float32)
    hits = jnp.einsum(
        "bs,ls->bl", reach.astype(jnp.bfloat16), member_keys, preferred_element_type=jnp.float32
    )
    return (hits > 0.5) & (key_index[None, :] <= row_index[:, None])


def turn(field, place, backward):
    half = field.shape[-1] // 2
    rates = jnp.exp(-math.log(theta) * 2.0 * jnp.arange(half, dtype=jnp.float32) / field.shape[-1])
    angle = place[:, None] * rates[None, :]
    cosine = jnp.cos(angle)[:, None, :]
    sine = jnp.sin(angle)[:, None, :]
    first_half = field[..., :half]
    second_half = field[..., half:]
    if backward:
        return jnp.concatenate(
            [first_half * cosine + second_half * sine, second_half * cosine - first_half * sine], -1
        )
    return jnp.concatenate(
        [first_half * cosine - second_half * sine, second_half * cosine + first_half * sine], -1
    )


def slot_of(route_flat):
    labels = jnp.arange(EXPERTS, dtype=jnp.int32)
    member = (route_flat[:, None] == labels[None, :]).astype(jnp.int32)
    ranks = jnp.cumsum(member, 0) - 1
    return route_flat * CAP + jnp.sum(ranks * member, 1)


def owner_of(slot_ids, count_rows, per_row):
    picked = jnp.arange(slot_ids.shape[0], dtype=jnp.int32) // per_row
    return jnp.full((EXPERTS * CAP,), count_rows, jnp.int32).at[slot_ids].set(picked)


def silu_slope(value):
    sigma = jax.nn.sigmoid(value)
    return sigma * (1.0 + value * (1.0 - sigma))


def block_scores(query_block, key_block, seg_block, index_block, key_segments, key_index, table):
    seen = visible(seg_block, index_block, key_segments, key_index, table)
    raw = jnp.einsum("bhd,lhd->hbl", query_block, key_block, preferred_element_type=jnp.float32)
    return jnp.where(seen[None], raw * HEAD_DIM ** (-0.5), -1e30)


def fetch(norm_gains, project, mixing, router, expander, reducer, spreader, collector):
    return (
        lax.all_gather(norm_gains, ("dp", "seq"), axis=1, tiled=True),
        lax.all_gather(project, ("dp", "seq"), axis=1, tiled=True),
        lax.all_gather(mixing, ("dp", "seq"), axis=1, tiled=True),
        lax.all_gather(router, ("dp", "seq"), axis=0, tiled=True),
        lax.all_gather(expander, ("dp", "seq"), axis=2, tiled=True),
        lax.all_gather(reducer, ("dp", "seq"), axis=2, tiled=True),
        lax.all_gather(spreader, ("dp", "seq"), axis=1, tiled=True),
        lax.all_gather(collector, ("dp", "seq"), axis=1, tiled=True),
    )


def reduce_end(grads):
    (
        gain_part,
        project_part,
        mixing_part,
        router_part,
        expander_part,
        reducer_part,
        spreader_part,
        collector_part,
    ) = grads
    return (
        lax.psum_scatter(gain_part, ("dp", "seq"), scatter_dimension=1, tiled=True),
        lax.psum_scatter(project_part, ("dp", "seq"), scatter_dimension=1, tiled=True),
        lax.psum_scatter(mixing_part, ("dp", "seq"), scatter_dimension=1, tiled=True),
        lax.psum_scatter(router_part, ("dp", "seq"), scatter_dimension=0, tiled=True),
        lax.psum_scatter(expander_part, ("dp", "seq"), scatter_dimension=2, tiled=True),
        lax.psum_scatter(reducer_part, ("dp", "seq"), scatter_dimension=2, tiled=True),
        lax.psum_scatter(spreader_part, ("dp", "seq"), scatter_dimension=1, tiled=True),
        lax.psum_scatter(collector_part, ("dp", "seq"), scatter_dimension=1, tiled=True),
    )


def forward_pass(tree_tokens, tree_segments, tree_parents, tree_routes, weights, offset):
    norm_gains, project, mixing, router, expander, reducer, spreader, collector = weights
    row_count = tree_tokens.shape[0]
    model_width = tree_tokens.shape[1]
    tree_length = tree_segments.shape[0]
    local_heads = project.shape[2] // HEAD_DIM
    table = ancestry(tree_parents)
    place = lax.dynamic_slice_in_dim(positions(tree_segments, table), offset, row_count).astype(
        jnp.float32
    )
    row_segments = lax.dynamic_slice_in_dim(tree_segments, offset, row_count)
    row_index = offset + jnp.arange(row_count, dtype=jnp.int32)
    key_index = jnp.arange(tree_length, dtype=jnp.int32)
    inputs = tree_tokens.astype(jnp.float32)
    scale_one = lax.rsqrt(jnp.mean(inputs * inputs, -1, keepdims=True) + epsilon)
    normed_one = inputs * scale_one
    first_in = (normed_one * norm_gains[0].astype(jnp.float32)).astype(jnp.bfloat16)
    mapped = jnp.einsum("td,cdh->cth", first_in, project, preferred_element_type=jnp.float32)
    head_shape = (row_count, local_heads, HEAD_DIM)
    queries = turn(mapped[0].reshape(head_shape), place, False).astype(jnp.bfloat16)
    keys_own = (
        turn(mapped[1].reshape(head_shape), place, False)
        .astype(jnp.bfloat16)
        .reshape(row_count, -1)
    )
    values_own = mapped[2].astype(jnp.bfloat16)
    keys_flat, values_flat = (
        lax.all_gather(keys_own, "seq", axis=0, tiled=True),
        lax.all_gather(values_own, "seq", axis=0, tiled=True),
    )
    keys_all = keys_flat.reshape(tree_length, local_heads, HEAD_DIM)
    values_all = values_flat.reshape(tree_length, local_heads, HEAD_DIM)
    blocks = row_count // QB
    query_blocks = queries.reshape(blocks, QB, local_heads, HEAD_DIM)
    seg_blocks = row_segments.reshape(blocks, QB)
    index_blocks = row_index.reshape(blocks, QB)

    def attend(entries):
        query_block, seg_block, index_block = entries
        scores = block_scores(
            query_block, keys_all, seg_block, index_block, tree_segments, key_index, table
        )
        row_peak = jnp.max(scores, -1, keepdims=True)
        expo = jnp.exp(scores - row_peak)
        row_total = jnp.sum(expo, -1, keepdims=True)
        chances_soft = expo / row_total
        mixed_block = jnp.einsum(
            "hbl,lhd->bhd",
            chances_soft.astype(jnp.bfloat16),
            values_all,
            preferred_element_type=jnp.float32,
        )
        return (mixed_block, (row_peak + jnp.log(row_total))[..., 0])

    mixed, log_totals = lax.map(attend, (query_blocks, seg_blocks, index_blocks))
    heads_out = mixed.reshape(row_count, -1).astype(jnp.bfloat16)
    attended = lax.psum(
        jnp.dot(heads_out, mixing, preferred_element_type=jnp.float32).astype(jnp.bfloat16),
        "tensor",
    ).astype(jnp.float32)
    second = inputs + attended
    scale_two = lax.rsqrt(jnp.mean(second * second, -1, keepdims=True) + epsilon)
    normed_two = second * scale_two
    hidden_in = (normed_two * norm_gains[1].astype(jnp.float32)).astype(jnp.bfloat16)
    logits = jnp.dot(hidden_in, router, preferred_element_type=jnp.float32)
    shifted = jnp.exp(logits - jnp.max(logits, -1, keepdims=True))
    chances = shifted / jnp.sum(shifted, -1, keepdims=True)
    picks = (tree_routes[:, :, None] == jnp.arange(EXPERTS, dtype=jnp.int32)[None, None, :]).astype(
        jnp.float32
    )
    gates = jnp.sum(picks * chances[:, None, :], -1)
    per_row = tree_routes.shape[1]
    slot_ids = slot_of(tree_routes.reshape(-1))
    owners = owner_of(slot_ids, row_count, per_row)
    padded = jnp.concatenate([hidden_in, jnp.zeros((1, model_width), jnp.bfloat16)], 0)
    routed = jnp.take(padded, owners, axis=0).reshape(EXPERTS, CAP, model_width)
    raised = jnp.einsum("ecd,egdf->gecf", routed, expander, preferred_element_type=jnp.float32)
    activated = (jax.nn.silu(raised[0]) * raised[1]).astype(jnp.bfloat16)
    lowered = jnp.einsum(
        "ecf,efd->ecd", activated, reducer, preferred_element_type=jnp.float32
    ).reshape(EXPERTS * CAP, model_width)
    returned = jnp.take(lowered, slot_ids, axis=0).reshape(row_count, per_row, model_width)
    blended = jnp.sum(gates[:, :, None] * returned, 1)
    spread = jnp.einsum("td,gdf->gtf", hidden_in, spreader, preferred_element_type=jnp.float32)
    common = (jax.nn.silu(spread[0]) * spread[1]).astype(jnp.bfloat16)
    shared_out = jnp.dot(common, collector, preferred_element_type=jnp.float32)
    branches = lax.psum((blended + shared_out).astype(jnp.bfloat16), "tensor").astype(jnp.float32)
    output_tree = (second + branches).astype(jnp.bfloat16)
    kept = {
        "table": table,
        "place": place,
        "offset": offset,
        "row_segments": row_segments,
        "seg_blocks": seg_blocks,
        "index_blocks": index_blocks,
        "scale_one": scale_one,
        "normed_one": normed_one,
        "first_in": first_in,
        "queries": queries,
        "query_blocks": query_blocks,
        "keys_all": keys_all,
        "values_all": values_all,
        "log_totals": log_totals,
        "heads_out": heads_out,
        "scale_two": scale_two,
        "normed_two": normed_two,
        "hidden_in": hidden_in,
        "chances": chances,
        "picks": picks,
        "gates": gates,
        "slot_ids": slot_ids,
        "routed": routed,
        "raised": raised,
        "activated": activated,
        "returned": returned,
        "spread": spread,
        "common": common,
    }
    return (kept, output_tree)


def backward_pass(tree_cot, tree_segments, kept, weights):
    norm_gains, project, mixing, router, expander, reducer, spreader, collector = weights
    upstream = tree_cot.astype(jnp.float32)
    row_count = upstream.shape[0]
    model_width = upstream.shape[1]
    shared_grad = upstream.astype(jnp.bfloat16)
    common_grad = jnp.einsum(
        "td,fd->tf", shared_grad, collector, preferred_element_type=jnp.float32
    )
    collector_part = jnp.einsum(
        "tf,td->fd", kept["common"], shared_grad, preferred_element_type=jnp.float32
    )
    spread = kept["spread"]
    spread_grad = jnp.stack(
        [common_grad * spread[1] * silu_slope(spread[0]), common_grad * jax.nn.silu(spread[0])]
    ).astype(jnp.bfloat16)
    spreader_part = jnp.einsum(
        "td,gtf->gdf", kept["hidden_in"], spread_grad, preferred_element_type=jnp.float32
    )
    hidden_grad = jnp.einsum(
        "gtf,gdf->td", spread_grad, spreader, preferred_element_type=jnp.float32
    )
    gates = kept["gates"]
    slot_ids = kept["slot_ids"]
    per_row = gates.shape[1]
    pair_grad = (
        (gates[:, :, None] * upstream[:, None, :])
        .astype(jnp.bfloat16)
        .reshape(row_count * per_row, model_width)
    )
    lowered_grad = (
        jnp.zeros((EXPERTS * CAP, model_width), jnp.bfloat16)
        .at[slot_ids]
        .set(pair_grad)
        .reshape(EXPERTS, CAP, model_width)
    )
    activated_grad = jnp.einsum(
        "ecd,efd->ecf", lowered_grad, reducer, preferred_element_type=jnp.float32
    )
    reducer_part = jnp.einsum(
        "ecf,ecd->efd", kept["activated"], lowered_grad, preferred_element_type=jnp.float32
    )
    raised = kept["raised"]
    raised_grad = jnp.stack(
        [
            activated_grad * raised[1] * silu_slope(raised[0]),
            activated_grad * jax.nn.silu(raised[0]),
        ]
    ).astype(jnp.bfloat16)
    expander_part = jnp.einsum(
        "ecd,gecf->egdf", kept["routed"], raised_grad, preferred_element_type=jnp.float32
    )
    routed_grad = jnp.einsum(
        "gecf,egdf->ecd", raised_grad, expander, preferred_element_type=jnp.float32
    ).reshape(EXPERTS * CAP, model_width)
    hidden_grad = hidden_grad + jnp.sum(
        jnp.take(routed_grad, slot_ids, axis=0).reshape(row_count, per_row, model_width), 1
    )
    gate_grad = jnp.sum(upstream[:, None, :] * kept["returned"], -1)
    hidden_grad, gate_grad = (
        lax.psum(hidden_grad.astype(jnp.bfloat16), "tensor").astype(jnp.float32),
        lax.psum(gate_grad.astype(jnp.bfloat16), "tensor").astype(jnp.float32),
    )
    chances = kept["chances"]
    chance_grad = jnp.sum(kept["picks"] * gate_grad[:, :, None], 1)
    logit_grad = chances * (chance_grad - jnp.sum(chances * chance_grad, -1, keepdims=True))
    hidden_grad = hidden_grad + jnp.dot(logit_grad, router.astype(jnp.float32).T, precision=highest)
    router_part = jnp.dot(kept["hidden_in"].astype(jnp.float32).T, logit_grad, precision=highest)
    normed_two = kept["normed_two"]
    gain_two = jnp.sum(hidden_grad * normed_two, 0)
    scaled_two = hidden_grad * norm_gains[1].astype(jnp.float32)
    second_grad = upstream + kept["scale_two"] * (
        scaled_two - normed_two * jnp.mean(scaled_two * normed_two, -1, keepdims=True)
    )
    branch_grad = second_grad.astype(jnp.bfloat16)
    mixing_part = jnp.einsum(
        "th,td->hd", kept["heads_out"], branch_grad, preferred_element_type=jnp.float32
    )
    heads_grad = jnp.einsum(
        "td,hd->th", branch_grad, mixing, preferred_element_type=jnp.float32
    ).astype(jnp.bfloat16)
    keys_all = kept["keys_all"]
    values_all = kept["values_all"]
    table = kept["table"]
    query_blocks = kept["query_blocks"]
    tree_length = keys_all.shape[0]
    local_heads = keys_all.shape[1]
    key_index = jnp.arange(tree_length, dtype=jnp.int32)
    grad_blocks = heads_grad.reshape(query_blocks.shape)
    factor = HEAD_DIM ** (-0.5)

    def attend_back(carry, entries):
        keys_grad, values_grad = carry
        query_block, grad_block, log_block, seg_block, index_block = entries
        scores = block_scores(
            query_block, keys_all, seg_block, index_block, tree_segments, key_index, table
        )
        chances_soft = jnp.exp(scores - log_block[..., None])
        prob_grad = jnp.einsum(
            "bhd,lhd->hbl", grad_block, values_all, preferred_element_type=jnp.float32
        )
        centre = jnp.sum(chances_soft * prob_grad, -1, keepdims=True)
        score_grad = (chances_soft * (prob_grad - centre) * factor).astype(jnp.bfloat16)
        query_grad_block = jnp.einsum(
            "hbl,lhd->bhd", score_grad, keys_all, preferred_element_type=jnp.float32
        )
        keys_grad = keys_grad + jnp.einsum(
            "hbl,bhd->lhd", score_grad, query_block, preferred_element_type=jnp.float32
        )
        values_grad = values_grad + jnp.einsum(
            "hbl,bhd->lhd",
            chances_soft.astype(jnp.bfloat16),
            grad_block,
            preferred_element_type=jnp.float32,
        )
        return ((keys_grad, values_grad), query_grad_block)

    zero_kv = jnp.zeros((tree_length, local_heads, HEAD_DIM), jnp.float32)
    (keys_grad, values_grad), query_grad = lax.scan(
        attend_back,
        (zero_kv, zero_kv),
        (query_blocks, grad_blocks, kept["log_totals"], kept["seg_blocks"], kept["index_blocks"]),
    )
    keys_own_grad, values_own_grad = (
        lax.psum_scatter(
            keys_grad.reshape(tree_length, -1).astype(jnp.bfloat16),
            "seq",
            scatter_dimension=0,
            tiled=True,
        ).astype(jnp.float32),
        lax.psum_scatter(
            values_grad.reshape(tree_length, -1).astype(jnp.bfloat16),
            "seq",
            scatter_dimension=0,
            tiled=True,
        ).astype(jnp.float32),
    )
    place = kept["place"]
    query_back = turn(query_grad.reshape(row_count, local_heads, HEAD_DIM), place, True).reshape(
        row_count, -1
    )
    key_back = turn(keys_own_grad.reshape(row_count, local_heads, HEAD_DIM), place, True).reshape(
        row_count, -1
    )
    mapped_grad = jnp.stack([query_back, key_back, values_own_grad]).astype(jnp.bfloat16)
    project_part = jnp.einsum(
        "td,cth->cdh", kept["first_in"], mapped_grad, preferred_element_type=jnp.float32
    )
    first_grad = lax.psum(
        jnp.einsum("cth,cdh->td", mapped_grad, project, preferred_element_type=jnp.float32).astype(
            jnp.bfloat16
        ),
        "tensor",
    ).astype(jnp.float32)
    normed_one = kept["normed_one"]
    gain_one = jnp.sum(first_grad * normed_one, 0)
    scaled_one = first_grad * norm_gains[0].astype(jnp.float32)
    input_tree = (
        second_grad
        + kept["scale_one"]
        * (scaled_one - normed_one * jnp.mean(scaled_one * normed_one, -1, keepdims=True))
    ).astype(jnp.bfloat16)
    gain_part = jnp.stack([gain_one, gain_two])
    return (
        input_tree,
        (
            gain_part,
            project_part,
            mixing_part,
            router_part,
            expander_part,
            reducer_part,
            spreader_part,
            collector_part,
        ),
    )


def local(
    tokens,
    cotangent,
    segments,
    parents,
    routes,
    norm_gains,
    project,
    mixing,
    router,
    expander,
    reducer,
    spreader,
    collector,
):
    tree_count = tokens.shape[0]
    offset = lax.axis_index("seq") * tokens.shape[1]
    outputs = []
    input_grads = []
    running = None
    for tree_index in range(tree_count):
        forward_weights = fetch(
            norm_gains, project, mixing, router, expander, reducer, spreader, collector
        )
        kept, output_tree = forward_pass(
            tokens[tree_index],
            segments[tree_index],
            parents[tree_index],
            routes[tree_index],
            forward_weights,
            offset,
        )
        backward_weights = fetch(
            norm_gains, project, mixing, router, expander, reducer, spreader, collector
        )
        input_tree, tree_grads = backward_pass(
            cotangent[tree_index], segments[tree_index], kept, backward_weights
        )
        outputs.append(output_tree)
        input_grads.append(input_tree)
        if running is None:
            running = tree_grads
        else:
            running = tuple((before + addend for before, addend in zip(running, tree_grads)))
    running = reduce_end(running)
    return (
        jnp.stack(outputs),
        jnp.stack(input_grads),
        running[0],
        running[1],
        running[2],
        running[3],
        running[4],
        running[5],
        running[6],
        running[7],
    )


def solution(mesh):
    in_specs = (
        P("dp", "seq", None),
        P("dp", "seq", None),
        P("dp", None),
        P("dp", None),
        P("dp", "seq", None),
        P(None, ("dp", "seq")),
        P(None, ("dp", "seq"), "tensor"),
        P("tensor", ("dp", "seq")),
        P(("dp", "seq"), None),
        P(None, None, ("dp", "seq"), "tensor"),
        P(None, "tensor", ("dp", "seq")),
        P(None, ("dp", "seq"), "tensor"),
        P("tensor", ("dp", "seq")),
    )
    out_specs = (
        P("dp", "seq", None),
        P("dp", "seq", None),
        P(None, ("dp", "seq")),
        P(None, ("dp", "seq"), "tensor"),
        P("tensor", ("dp", "seq")),
        P(("dp", "seq"), None),
        P(None, None, ("dp", "seq"), "tensor"),
        P(None, "tensor", ("dp", "seq")),
        P(None, ("dp", "seq"), "tensor"),
        P("tensor", ("dp", "seq")),
    )
    return jax.shard_map(local, mesh=mesh, in_specs=in_specs, out_specs=out_specs, check_vma=False)
```

profile of v0, /device:TPU:0, one launch (start us, length us, event | category | flops | bytes accessed | tf_op | source)
XLA Modules:
  0.0 2119.6 jit_solution(11682005284348731148)
XLA Ops:
  10.7 41.6 %all_gather.25 = bf16[3,768,192]{2,0,1:T(4,128)(2,1)S(1)} all-gather(bf16[3,96,192]{2,0,1:T(4,128)(2,1)S(1)} %copy.132), channel_id=1, replica_groups=mesh['dp'=2,'seq'=4,'tensor'=4] {'dp','seq'}, dimensions={1}, use_global_device_ids=true | all-gather | bytes 995328 | tf_op jit(solution)/shard_map/all_gather | solution.py:92
  54.7 18.5 all-gather.2
  118.2 32.0 %all_gather.28 = bf16[192,768]{0,1:T(8,128)(2,1)S(1)} all-gather(bf16[192,96]{0,1:T(8,128)(2,1)S(1)} %copy.134), channel_id=1, replica_groups=mesh['dp'=2,'seq'=4,'tensor'=4] {'dp','seq'}, dimensions={1}, use_global_device_ids=true | all-gather | bytes 331776 | tf_op jit(solution)/shard_map/all_gather | solution.py:93
  150.2 18.8 all-gather
  272.9 27.0 %all-gather.3 = bf16[8,96,8]{1,2,0:T(8,128)(2,1)S(1)} all-gather(bf16[1,96,8]{1,2,0:T(8,128)(2,1)S(1)} %bitcast.539), channel_id=1, replica_groups=mesh['dp'=2,'seq'=4,'tensor'=4] {'dp','seq'}, dimensions={0}, use_global_device_ids=true | all-gather | bytes 13824 | tf_op jit(solution)/shard_map/all_gather | solution.py:94
  300.1 38.7 %all_gather.33 = bf16[512,768]{0,1:T(8,128)(2,1)} all-gather(bf16[512,96]{0,1:T(8,128)(2,1)S(1)} %copy-done.64), channel_id=1, replica_groups=mesh['dp'=2,'seq'=4,'tensor'=4] {'dp','seq'}, dimensions={1}, use_global_device_ids=true | all-gather | bytes 884736 | tf_op jit(solution)/shard_map/all_gather | solution.py:98
  370.5 97.2 %all-gather.8.cloned.1.call-done = bf16[8,2,768,512]{3,2,1,0:T(8,128)(2,1)} async-done(((bf16[8,2,96,512]{3,2,1,0:T(8,128)(2,1)}), bf16[8,2,768,512]{3,2,1,0:T(8,128)(2,1)}) %all-gather.8.cloned.1.call-update) | async-done | bytes 12582928 | tf_op jit(solution)/shard_map/all_gather | solution.py:95
  478.3 88.4 %all-gather.10.cloned.1.call-done = bf16[8,512,768]{1,2,0:T(8,128)(2,1)} async-done(((bf16[8,512,96]{1,2,0:T(8,128)(2,1)}), bf16[8,512,768]{1,2,0:T(8,128)(2,1)}) %all-gather.10.cloned.1.call-update) | async-done | bytes 6291472 | tf_op jit(solution)/shard_map/all_gather | solution.py:96
  736.7 39.5 %all-reduce.16.cloned.1.call-done = (bf16[512,768]{1,0:T(8,128)(2,1)}, bf16[512,768]{1,0:T(8,128)(2,1)}) async-done(((bf16[512,768]{1,0:T(8,128)(2,1)}, bf16[512,768]{1,0:T(8,128)(2,1)}), (bf16[512,768]{1,0:T(8,128)(2,1)}, bf16[512,768]{1,0:T(8,128)(2,1)})) %all-reduce.16.cloned.1.call-update) | async-done | bytes 1572880 | tf_op jit(solution)/shard_map/psum | solution.py:306
  792.1 27.6 %fusion.88 = bf16[3,64,2048]{2,1,0:T(8,128)(2,1)} fusion(f32[3,512,2048]{2,1,0:T(8,128)} %fusion.298, f32[3,512,2048]{2,1,0:T(8,128)} %get-tuple-element.316, f32[3,512]{1,0:T(4,128)S(1)} %copy-done.92, pred[512,2048]{1,0:T(8,128)(4,1)} %fusion.72, bf16[512,3,32]{0,2,1:T(8,128)(2,1)} %get-tuple-element.284, bf16[512,3,32]{0,2,1:T(8,128)(2,1)} %get-tuple-element.283), kind=kOutput, calls=%fused_computation.101 | convolution fusion | flops 438046208 | bytes 27203584 | tf_op jit(solution)/shard_map/while/body/eval_jaxpr/hbl,bhd->lhd/dot_general | solution.py:352
  839.9 27.4 %fusion.91 = bf16[3,64,2048]{2,1,0:T(8,128)(2,1)} fusion(f32[3,512,2048]{2,1,0:T(8,128)} %fusion.297, f32[3,512,2048]{2,1,0:T(8,128)} %get-tuple-element.318, f32[3,512]{1,0:T(4,128)S(1)} %log_add_fusion.1, pred[512,2048]{1,0:T(8,128)(4,1)} %fusion.73, bf16[512,3,32]{0,2,1:T(8,128)(2,1)} %copy-done.66, bf16[512,3,32]{0,2,1:T(8,128)(2,1)} %copy-done.65), kind=kOutput, calls=%fused_computation.102 | convolution fusion | flops 438046208 | bytes 27203584 | tf_op jit(solution)/shard_map/while/body/eval_jaxpr/hbl,bhd->lhd/dot_general | solution.py:352
  900.6 24.1 %fusion.130 = f32[512,3,64]{0,2,1:T(8,128)} fusion(bf16[2048,3,64]{0,2,1:T(8,128)(2,1)} %bitcast.499, f32[3,512,2048]{2,1,0:T(8,128)} %fusion.298, f32[3,512,2048]{2,1,0:T(8,128)} %get-tuple-element.316, f32[3,512]{1,0:T(4,128)S(1)} %copy-done.92, pred[512,2048]{1,0:T(8,128)(4,1)} %fusion.72), kind=kOutput, calls=%fused_computation.182 | convolution fusion | flops 437259776 | bytes 27400192 | tf_op jit(solution)/shard_map/while/body/eval_jaxpr/hbl,lhd->bhd/dot_general | solution.py:349
  924.6 24.1 %fusion.133 = f32[512,3,64]{0,2,1:T(8,128)} fusion(bf16[2048,3,64]{0,2,1:T(8,128)(2,1)} %bitcast.501, f32[3,512,2048]{2,1,0:T(8,128)} %fusion.297, f32[3,512,2048]{2,1,0:T(8,128)} %get-tuple-element.318, f32[3,512]{1,0:T(4,128)S(1)} %log_add_fusion.1, pred[512,2048]{1,0:T(8,128)(4,1)} %fusion.73), kind=kOutput, calls=%fused_computation.183 | convolution fusion | flops 437259776 | bytes 27400192 | tf_op jit(solution)/shard_map/while/body/eval_jaxpr/hbl,lhd->bhd/dot_general | solution.py:349
  987.1 44.5 %all-reduce.14.cloned.1.call-done = (bf16[512,768]{1,0:T(8,128)(2,1)}, bf16[512,768]{1,0:T(8,128)(2,1)}, bf16[512,768]{1,0:T(8,128)(2,1)}, bf16[512,768]{1,0:T(8,128)(2,1)}) async-done(((bf16[512,768]{1,0:T(8,128)(2,1)}, bf16[512,768]{1,0:T(8,128)(2,1)}, bf16[512,768]{1,0:T(8,128)(2,1)}, bf16[512,768]{1,0:T(8,128)(2,1)}), (bf16[512,768]{1,0:T(8,128)(2,1)}, bf16[512,768]{1,0:T(8,128)(2,1)}, ...) | async-done | bytes 3145744 | tf_op jit(solution)/shard_map/psum | solution.py:211
  1062.8 19.2 add_bitcast_fusion
  1082.1 25.3 %copy.157 = f32[8,2,768,512]{3,0,1,2:T(8,128)} copy(f32[8,2,768,512]{2,3,1,0:T(8,128)} %add_bitcast_fusion) | data formatting | bytes 50331648 | tf_op jit(solution)/shard_map/add | solution.py:467
  1126.9 37.2 %all-reduce.12.cloned.1.call-done = f32[2,768,512]{2,0,1:T(2,128)} async-done(((f32[2,768,512]{2,0,1:T(2,128)}), f32[2,768,512]{2,0,1:T(2,128)}) %all-reduce.12.cloned.1.call-update) | async-done | bytes 3145744
  1166.0 62.2 %reduce-scatter.40.cloned.1.call-done = f32[96,8]{1,0:T(8,128)} async-done(((f32[768,8]{1,0:T(8,128)}), f32[96,8]{1,0:T(8,128)}) %reduce-scatter.40.cloned.1.call-update) | async-done | bytes 3088
  1229.6 63.5 %reduce-scatter.38.cloned.1.call-done = f32[96,192]{1,0:T(8,128)} async-done(((f32[768,192]{1,0:T(8,128)}), f32[96,192]{1,0:T(8,128)}) %reduce-scatter.38.cloned.1.call-update) | async-done | bytes 73744
  1300.9 55.9 %reduce-scatter.34.cloned.1.call-done = f32[96,2]{1,0:T(8,128)} async-done(((f32[768,2]{1,0:T(8,128)}), f32[96,2]{1,0:T(8,128)}) %reduce-scatter.34.cloned.1.call-update) | async-done | bytes 784
  1358.3 67.5 %reduce-scatter.36.cloned.1.call-done = f32[96,576]{1,0:T(8,128)} async-done(((f32[768,576]{1,0:T(8,128)}), f32[96,576]{1,0:T(8,128)}) %reduce-scatter.36.cloned.1.call-update) | async-done | bytes 221200
  1427.7 405.8 %reduce-scatter.28.cloned.1.call-done = f32[8,2,96,512]{3,0,1,2:T(8,128)} async-done(((f32[8,2,768,512]{3,0,1,2:T(8,128)}), f32[8,2,96,512]{3,0,1,2:T(8,128)}) %reduce-scatter.28.cloned.1.call-update) | async-done | bytes 3145744 | tf_op jit(solution)/shard_map/reduce_scatter | solution.py:118
  1838.9 62.8 %reduce-scatter.32.cloned.1.call-done = f32[512,96]{0,1:T(8,128)} async-done(((f32[512,768]{0,1:T(8,128)}), f32[512,96]{0,1:T(8,128)}) %reduce-scatter.32.cloned.1.call-update) | async-done | bytes 196624 | tf_op jit(solution)/shard_map/reduce_scatter | solution.py:121
  1901.7 210.4 %reduce-scatter.30.cloned.1.call-done = f32[8,512,96]{1,2,0:T(8,128)} async-done(((f32[8,512,768]{1,2,0:T(8,128)}), f32[8,512,96]{1,2,0:T(8,128)}) %reduce-scatter.30.cloned.1.call-update) | async-done | bytes 1572880 | tf_op jit(solution)/shard_map/reduce_scatter | solution.py:119
  (492 shorter events, 542.3 us)
Async XLA Ops:
  8.0 330.7 %all-reduce.18.cloned.1.call-start = ((), (), s32[]{:S(2)}) async-start(), calls=%async_computation.28 | async-start | bytes 3145728 | tf_op jit(solution)/shard_map/psum | solution.py:181
  93.4 113.7 %copy-start.26 = (bf16[1,2048,192]{1,2,0:T(8,128)(2,1)}, bf16[1,2048,192]{1,2,0:T(8,128)(2,1)S(1)}, u32[]{:S(2)}) copy-start(bf16[1,2048,192]{1,2,0:T(8,128)(2,1)S(1)} %all-gather.1) | copy-start | bytes 2359300
  98.5 76.1 %copy-start.52 = (f32[512,32]{0,1:T(8,128)}, f32[512,32]{0,1:T(8,128)S(1)}, u32[]{:S(2)}) copy-start(f32[512,32]{0,1:T(8,128)S(1)} %get-tuple-element.303) | copy-start | bytes 196612
  98.5 76.1 %copy-start.54 = (f32[512,32]{0,1:T(8,128)}, f32[512,32]{0,1:T(8,128)S(1)}, u32[]{:S(2)}) copy-start(f32[512,32]{0,1:T(8,128)S(1)} %get-tuple-element.304) | copy-start | bytes 196612
  150.2 84.7 %copy-start.19 = (bf16[192,768]{0,1:T(8,128)(2,1)}, bf16[192,768]{0,1:T(8,128)(2,1)S(1)}, u32[]{:S(2)}) copy-start(bf16[192,768]{0,1:T(8,128)(2,1)S(1)} %all_gather.28) | copy-start | bytes 884740
  236.3 125.3 %all-gather.12.cloned.1.call-start = ((), (), s32[]{:S(2)}) async-start(), calls=%async_computation.13 | async-start | bytes 1769472 | tf_op jit(solution)/shard_map/all_gather | solution.py:97
  236.9 230.8 %all-gather.8.cloned.1.call-start = ((), (), s32[]{:S(2)}) async-start(), calls=%async_computation.11 | async-start | bytes 14155776 | tf_op jit(solution)/shard_map/all_gather | solution.py:95
  237.4 329.2 %all-gather.10.cloned.1.call-start = ((), (), s32[]{:S(2)}) async-start(), calls=%async_computation.12 | async-start | bytes 7077888 | tf_op jit(solution)/shard_map/all_gather | solution.py:96
  238.0 538.2 %all-reduce.16.cloned.1.call-start = ((), (), s32[]{:S(2)}) async-start(), calls=%async_computation.27 | async-start | bytes 3145728 | tf_op jit(solution)/shard_map/psum | solution.py:306
  300.0 312.9 %copy-start.88 = (pred[1024]{0:T(1024)(128)(4,1)}, pred[1024]{0:T(1024)(128)(4,1)S(1)}, u32[]{:S(2)}) copy-start(pred[1024]{0:T(1024)(128)(4,1)S(1)} %compare_and_fusion.3) | copy-start | bytes 3076
  478.3 95.6 %copy-start.9 = (bf16[8,192,512]{2,1,0:T(8,128)(2,1)}, bf16[8,192,512]{2,1,0:T(8,128)(2,1)S(1)}, u32[]{:S(2)}) copy-start(bf16[8,192,512]{2,1,0:T(8,128)(2,1)S(1)} %multiply_convert_fusion.8) | copy-start | bytes 4718596
  734.5 214.2 %reduce-scatter.24.cloned.1.call-start = ((), (), s32[]{:S(2)}) async-start(), calls=%async_computation.16 | async-start | bytes 983040 | tf_op jit(solution)/shard_map/reduce_scatter | solution.py:370
  819.7 130.8 %reduce-scatter.20.cloned.1.call-start = ((), (), s32[]{:S(2)}) async-start(), calls=%async_computation.14 | async-start | bytes 983040 | tf_op jit(solution)/shard_map/reduce_scatter | solution.py:370
  867.3 88.8 %reduce-scatter.26.cloned.1.call-start = ((), (), s32[]{:S(2)}) async-start(), calls=%async_computation.17 | async-start | bytes 983040 | tf_op jit(solution)/shard_map/reduce_scatter | solution.py:376
  887.0 72.2 %reduce-scatter.22.cloned.1.call-start = ((), (), s32[]{:S(2)}) async-start(), calls=%async_computation.15 | async-start | bytes 983040 | tf_op jit(solution)/shard_map/reduce_scatter | solution.py:376
  900.3 131.3 %all-reduce.14.cloned.1.call-start = ((), (), s32[]{:S(2)}) async-start(), calls=%async_computation.26 | async-start | bytes 6291456 | tf_op jit(solution)/shard_map/psum | solution.py:211
  962.4 201.7 %all-reduce.12.cloned.1.call-start = ((), (), s32[]{:S(2)}) async-start(), calls=%async_computation.25 | async-start | bytes 6291456
  973.8 254.4 %reduce-scatter.40.cloned.1.call-start = ((), (), s32[]{:S(2)}) async-start(), calls=%async_computation.24 | async-start | bytes 442368
  978.4 314.7 %reduce-scatter.38.cloned.1.call-start = ((), (), s32[]{:S(2)}) async-start(), calls=%async_computation.23 | async-start | bytes 884736
  983.4 373.4 %reduce-scatter.34.cloned.1.call-start = ((), (), s32[]{:S(2)}) async-start(), calls=%async_computation.21 | async-start | bytes 442368
  1035.3 390.5 %reduce-scatter.36.cloned.1.call-start = ((), (), s32[]{:S(2)}) async-start(), calls=%async_computation.22 | async-start | bytes 2211840
  1048.1 785.4 %reduce-scatter.28.cloned.1.call-start = ((), (), s32[]{:S(2)}) async-start(), calls=%async_computation.18 | async-start | bytes 28311552 | tf_op jit(solution)/shard_map/reduce_scatter | solution.py:118
  1107.4 794.3 %reduce-scatter.32.cloned.1.call-start = ((), (), s32[]{:S(2)}) async-start(), calls=%async_computation.20 | async-start | bytes 1769472 | tf_op jit(solution)/shard_map/reduce_scatter | solution.py:121
  1112.4 999.7 %reduce-scatter.30.cloned.1.call-start = ((), (), s32[]{:S(2)}) async-start(), calls=%async_computation.19 | async-start | bytes 14155776 | tf_op jit(solution)/shard_map/reduce_scatter | solution.py:119
  (105 other events, 1133.6 us)
Sparse Core Ops, SparseCore 0:
  236.4 41.6 all-reduce.17
  734.7 41.4 all-reduce.15
  819.8 23.3 reduce-scatter.23
  867.5 23.4 reduce-scatter.19
  893.7 22.5 reduce-scatter.25
  918.4 22.5 reduce-scatter.21
  962.6 69.0 all-reduce.13
  1035.2 128.8 all-reduce.11
  1167.8 60.3 reduce-scatter.39
  1231.7 61.4 reduce-scatter.37
  1296.5 60.3 reduce-scatter.33
  1360.2 65.6 reduce-scatter.35
  1430.2 403.2 reduce-scatter.27
  1837.7 63.8 reduce-scatter.31
  1905.7 206.3 reduce-scatter.29
Sparse Core Ops, SparseCore 1:
  238.9 44.7 all-gather.11
  285.6 182.0 all-gather.7
  469.7 96.9 all-gather.9
where the time goes:
time: 2130 us; the launch traced here: 2120 us
  waiting for transfers between devices  1240 us (58%)
  matrix products  343 us (16%)
  blocking collectives  231 us (11%)
  local copies, waits for them, and re-layouts  172 us (8%)
  other arithmetic  116 us (5%)
    reduce_scatter x1, waiting for transfers between devices, reduce_end(): lax.psum_scatter(expander_part, ('dp', 'seq'), scatter_dimension=2, tiled...  406 us
    unnamed x23, waiting for transfers between devices  288 us
    reduce_scatter x1, waiting for transfers between devices, reduce_end(): lax.psum_scatter(reducer_part, ('dp', 'seq'), scatter_dimension=2, tiled=...  210 us
    all_gather x1, waiting for transfers between devices, fetch(): lax.all_gather(expander, ('dp', 'seq'), axis=2, tiled=True)  97.2 us
    all_gather x1, waiting for transfers between devices, fetch(): lax.all_gather(reducer, ('dp', 'seq'), axis=2, tiled=True)  88.4 us
    reduce_scatter x1, waiting for transfers between devices, reduce_end(): lax.psum_scatter(collector_part, ('dp', 'seq'), scatter_dimension=1, tile...  62.8 us
    dot_general x2, matrix products, attend_back(): jnp.einsum('hbl,bhd->lhd', score_grad, query_block, preferred_element_typ...  54.9 us
    dot_general x2, matrix products, attend_back(): jnp.einsum('hbl,lhd->bhd', score_grad, keys_all, preferred_element_type=j...  48.1 us
  transfers between devices with their start and end apart: 18, of which 12 were waited for; matrix products, arithmetic and copies ran while one was open for 16% of the time, Pallas kernels for 0%

commit v1 on v0

--- a/solution.py
+++ b/solution.py
@@ -1,14 +1,22 @@
+import functools
 import math
+import types
 
 import jax
 import jax.numpy as jnp
 from jax import lax
+from jax.experimental import pallas as pl
+from jax.experimental.pallas import tpu as pltpu
 from jax.sharding import PartitionSpec as P
 
 HEAD_DIM = 64
 EXPERTS = 8
 CAP = 192
 QB = 512
+DP = "dp"
+SEQ = "seq"
+TENSOR = "tensor"
+GROUP = (DP, SEQ)
 
 
 epsilon = 1e-05
@@ -88,14 +96,14 @@
 
 def fetch(norm_gains, project, mixing, router, expander, reducer, spreader, collector):
     return (
-        lax.all_gather(norm_gains, ("dp", "seq"), axis=1, tiled=True),
-        lax.all_gather(project, ("dp", "seq"), axis=1, tiled=True),
-        lax.all_gather(mixing, ("dp", "seq"), axis=1, tiled=True),
-        lax.all_gather(router, ("dp", "seq"), axis=0, tiled=True),
-        lax.all_gather(expander, ("dp", "seq"), axis=2, tiled=True),
-        lax.all_gather(reducer, ("dp", "seq"), axis=2, tiled=True),
-        lax.all_gather(spreader, ("dp", "seq"), axis=1, tiled=True),
-        lax.all_gather(collector, ("dp", "seq"), axis=1, tiled=True),
+        lax.all_gather(norm_gains, GROUP, axis=1, tiled=True),
+        lax.all_gather(project, GROUP, axis=1, tiled=True),
+        lax.all_gather(mixing, GROUP, axis=1, tiled=True),
+        lax.all_gather(router, GROUP, axis=0, tiled=True),
+        lax.all_gather(expander, GROUP, axis=2, tiled=True),
+        lax.all_gather(reducer, GROUP, axis=2, tiled=True),
+        lax.all_gather(spreader, GROUP, axis=1, tiled=True),
+        lax.all_gather(collector, GROUP, axis=1, tiled=True),
     )
 
 
@@ -111,14 +119,14 @@
         collector_part,
     ) = grads
     return (
-        lax.psum_scatter(gain_part, ("dp", "seq"), scatter_dimension=1, tiled=True),
-        lax.psum_scatter(project_part, ("dp", "seq"), scatter_dimension=1, tiled=True),
-        lax.psum_scatter(mixing_part, ("dp", "seq"), scatter_dimension=1, tiled=True),
-        lax.psum_scatter(router_part, ("dp", "seq"), scatter_dimension=0, tiled=True),
-        lax.psum_scatter(expander_part, ("dp", "seq"), scatter_dimension=2, tiled=True),
-        lax.psum_scatter(reducer_part, ("dp", "seq"), scatter_dimension=2, tiled=True),
-        lax.psum_scatter(spreader_part, ("dp", "seq"), scatter_dimension=1, tiled=True),
-        lax.psum_scatter(collector_part, ("dp", "seq"), scatter_dimension=1, tiled=True),
+        lax.psum_scatter(gain_part, GROUP, scatter_dimension=1, tiled=True),
+        lax.psum_scatter(project_part, GROUP, scatter_dimension=1, tiled=True),
+        lax.psum_scatter(mixing_part, GROUP, scatter_dimension=1, tiled=True),
+        lax.psum_scatter(router_part, GROUP, scatter_dimension=0, tiled=True),
+        lax.psum_scatter(expander_part, GROUP, scatter_dimension=2, tiled=True),
+        lax.psum_scatter(reducer_part, GROUP, scatter_dimension=2, tiled=True),
+        lax.psum_scatter(spreader_part, GROUP, scatter_dimension=1, tiled=True),
+        lax.psum_scatter(collector_part, GROUP, scatter_dimension=1, tiled=True),
     )
 
 
@@ -149,8 +157,8 @@
     )
     values_own = mapped[2].astype(jnp.bfloat16)
     keys_flat, values_flat = (
-        lax.all_gather(keys_own, "seq", axis=0, tiled=True),
-        lax.all_gather(values_own, "seq", axis=0, tiled=True),
+        lax.all_gather(keys_own, SEQ, axis=0, tiled=True),
+        lax.all_gather(values_own, SEQ, axis=0, tiled=True),
     )
     keys_all = keys_flat.reshape(tree_length, local_heads, HEAD_DIM)
     values_all = values_flat.reshape(tree_length, local_heads, HEAD_DIM)
@@ -180,7 +188,7 @@
     heads_out = mixed.reshape(row_count, -1).astype(jnp.bfloat16)
     attended = lax.psum(
         jnp.dot(heads_out, mixing, preferred_element_type=jnp.float32).astype(jnp.bfloat16),
-        "tensor",
+        TENSOR,
     ).astype(jnp.float32)
     second = inputs + attended
     scale_two = lax.rsqrt(jnp.mean(second * second, -1, keepdims=True) + epsilon)
@@ -208,38 +216,38 @@
     spread = jnp.einsum("td,gdf->gtf", hidden_in, spreader, preferred_element_type=jnp.float32)
     common = (jax.nn.silu(spread[0]) * spread[1]).astype(jnp.bfloat16)
     shared_out = jnp.dot(common, collector, preferred_element_type=jnp.float32)
-    branches = lax.psum((blended + shared_out).astype(jnp.bfloat16), "tensor").astype(jnp.float32)
+    branches = lax.psum((blended + shared_out).astype(jnp.bfloat16), TENSOR).astype(jnp.float32)
     output_tree = (second + branches).astype(jnp.bfloat16)
-    kept = {
-        "table": table,
-        "place": place,
-        "offset": offset,
-        "row_segments": row_segments,
-        "seg_blocks": seg_blocks,
-        "index_blocks": index_blocks,
-        "scale_one": scale_one,
-        "normed_one": normed_one,
-        "first_in": first_in,
-        "queries": queries,
-        "query_blocks": query_blocks,
-        "keys_all": keys_all,
-        "values_all": values_all,
-        "log_totals": log_totals,
-        "heads_out": heads_out,
-        "scale_two": scale_two,
-        "normed_two": normed_two,
-        "hidden_in": hidden_in,
-        "chances": chances,
-        "picks": picks,
-        "gates": gates,
-        "slot_ids": slot_ids,
-        "routed": routed,
-        "raised": raised,
-        "activated": activated,
-        "returned": returned,
-        "spread": spread,
-        "common": common,
-    }
+    kept = types.SimpleNamespace(
+        table=table,
+        place=place,
+        offset=offset,
+        row_segments=row_segments,
+        seg_blocks=seg_blocks,
+        index_blocks=index_blocks,
+        scale_one=scale_one,
+        normed_one=normed_one,
+        first_in=first_in,
+        queries=queries,
+        query_blocks=query_blocks,
+        keys_all=keys_all,
+        values_all=values_all,
+        log_totals=log_totals,
+        heads_out=heads_out,
+        scale_two=scale_two,
+        normed_two=normed_two,
+        hidden_in=hidden_in,
+        chances=chances,
+        picks=picks,
+        gates=gates,
+        slot_ids=slot_ids,
+        routed=routed,
+        raised=raised,
+        activated=activated,
+        returned=returned,
+        spread=spread,
+        common=common,
+    )
     return (kept, output_tree)
 
 
@@ -253,20 +261,20 @@
         "td,fd->tf", shared_grad, collector, preferred_element_type=jnp.float32
     )
     collector_part = jnp.einsum(
-        "tf,td->fd", kept["common"], shared_grad, preferred_element_type=jnp.float32
-    )
-    spread = kept["spread"]
+        "tf,td->fd", kept.common, shared_grad, preferred_element_type=jnp.float32
+    )
+    spread = kept.spread
     spread_grad = jnp.stack(
         [common_grad * spread[1] * silu_slope(spread[0]), common_grad * jax.nn.silu(spread[0])]
     ).astype(jnp.bfloat16)
     spreader_part = jnp.einsum(
-        "td,gtf->gdf", kept["hidden_in"], spread_grad, preferred_element_type=jnp.float32
+        "td,gtf->gdf", kept.hidden_in, spread_grad, preferred_element_type=jnp.float32
     )
     hidden_grad = jnp.einsum(
         "gtf,gdf->td", spread_grad, spreader, preferred_element_type=jnp.float32
     )
-    gates = kept["gates"]
-    slot_ids = kept["slot_ids"]
+    gates = kept.gates
+    slot_ids = kept.slot_ids
     per_row = gates.shape[1]
     pair_grad = (
         (gates[:, :, None] * upstream[:, None, :])
@@ -283,9 +291,9 @@
         "ecd,efd->ecf", lowered_grad, reducer, preferred_element_type=jnp.float32
     )
     reducer_part = jnp.einsum(
-        "ecf,ecd->efd", kept["activated"], lowered_grad, preferred_element_type=jnp.float32
-    )
-    raised = kept["raised"]
+        "ecf,ecd->efd", kept.activated, lowered_grad, preferred_element_type=jnp.float32
+    )
+    raised = kept.raised
     raised_grad = jnp.stack(
         [
             activated_grad * raised[1] * silu_slope(raised[0]),
@@ -293,7 +301,7 @@
         ]
     ).astype(jnp.bfloat16)
     expander_part = jnp.einsum(
-        "ecd,gecf->egdf", kept["routed"], raised_grad, preferred_element_type=jnp.float32
+        "ecd,gecf->egdf", kept.routed, raised_grad, preferred_element_type=jnp.float32
     )
     routed_grad = jnp.einsum(
         "gecf,egdf->ecd", raised_grad, expander, preferred_element_type=jnp.float32
@@ -301,33 +309,33 @@
     hidden_grad = hidden_grad + jnp.sum(
         jnp.take(routed_grad, slot_ids, axis=0).reshape(row_count, per_row, model_width), 1
     )
-    gate_grad = jnp.sum(upstream[:, None, :] * kept["returned"], -1)
+    gate_grad = jnp.sum(upstream[:, None, :] * kept.returned, -1)
     hidden_grad, gate_grad = (
-        lax.psum(hidden_grad.astype(jnp.bfloat16), "tensor").astype(jnp.float32),
-        lax.psum(gate_grad.astype(jnp.bfloat16), "tensor").astype(jnp.float32),
-    )
-    chances = kept["chances"]
-    chance_grad = jnp.sum(kept["picks"] * gate_grad[:, :, None], 1)
+        lax.psum(hidden_grad.astype(jnp.bfloat16), TENSOR).astype(jnp.float32),
+        lax.psum(gate_grad.astype(jnp.bfloat16), TENSOR).astype(jnp.float32),
+    )
+    chances = kept.chances
+    chance_grad = jnp.sum(kept.picks * gate_grad[:, :, None], 1)
     logit_grad = chances * (chance_grad - jnp.sum(chances * chance_grad, -1, keepdims=True))
     hidden_grad = hidden_grad + jnp.dot(logit_grad, router.astype(jnp.float32).T, precision=highest)
-    router_part = jnp.dot(kept["hidden_in"].astype(jnp.float32).T, logit_grad, precision=highest)
-    normed_two = kept["normed_two"]
+    router_part = jnp.dot(kept.hidden_in.astype(jnp.float32).T, logit_grad, precision=highest)
+    normed_two = kept.normed_two
     gain_two = jnp.sum(hidden_grad * normed_two, 0)
     scaled_two = hidden_grad * norm_gains[1].astype(jnp.float32)
-    second_grad = upstream + kept["scale_two"] * (
+    second_grad = upstream + kept.scale_two * (
         scaled_two - normed_two * jnp.mean(scaled_two * normed_two, -1, keepdims=True)
     )
     branch_grad = second_grad.astype(jnp.bfloat16)
     mixing_part = jnp.einsum(
-        "th,td->hd", kept["heads_out"], branch_grad, preferred_element_type=jnp.float32
+        "th,td->hd", kept.heads_out, branch_grad, preferred_element_type=jnp.float32
     )
     heads_grad = jnp.einsum(
         "td,hd->th", branch_grad, mixing, preferred_element_type=jnp.float32
     ).astype(jnp.bfloat16)
-    keys_all = kept["keys_all"]
-    values_all = kept["values_all"]
-    table = kept["table"]
-    query_blocks = kept["query_blocks"]
+    keys_all = kept.keys_all
+    values_all = kept.values_all
+    table = kept.table
+    query_blocks = kept.query_blocks
     tree_length = keys_all.shape[0]
     local_heads = keys_all.shape[1]
     key_index = jnp.arange(tree_length, dtype=jnp.int32)
@@ -364,23 +372,23 @@
     (keys_grad, values_grad), query_grad = lax.scan(
         attend_back,
         (zero_kv, zero_kv),
-        (query_blocks, grad_blocks, kept["log_totals"], kept["seg_blocks"], kept["index_blocks"]),
+        (query_blocks, grad_blocks, kept.log_totals, kept.seg_blocks, kept.index_blocks),
     )
     keys_own_grad, values_own_grad = (
         lax.psum_scatter(
             keys_grad.reshape(tree_length, -1).astype(jnp.bfloat16),
-            "seq",
+            SEQ,
             scatter_dimension=0,
             tiled=True,
         ).astype(jnp.float32),
         lax.psum_scatter(
             values_grad.reshape(tree_length, -1).astype(jnp.bfloat16),
-            "seq",
+            SEQ,
             scatter_dimension=0,
             tiled=True,
         ).astype(jnp.float32),
     )
-    place = kept["place"]
+    place = kept.place
     query_back = turn(query_grad.reshape(row_count, local_heads, HEAD_DIM), place, True).reshape(
         row_count, -1
     )
@@ -389,20 +397,20 @@
     )
     mapped_grad = jnp.stack([query_back, key_back, values_own_grad]).astype(jnp.bfloat16)
     project_part = jnp.einsum(
-        "td,cth->cdh", kept["first_in"], mapped_grad, preferred_element_type=jnp.float32
+        "td,cth->cdh", kept.first_in, mapped_grad, preferred_element_type=jnp.float32
     )
     first_grad = lax.psum(
         jnp.einsum("cth,cdh->td", mapped_grad, project, preferred_element_type=jnp.float32).astype(
             jnp.bfloat16
         ),
-        "tensor",
+        TENSOR,
     ).astype(jnp.float32)
-    normed_one = kept["normed_one"]
+    normed_one = kept.normed_one
     gain_one = jnp.sum(first_grad * normed_one, 0)
     scaled_one = first_grad * norm_gains[0].astype(jnp.float32)
     input_tree = (
         second_grad
-        + kept["scale_one"]
+        + kept.scale_one
         * (scaled_one - normed_one * jnp.mean(scaled_one * normed_one, -1, keepdims=True))
     ).astype(jnp.bfloat16)
     gain_part = jnp.stack([gain_one, gain_two])
@@ -437,7 +445,7 @@
     collector,
 ):
     tree_count = tokens.shape[0]
-    offset = lax.axis_index("seq") * tokens.shape[1]
+    offset = lax.axis_index(SEQ) * tokens.shape[1]
     outputs = []
     input_grads = []
     running = None
@@ -480,32 +488,648 @@
     )
 
 
+VMEM_BYTES = 56 << 20
+
+
+def contract(left, right, left_dim, right_dim):
+    return lax.dot_general(
+        left, right, (((left_dim,), (right_dim,)), ((), ())), preferred_element_type=jnp.float32
+    )
+
+
+def scores_of(keys, queries, seen):
+    return jnp.where(seen, contract(keys, queries, 0, 0), -1e30)
+
+
+def seen_block(number, place_ref, key_bits_ref, query_bits, length):
+    start = pl.multiple_of((place_ref[0] - number) * length, length)
+    seen = (key_bits_ref[pl.ds(start, length), :] & query_bits) != 0
+    if number == 0:
+        keys = lax.broadcasted_iota(jnp.int32, seen.shape, 0)
+        rows = lax.broadcasted_iota(jnp.int32, seen.shape, 1)
+        seen = seen & (keys <= rows)
+    return seen
+
+
+def attend_kernel(count, heads, place_ref, query_ref, key_bits_ref, query_bits_ref, *refs):
+    pair_refs = refs[:count]
+    out_ref, log_ref, peak_ref, total_ref, mixed_ref = refs[count:]
+    length = query_ref.shape[1]
+    width = heads * HEAD_DIM
+
+    def block(number):
+        pair_ref = pair_refs[number]
+        seen = seen_block(number, place_ref, key_bits_ref, query_bits_ref[...], length)
+        for head in range(heads):
+            span = slice(head * HEAD_DIM, (head + 1) * HEAD_DIM)
+            value_span = slice(width + head * HEAD_DIM, width + (head + 1) * HEAD_DIM)
+            row = slice(head, head + 1)
+            scores = scores_of(pair_ref[span, :], query_ref[span, :], seen)
+            peak = jnp.max(scores, 0, keepdims=True)
+            if number:
+                before = peak_ref[row, :]
+                peak = jnp.maximum(before, peak)
+                shrink = jnp.exp(before - peak)
+            expo = jnp.exp(scores - peak)
+            total = jnp.sum(expo, 0, keepdims=True)
+            mixed = jnp.dot(
+                pair_ref[value_span, :],
+                expo.astype(jnp.bfloat16),
+                preferred_element_type=jnp.float32,
+            )
+            if number:
+                total = total + shrink * total_ref[row, :]
+                mixed = mixed + shrink * mixed_ref[span, :]
+            peak_ref[row, :] = peak
+            total_ref[row, :] = total
+            mixed_ref[span, :] = mixed
+
+    block(0)
+    for number in range(1, count):
+        pl.when(place_ref[0] >= number)(lambda number=number: block(number))
+    for head in range(heads):
+        span = slice(head * HEAD_DIM, (head + 1) * HEAD_DIM)
+        row = slice(head, head + 1)
+        out_ref[span, :] = (mixed_ref[span, :] / total_ref[row, :]).astype(out_ref.dtype)
+        log_ref[row, :] = peak_ref[row, :] + jnp.log(total_ref[row, :])
+
+
+def attend_back_kernel(
+    count,
+    heads,
+    place_ref,
+    query_ref,
+    out_ref,
+    grad_ref,
+    log_ref,
+    key_bits_ref,
+    query_bits_ref,
+    *refs
+):
+    pair_refs = refs[:count]
+    query_grad_ref = refs[count]
+    pair_grad_refs = refs[count + 1 : 2 * count + 1]
+    length = query_ref.shape[1]
+    width = heads * HEAD_DIM
+
+    def block(number):
+        pair_ref = pair_refs[number]
+        pair_grad_ref = pair_grad_refs[number]
+        seen = seen_block(number, place_ref, key_bits_ref, query_bits_ref[...], length)
+        for head in range(heads):
+            span = slice(head * HEAD_DIM, (head + 1) * HEAD_DIM)
+            value_span = slice(width + head * HEAD_DIM, width + (head + 1) * HEAD_DIM)
+            row = slice(head, head + 1)
+            queries = query_ref[span, :]
+            grads = grad_ref[span, :]
+            keys = pair_ref[span, :]
+            centre = jnp.sum(
+                grads.astype(jnp.float32) * out_ref[span, :].astype(jnp.float32), 0, keepdims=True
+            )
+            chances = jnp.exp(scores_of(keys, queries, seen) - log_ref[row, :])
+            prob_grad = contract(pair_ref[value_span, :], grads, 0, 0)
+            score_grad = (chances * (prob_grad - centre)).astype(jnp.bfloat16)
+            value_grad = contract(grads, chances.astype(jnp.bfloat16), 1, 1)
+            key_grad = contract(queries, score_grad, 1, 1)
+            query_grad = jnp.dot(keys, score_grad, preferred_element_type=jnp.float32)
+            pair_grad_ref[span, :] = key_grad.astype(pair_grad_ref.dtype)
+            pair_grad_ref[value_span, :] = value_grad.astype(pair_grad_ref.dtype)
+            if number:
+                query_grad = query_grad + query_grad_ref[span, :]
+            query_grad_ref[span, :] = query_grad
+
+    block(0)
+    for number in range(1, count):
+        pl.when(place_ref[0] >= number)(lambda number=number: block(number))
+
+
+def whole():
+    return pl.BlockSpec(memory_space=pltpu.VMEM)
+
+
+def scalars():
+    return pl.BlockSpec(memory_space=pltpu.SMEM)
+
+
+def attend(place, queries, key_bits, query_bits, pairs):
+    width, length = queries.shape
+    heads = width // HEAD_DIM
+    count = len(pairs)
+    return pl.pallas_call(
+        functools.partial(attend_kernel, count, heads),
+        out_shape=(
+            jax.ShapeDtypeStruct((width, length), jnp.bfloat16),
+            jax.ShapeDtypeStruct((heads, length), jnp.float32),
+        ),
+        in_specs=[scalars()] + [whole()] * (3 + count),
+        out_specs=(whole(), whole()),
+        scratch_shapes=[
+            pltpu.VMEM((heads, length), jnp.float32),
+            pltpu.VMEM((heads, length), jnp.float32),
+            pltpu.VMEM((width, length), jnp.float32),
+        ],
+        compiler_params=pltpu.CompilerParams(vmem_limit_bytes=VMEM_BYTES),
+        cost_estimate=pl.CostEstimate(
+            flops=16 * count * width * length * length,
+            transcendentals=count * heads * length * length,
+            bytes_accessed=4 * (count + 2) * width * length,
+        ),
+        name="attend",
+    )(place, queries, key_bits, query_bits, *pairs)
+
+
+def attend_back(place, queries, outs, grads, logs, key_bits, query_bits, pairs):
+    width, length = queries.shape
+    heads = width // HEAD_DIM
+    count = len(pairs)
+    results = pl.pallas_call(
+        functools.partial(attend_back_kernel, count, heads),
+        out_shape=(jax.ShapeDtypeStruct((width, length), jnp.float32),)
+        + (jax.ShapeDtypeStruct((2 * width, length), jnp.float32),)
+        + (jax.ShapeDtypeStruct((2 * width, length), jnp.bfloat16),) * (count - 1),
+        in_specs=[scalars()] + [whole()] * (6 + count),
+        out_specs=(whole(),) * (count + 1),
+        compiler_params=pltpu.CompilerParams(vmem_limit_bytes=VMEM_BYTES),
+        cost_estimate=pl.CostEstimate(
+            flops=40 * count * width * length * length,
+            transcendentals=count * heads * length * length,
+            bytes_accessed=8 * (count + 2) * width * length,
+        ),
+        name="attend_back",
+    )(place, queries, outs, grads, logs, key_bits, query_bits, *pairs)
+    return (results[0], results[1:])
+
+
+def gated_kernel(rows_ref, grads_ref, weights_ref, lowered_ref, routed_ref, parts_ref):
+    rows = rows_ref[...]
+    grads = grads_ref[...]
+    gate_weights = weights_ref[0, 0]
+    up_weights = weights_ref[0, 1]
+    down_weights = weights_ref[0, 2]
+    first = jnp.dot(rows, gate_weights, preferred_element_type=jnp.float32)
+    second = jnp.dot(rows, up_weights, preferred_element_type=jnp.float32)
+    sigma = 1.0 / (1.0 + jnp.exp(-first))
+    swish = first * sigma
+    activated = (swish * second).astype(jnp.bfloat16)
+    activated_grad = jnp.dot(grads, down_weights, preferred_element_type=jnp.float32)
+    first_grad = (activated_grad * second * (sigma + swish * (1.0 - sigma))).astype(jnp.bfloat16)
+    second_grad = (activated_grad * swish).astype(jnp.bfloat16)
+    lowered = contract(activated, down_weights, 1, 1)
+    routed = contract(first_grad, gate_weights, 1, 1) + contract(second_grad, up_weights, 1, 1)
+
+    @pl.when(pl.program_id(0) == 0)
+    def _():
+        lowered_ref[...] = lowered
+        routed_ref[...] = routed
+
+    @pl.when(pl.program_id(0) > 0)
+    def _():
+        lowered_ref[...] += lowered
+        routed_ref[...] += routed
+
+    parts_ref[0, 0] = contract(rows, first_grad, 0, 0).astype(jnp.bfloat16)
+    parts_ref[0, 1] = contract(rows, second_grad, 0, 0).astype(jnp.bfloat16)
+    parts_ref[0, 2] = contract(grads, activated, 0, 0).astype(jnp.bfloat16)
+
+
+def gated(rows, grads, weights, tile):
+    count, model_width = rows.shape
+    chunks, _, _, hidden = weights.shape
+    tiles = hidden // tile
+    fixed = pl.BlockSpec((count, model_width), lambda step: (0, 0))
+    moving = pl.BlockSpec(
+        (1, 3, model_width, tile), lambda step: (step // tiles, 0, 0, step % tiles)
+    )
+    return pl.pallas_call(
+        gated_kernel,
+        grid=(chunks * tiles,),
+        out_shape=(
+            jax.ShapeDtypeStruct((count, model_width), jnp.float32),
+            jax.ShapeDtypeStruct((count, model_width), jnp.float32),
+            jax.ShapeDtypeStruct(weights.shape, jnp.bfloat16),
+        ),
+        in_specs=[fixed, fixed, moving],
+        out_specs=(fixed, fixed, moving),
+        compiler_params=pltpu.CompilerParams(vmem_limit_bytes=VMEM_BYTES),
+        cost_estimate=pl.CostEstimate(
+            flops=18 * count * model_width * chunks * hidden,
+            transcendentals=count * chunks * hidden,
+            bytes_accessed=12 * count * model_width + 12 * chunks * model_width * hidden,
+        ),
+        name="gated",
+    )(rows, grads, weights)
+
+
+def swap(piece, axes, size, step):
+    return lax.ppermute(piece, axes, [(i, i ^ step) for i in range(size)])
+
+
+def pick(stacked, index):
+    return lax.dynamic_index_in_dim(stacked, index, 0, keepdims=False)
+
+
+def share(piece, axes, size):
+    return [piece] + [swap(piece, axes, size, step) for step in range(1, size)]
+
+
+def natural(pieces, index):
+    stacked = jnp.stack(pieces)
+    return [pick(stacked, index ^ other) for other in range(len(pieces))]
+
+
+def turned(field, cosine, sine, backward):
+    half = HEAD_DIM // 2
+    shape = field.shape
+    split = field.reshape(shape[0], -1, 2, half, shape[-1])
+    first_half = split[:, :, 0]
+    second_half = split[:, :, 1]
+    if backward:
+        parts = [
+            first_half * cosine + second_half * sine,
+            second_half * cosine - first_half * sine,
+        ]
+    else:
+        parts = [
+            first_half * cosine - second_half * sine,
+            second_half * cosine + first_half * sine,
+        ]
+    return jnp.stack(parts, 2).reshape(shape)
+
+
+def tree_tables(segments, parents):
+    count = parents.shape[1]
+    labels = jnp.arange(count, dtype=jnp.int32)
+    is_parent = parents[:, :, None] == labels[None, None, :]
+    grand = jnp.sum(jnp.where(is_parent, parents[:, None, :], 0), 2)
+    itself = labels[None, :, None] == labels[None, None, :]
+    table = itself | is_parent | (grand[:, :, None] == labels[None, None, :])
+    member = segments[:, None, :] == labels[None, :, None]
+    lengths = jnp.sum(member.astype(jnp.int32), 2)
+    ahead = jnp.sum(jnp.where(labels[:, None] > labels[None, :], lengths[:, None, :], 0), 2)
+    moving = jnp.sum(jnp.where(table, lengths[:, None, :], 0), 2) - lengths - ahead
+    place = jnp.arange(segments.shape[1], dtype=jnp.int32) + jnp.sum(
+        jnp.where(member, moving[:, :, None], 0), 1
+    )
+    bits = jnp.sum(jnp.where(table, jnp.left_shift(1, labels)[None, None, :], 0), 2)
+    paths = jnp.sum(jnp.where(member, bits[:, :, None], 0), 1)
+    return (place, paths, jnp.left_shift(1, segments))
+
+
+def local_fast(
+    tokens,
+    cotangent,
+    segments,
+    parents,
+    routes,
+    norm_gains,
+    project,
+    mixing,
+    router,
+    expander,
+    reducer,
+    spreader,
+    collector,
+):
+    bf16, f32 = jnp.bfloat16, jnp.float32
+    group_size = lax.axis_size(GROUP)
+    seq_size = lax.axis_size(SEQ)
+    shards = lax.axis_size(TENSOR)
+    member_index = lax.axis_index(GROUP)
+    seq_index = lax.axis_index(SEQ)
+    shard = lax.axis_index(TENSOR)
+    trees, rows, model_width = tokens.shape
+    part_width = project.shape[2]
+    owned = project.shape[1]
+    hidden = spreader.shape[2]
+    slots = CAP // shards
+    quarter = rows // shards
+    place_arg = seq_index.astype(jnp.int32).reshape(1)
+
+    extra = EXPERTS + 2
+    pad = -extra % 128
+    small = jnp.concatenate(
+        [
+            project[0],
+            project[1],
+            project[2],
+            mixing.T,
+            router,
+            norm_gains.T,
+            jnp.zeros((owned, pad), bf16),
+        ],
+        1,
+    )
+    small = lax.all_gather(small, GROUP, axis=0, tiled=True)
+    project_all = small[:, : 3 * part_width]
+    mixing_own = small[:, 3 * part_width : 4 * part_width].T
+    router_all = small[:, 4 * part_width : 4 * part_width + EXPERTS]
+    gains = small[:, 4 * part_width + EXPERTS : 4 * part_width + extra].T.astype(f32)
+    mixing_all = jnp.concatenate(share(mixing_own, TENSOR, shards), 0)
+    shared_weights = lax.all_gather(
+        jnp.concatenate([spreader, collector.T[None]], 0), GROUP, axis=1, tiled=True
+    )
+
+    bundles = jnp.concatenate([expander, reducer.transpose(0, 2, 1)[:, None]], 1)
+    arrived = [
+        pick(bundles, member_index ^ step)
+        if step == 0
+        else swap(pick(bundles, member_index ^ step), GROUP, group_size, step)
+        for step in range(group_size)
+    ]
+    own_expert = jnp.concatenate(natural(arrived, member_index), 1)
+    expert_weights = lax.all_gather(own_expert, TENSOR, axis=0, tiled=False)
+
+    labels = member_index ^ jnp.arange(EXPERTS, dtype=jnp.int32)
+    named = jnp.any(routes[:, None, :, :] == labels[None, :, None, None], 3)
+    earlier = (
+        jnp.arange(rows, dtype=jnp.int32)[:, None] < jnp.arange(rows, dtype=jnp.int32)[None, :]
+    )
+    ranks = jnp.einsum(
+        "bes,st->bet", named.astype(bf16), earlier.astype(bf16), preferred_element_type=f32
+    ).astype(jnp.int32)
+    slot_index = shard * slots + jnp.arange(slots, dtype=jnp.int32)
+    chosen = (
+        (named[:, :, None, :] & (ranks[:, :, None, :] == slot_index[None, None, :, None]))
+        .astype(bf16)
+        .reshape(trees, EXPERTS * slots, rows)
+    )
+
+    def send_rows(field):
+        picked = jnp.einsum("bst,btd->bsd", chosen, field, preferred_element_type=f32).astype(bf16)
+        picked = picked.reshape(trees, EXPERTS, slots, field.shape[-1])
+        pieces = [picked[:, step] for step in range(EXPERTS)]
+        pieces = pieces[:1] + [
+            swap(pieces[step], GROUP, group_size, step) for step in range(1, EXPERTS)
+        ]
+        return jnp.stack(pieces).reshape(EXPERTS * trees * slots, field.shape[-1])
+
+    def return_rows(field):
+        pieces = field.reshape(EXPERTS, trees, slots, field.shape[-1])
+        pieces = [pieces[0]] + [
+            swap(pieces[step], GROUP, group_size, step) for step in range(1, EXPERTS)
+        ]
+        stacked = jnp.stack(pieces, 1).reshape(trees, EXPERTS * slots, field.shape[-1])
+        return jnp.einsum("bst,bsd->btd", chosen, stacked, preferred_element_type=f32)
+
+    upstream_rows = send_rows(cotangent)
+
+    place, paths, key_bits = tree_tables(segments, parents)
+    offset = seq_index * rows
+    own_place = lax.dynamic_slice_in_dim(place, offset, rows, 1).astype(f32)
+    own_paths = lax.dynamic_slice_in_dim(paths, offset, rows, 1)
+    half = HEAD_DIM // 2
+    rates = jnp.exp(-math.log(theta) * 2.0 * jnp.arange(half, dtype=f32) / HEAD_DIM)
+    angle = rates[None, :, None] * own_place[:, None, :]
+    cosine = jnp.cos(angle)[:, None]
+    sine = jnp.sin(angle)[:, None]
+    inputs = tokens.astype(f32)
+    scale_one = lax.rsqrt(jnp.mean(inputs * inputs, -1, keepdims=True) + epsilon)
+    first_in = (inputs * scale_one * gains[0]).astype(bf16)
+    mapped = jnp.einsum("dh,btd->bht", project_all, first_in, preferred_element_type=f32)
+    queries = (
+        turned(mapped[:, :part_width], cosine, sine, False) * HEAD_DIM ** (-0.5)
+    ).astype(bf16)
+    pairs_own = jnp.concatenate(
+        [
+            turned(mapped[:, part_width : 2 * part_width], cosine, sine, False).astype(bf16),
+            mapped[:, 2 * part_width :].astype(bf16),
+        ],
+        1,
+    )
+    pairs = []
+    outs = []
+    logs = []
+    for tree in range(trees):
+        pairs.append(
+            [pairs_own[tree]]
+            + [
+                lax.ppermute(
+                    pairs_own[tree], SEQ, [(i, i + step) for i in range(seq_size - step)]
+                )
+                for step in range(1, seq_size)
+            ]
+        )
+        out, log = attend(
+            place_arg, queries[tree], key_bits[tree][:, None], own_paths[tree][None], pairs[tree]
+        )
+        outs.append(out)
+        logs.append(log)
+    heads = [jnp.concatenate(share(out, TENSOR, shards), 0) for out in outs]
+    second = inputs + jnp.stack(
+        [
+            jnp.einsum("ht,hd->td", head, mixing_all, preferred_element_type=f32)
+            for head in heads
+        ]
+    )
+
+    scale_two = lax.rsqrt(jnp.mean(second * second, -1, keepdims=True) + epsilon)
+    hidden_in = (second * scale_two * gains[1]).astype(bf16)
+    expert_rows = send_rows(hidden_in)
+    flat = (trees * rows, model_width)
+    shared_out, shared_back, shared_parts = gated(
+        hidden_in.reshape(flat), cotangent.reshape(flat), shared_weights[None], 256
+    )
+    row_chances = jax.nn.softmax(jnp.dot(expert_rows, router_all, preferred_element_type=f32), -1)
+    own_label = jnp.arange(EXPERTS, dtype=jnp.int32) == member_index
+    row_gates = jnp.sum(jnp.where(own_label[None], row_chances, 0.0), -1, keepdims=True)
+    row_grads = (row_gates * upstream_rows.astype(f32)).astype(bf16)
+    lowered, routed_back, expert_parts = gated(expert_rows, row_grads, expert_weights, 256)
+    gate_grads = jnp.sum(upstream_rows.astype(f32) * lowered, -1, keepdims=True)
+    lanes = jnp.arange(128, dtype=jnp.int32)[None]
+    back_rows = jnp.concatenate(
+        [
+            routed_back.astype(bf16),
+            jnp.where(lanes == member_index, gate_grads, 0.0).astype(bf16),
+        ],
+        1,
+    )
+    returned_back = return_rows(back_rows)
+    returned_out = return_rows((row_gates * lowered).astype(bf16))
+
+    expert_own = lax.psum_scatter(expert_parts, TENSOR, scatter_dimension=0, tiled=False)
+    blocks = expert_own.reshape(3, group_size, owned, hidden)
+    blocks = [
+        lax.dynamic_index_in_dim(blocks, member_index ^ step, 1, keepdims=False)
+        for step in range(group_size)
+    ]
+    blocks = blocks[:1] + [
+        swap(blocks[step], GROUP, group_size, step) for step in range(1, group_size)
+    ]
+    expert_grads = jnp.stack(natural(blocks, member_index)).astype(f32)
+    expander_grad = expert_grads[:, :2]
+    reducer_grad = expert_grads[:, 2].transpose(0, 2, 1)
+    shared_grads = lax.psum_scatter(
+        shared_parts[0], GROUP, scatter_dimension=1, tiled=True
+    ).astype(f32)
+    spreader_grad = shared_grads[:2]
+    collector_grad = shared_grads[2].T
+
+    branches = lax.psum(
+        (returned_out + shared_out.reshape(trees, rows, model_width)).astype(bf16), TENSOR
+    ).astype(f32)
+    output = (second + branches).astype(bf16)
+
+    def own_rows(field):
+        return lax.dynamic_slice_in_dim(field, shard * quarter, quarter, 1)
+
+    def add_shards(field):
+        pieces = field.astype(bf16)
+        mine = own_rows(pieces).astype(f32)
+        for step in range(1, shards):
+            sent = lax.dynamic_slice_in_dim(pieces, (shard ^ step) * quarter, quarter, 1)
+            mine = mine + swap(sent, TENSOR, shards, step).astype(f32)
+        return mine
+
+    def spread_shards(field):
+        return jnp.concatenate(natural(share(field, TENSOR, shards), shard), 1)
+
+    summed = add_shards(
+        returned_back
+        + jnp.pad(shared_back.reshape(trees, rows, model_width), ((0, 0), (0, 0), (0, 128)))
+    )
+    chance_grad = summed[..., model_width : model_width + EXPERTS]
+    quarter_second = own_rows(second)
+    quarter_scale = own_rows(scale_two)
+    quarter_normed = quarter_second * quarter_scale
+    quarter_hidden = own_rows(hidden_in)
+    logits = jnp.dot(quarter_hidden, router_all, preferred_element_type=f32)
+    chances = jax.nn.softmax(logits, -1)
+    logit_grad = chances * (chance_grad - jnp.sum(chances * chance_grad, -1, keepdims=True))
+    hidden_grad = summed[..., :model_width] + jnp.einsum(
+        "bte,de->btd", logit_grad, router_all.astype(f32), precision=highest
+    )
+    router_part = jnp.einsum(
+        "btd,bte->ed", quarter_hidden.astype(f32), logit_grad, precision=highest
+    )
+    gain_two = jnp.sum(hidden_grad * quarter_normed, (0, 1))
+    scaled_two = hidden_grad * gains[1]
+    second_grad = own_rows(cotangent).astype(f32) + quarter_scale * (
+        scaled_two - quarter_normed * jnp.mean(scaled_two * quarter_normed, -1, keepdims=True)
+    )
+    branch_grad = spread_shards(second_grad.astype(bf16))
+
+    heads_grad = jnp.einsum(
+        "hd,btd->bht", mixing_own, branch_grad, preferred_element_type=f32
+    ).astype(bf16)
+    outs_all = jnp.stack(outs)
+    mixing_part = jnp.einsum("btd,bht->dh", branch_grad, outs_all, preferred_element_type=f32)
+    mapped_grads = []
+    for tree in range(trees):
+        query_grad, pair_grads = attend_back(
+            place_arg,
+            queries[tree],
+            outs[tree],
+            heads_grad[tree],
+            logs[tree],
+            key_bits[tree][:, None],
+            own_paths[tree][None],
+            pairs[tree],
+        )
+        pair_grad = pair_grads[0]
+        for step in range(1, seq_size):
+            pair_grad = pair_grad + lax.ppermute(
+                pair_grads[step], SEQ, [(i + step, i) for i in range(seq_size - step)]
+            ).astype(f32)
+        mapped_grads.append(
+            jnp.concatenate(
+                [
+                    turned(
+                        query_grad[None] * HEAD_DIM ** (-0.5),
+                        cosine[tree : tree + 1],
+                        sine[tree : tree + 1],
+                        True,
+                    ),
+                    turned(
+                        pair_grad[None, :part_width],
+                        cosine[tree : tree + 1],
+                        sine[tree : tree + 1],
+                        True,
+                    ),
+                    pair_grad[None, part_width:],
+                ],
+                1,
+            ).astype(bf16)
+        )
+    mapped_grad = jnp.concatenate(mapped_grads, 0)
+    project_part = jnp.einsum("btd,bht->dh", first_in, mapped_grad, preferred_element_type=f32)
+    first_grad = add_shards(
+        jnp.einsum("bht,dh->btd", mapped_grad, project_all, preferred_element_type=f32)
+    )
+    quarter_scale_one = own_rows(scale_one)
+    quarter_normed_one = own_rows(inputs) * quarter_scale_one
+    gain_one = jnp.sum(first_grad * quarter_normed_one, (0, 1))
+    scaled_one = first_grad * gains[0]
+    input_grad = spread_shards(
+        (
+            second_grad
+            + quarter_scale_one
+            * (
+                scaled_one
+                - quarter_normed_one * jnp.mean(scaled_one * quarter_normed_one, -1, keepdims=True)
+            )
+        ).astype(bf16)
+    )
+
+    small_parts = jnp.concatenate([project_part, mixing_part], 1).astype(bf16)
+    small_grads = lax.psum_scatter(
+        small_parts, GROUP, scatter_dimension=0, tiled=True
+    ).astype(f32)
+    project_grad = (
+        small_grads[:, : 3 * part_width].reshape(owned, 3, part_width).transpose(1, 0, 2)
+    )
+    mixing_grad = small_grads[:, 3 * part_width :].T
+    tiny = lax.psum(
+        jnp.concatenate([router_part, gain_one[None], gain_two[None]], 0),
+        (DP, SEQ, TENSOR),
+    )
+    tiny = lax.dynamic_slice_in_dim(tiny, member_index * owned, owned, 1)
+    router_grad = tiny[:EXPERTS].T
+    gain_grad = tiny[EXPERTS:]
+    return (
+        output,
+        input_grad,
+        gain_grad,
+        project_grad,
+        mixing_grad,
+        router_grad,
+        expander_grad,
+        reducer_grad,
+        spreader_grad,
+        collector_grad,
+    )
+
+
 def solution(mesh):
     in_specs = (
-        P("dp", "seq", None),
-        P("dp", "seq", None),
-        P("dp", None),
-        P("dp", None),
-        P("dp", "seq", None),
-        P(None, ("dp", "seq")),
-        P(None, ("dp", "seq"), "tensor"),
-        P("tensor", ("dp", "seq")),
-        P(("dp", "seq"), None),
-        P(None, None, ("dp", "seq"), "tensor"),
-        P(None, "tensor", ("dp", "seq")),
-        P(None, ("dp", "seq"), "tensor"),
-        P("tensor", ("dp", "seq")),
+        P(DP, SEQ, None),
+        P(DP, SEQ, None),
+        P(DP, None),
+        P(DP, None),
+        P(DP, SEQ, None),
+        P(None, GROUP),
+        P(None, GROUP, TENSOR),
+        P(TENSOR, GROUP),
+        P(GROUP, None),
+        P(None, None, GROUP, TENSOR),
+        P(None, TENSOR, GROUP),
+        P(None, GROUP, TENSOR),
+        P(TENSOR, GROUP),
     )
     out_specs = (
-        P("dp", "seq", None),
-        P("dp", "seq", None),
-        P(None, ("dp", "seq")),
-        P(None, ("dp", "seq"), "tensor"),
-        P("tensor", ("dp", "seq")),
-        P(("dp", "seq"), None),
-        P(None, None, ("dp", "seq"), "tensor"),
-        P(None, "tensor", ("dp", "seq")),
-        P(None, ("dp", "seq"), "tensor"),
-        P("tensor", ("dp", "seq")),
-    )
-    return jax.shard_map(local, mesh=mesh, in_specs=in_specs, out_specs=out_specs, check_vma=False)
+        P(DP, SEQ, None),
+        P(DP, SEQ, None),
+        P(None, GROUP),
+        P(None, GROUP, TENSOR),
+        P(TENSOR, GROUP),
+        P(GROUP, None),
+        P(None, None, GROUP, TENSOR),
+        P(None, TENSOR, GROUP),
+        P(None, GROUP, TENSOR),
+        P(TENSOR, GROUP),
+    )
+    sizes = mesh.shape
+    group_size = sizes[DP] * sizes[SEQ]
+    shards = sizes[TENSOR]
+    fits = group_size == EXPERTS and shards & (shards - 1) == 0 and CAP % shards == 0
+    body = local_fast if fits else local
+    return jax.shard_map(body, mesh=mesh, in_specs=in_specs, out_specs=out_specs, check_vma=False)

time: 2130 us -> 801 us (0.38)
  waiting for transfers between devices: 1240 us -> 342 us
  matrix products: 343 us -> 26.2 us
  blocking collectives: 231 us -> 44.9 us
  starting transfers between devices: 2.73 us -> 155 us
  other arithmetic: 116 us -> 36.1 us
  local copies, waits for them, and re-layouts: 172 us -> 97.5 us
  Pallas kernels: 0 us -> 71.5 us
    reduce_scatter x7 -> x2, waiting for transfers between devices: 679 us -> 52.4 us  [the longest x1 52.4 us: local_fast(): lax.psum_scatter(expert_parts, TENSOR, scatter_dimension=0, tiled=False)]
    dot_general x54 -> x15, matrix products: 341 us -> 24.3 us  [the longest x2 3.34 us: return_rows(): jnp.einsum('bst,bsd->btd', chosen, stacked, preferred_element_type=f32)]
    ppermute x0 -> x75, waiting for transfers between devices: none -> 289 us  [the longest x63 220 us: swap(): return lax.ppermute(piece, axes, [(i, i ^ step) for i in range(size)])]
    unnamed x23 -> x8, waiting for transfers between devices: 288 us -> 0.54 us
    all_gather x9 -> x0, blocking collectives: 225 us -> none  [the longest x1 41.6 us: fetch(): lax.all_gather(project, ('dp', 'seq'), axis=1, tiled=True)]
    all_gather x3, waiting for transfers between devices: 186 us -> 0.04 us  [the longest x1 0.02 us: local_fast(): small = lax.all_gather(small, GROUP, axis=0, tiled=True)]
    ppermute x0 -> x75, starting transfers between devices: none -> 154 us  [the longest x63 96.4 us: swap(): return lax.ppermute(piece, axes, [(i, i ^ step) for i in range(size)])]
    psum x3 -> x1, waiting for transfers between devices: 84 us -> 0.01 us  [local_fast(): lax.psum((returned_out + shared_out.reshape(trees, rows, model_width)).as...]
  transfers between devices with their start and end apart: 18 -> 82, of which waited for: 12 -> 32; matrix products, arithmetic and copies ran while one was open for 16% -> 18% of each run, Pallas kernels for 0% -> 9%
where the time goes in v1:
time: 801 us; the launch traced here: 789 us
  waiting for transfers between devices  342 us (43%)
  starting transfers between devices  155 us (19%)
  local copies, waits for them, and re-layouts  97.5 us (12%)
  Pallas kernels  71.5 us (9%)
  blocking collectives  44.9 us (6%)
  other arithmetic  36.1 us (5%)
  matrix products  26.2 us (3%)
  between operations  16.4 us (2%)
    ppermute x63, waiting for transfers between devices, swap(): return lax.ppermute(piece, axes, [(i, i ^ step) for i in range(size)])  220 us
    ppermute x63, starting transfers between devices, swap(): return lax.ppermute(piece, axes, [(i, i ^ step) for i in range(size)])  96.4 us
    ppermute x6, waiting for transfers between devices, local_fast(): lax.ppermute(pair_grads[step], SEQ, [(i + step, i) for i in range(seq_siz...  68.8 us
    reduce_scatter x1, waiting for transfers between devices, local_fast(): lax.psum_scatter(expert_parts, TENSOR, scatter_dimension=0, tiled=False)  52.4 us
    pallas_call x2, Pallas kernels, gated(): pl.pallas_call(gated_kernel, grid=(chunks * tiles,), out_shape=(jax.Shape...  51.2 us
    unnamed x214, local copies, waits for them, and re-layouts  50 us
    ppermute x6, starting transfers between devices, local_fast(): lax.ppermute(pairs_own[tree], SEQ, [(i, i + step) for i in range(seq_size...  49.7 us
    psum x1, blocking collectives, local_fast(): lax.psum(jnp.concatenate([router_part, gain_one[None], gain_two[None]], 0...  44.9 us
  transfers between devices with their start and end apart: 82, of which 32 were waited for; matrix products, arithmetic and copies ran while one was open for 18% of the time, Pallas kernels for 9%

profile of v1, /device:TPU:0, one launch (start us, length us, event | category | flops | bytes accessed | tf_op | source)
XLA Modules:
  0.0 789.0 jit_solution(11753832775321041969)
XLA Ops:
  25.3 11.7 %collective-permute-done.29 = bf16[3,96,512]{2,1,0:T(8,128)(2,1)} collective-permute-done((bf16[3,96,512]{2,1,0:T(8,128)(2,1)}, bf16[3,96,512]{2,1,0:T(8,128)(2,1)}, u32[]{:S(2)}, u32[]{:S(2)}) %collective-permute-start.29) | collective-permute-done | bytes 294944 | tf_op jit(solution)/shard_map/ppermute | solution.py:724
  56.9 27.9 %collective-permute-done.34 = bf16[3,96,512]{2,1,0:T(8,128)(2,1)S(1)} collective-permute-done((bf16[3,96,512]{2,1,0:T(8,128)(2,1)}, bf16[3,96,512]{2,1,0:T(8,128)(2,1)S(1)}, u32[]{:S(2)}, u32[]{:S(2)}) %collective-permute-start.34) | collective-permute-done | bytes 294944 | tf_op jit(solution)/shard_map/ppermute | solution.py:724
  138.4 6.1 collective-permute-done.27
  158.4 35.8 %collective-permute-start.9 = (bf16[384,512]{1,0:T(8,128)(2,1)S(1)}, bf16[384,512]{1,0:T(8,128)(2,1)S(1)}, u32[]{:S(2)}, u32[]{:S(2)}) collective-permute-start(bf16[384,512]{1,0:T(8,128)(2,1)S(1)} %get-tuple-element.201.refs_0_), channel_id=1, source_target_pairs={{0,4},{4,8},{8,12},{1,5},{5,9},{9,13},{2,6},{6,10},{10,14},{3,7},{... | collective-permute-start | bytes 1179656 | tf_op jit(solution)/shard_map/ppermute | solution.py:906
  212.7 11.9 %collective-permute-done.8 = bf16[192,768]{1,0:T(8,128)(2,1)S(1)} collective-permute-done((bf16[192,768]{1,0:T(8,128)(2,1)S(1)}, bf16[192,768]{1,0:T(8,128)(2,1)S(1)}, u32[]{:S(2)}, u32[]{:S(2)}) %collective-permute-start.8) | collective-permute-done | bytes 294944 | tf_op jit(solution)/shard_map/ppermute | solution.py:724
  226.9 6.2 collective-permute-done.4
  270.3 7.7 collective-permute-start.21
  287.1 14.3 %gated.3 = (f32[1024,768]{1,0:T(8,128)}, f32[1024,768]{1,0:T(8,128)}, bf16[1,3,768,512]{3,2,1,0:T(8,128)(2,1)}) custom-call(bf16[1024,768]{1,0:T(8,128)(2,1)} %bitcast.391, bf16[1024,768]{1,0:T(8,128)(2,1)} %bitcast.453, bf16[1,3,768,512]{3,2,1,0:T(8,128)(2,1)} %bitcast.455), custom_call_target="tpu_custom_call" | custom-call | flops 7247757312 | bytes 14155776 | tf_op jit(solution)/shard_map/gated/pallas_call | solution.py:703
  309.0 36.9 %gated.2 = (f32[768,768]{1,0:T(8,128)}, f32[768,768]{1,0:T(8,128)}, bf16[4,3,768,512]{3,2,1,0:T(8,128)(2,1)}) custom-call(bf16[768,768]{1,0:T(8,128)(2,1)} %bitcast.402, bf16[768,768]{1,0:T(8,128)(2,1)} %fusion.1.grads_ref, bf16[4,3,768,512]{3,2,1,0:T(8,128)(2,1)} %bitcast.454), custom_call_target="tpu_custom_call" | custom-call | flops 21743271936 | bytes 25952256 | tf_op jit(solution)/shard_map/gated/pallas_call | solution.py:703
  356.6 16.2 %collective-permute-done.36 = bf16[2,48,768]{2,1,0:T(8,128)(2,1)S(1)} collective-permute-done((bf16[2,48,768]{2,1,0:T(8,128)(2,1)S(1)}, bf16[2,48,768]{2,1,0:T(8,128)(2,1)S(1)}, u32[]{:S(2)}, u32[]{:S(2)}) %collective-permute-start.36) | collective-permute-done | bytes 147488 | tf_op jit(solution)/shard_map/ppermute | solution.py:724
  373.2 13.2 %collective-permute-done.37 = bf16[2,48,768]{2,1,0:T(8,128)(2,1)S(1)} collective-permute-done((bf16[2,48,768]{2,1,0:T(8,128)(2,1)S(1)}, bf16[2,48,768]{2,1,0:T(8,128)(2,1)S(1)}, u32[]{:S(2)}, u32[]{:S(2)}) %collective-permute-start.37) | collective-permute-done | bytes 147488 | tf_op jit(solution)/shard_map/ppermute | solution.py:724
  425.5 7.2 collective-permute-done.51
  432.7 8.9 %collective-permute-done.52 = bf16[2,128,896]{1,2,0:T(8,128)(2,1)S(1)} collective-permute-done((bf16[2,128,896]{1,2,0:T(8,128)(2,1)S(1)}, bf16[2,128,896]{1,2,0:T(8,128)(2,1)S(1)}, u32[]{:S(2)}, u32[]{:S(2)}) %collective-permute-start.52) | collective-permute-done | bytes 458784 | tf_op jit(solution)/shard_map/ppermute | solution.py:724
  449.9 8.1 %collective-permute-done.54 = bf16[2,128,768]{1,2,0:T(8,128)(2,1)} collective-permute-done((bf16[2,128,768]{1,2,0:T(8,128)(2,1)}, bf16[2,128,768]{1,2,0:T(8,128)(2,1)}, u32[]{:S(2)}, u32[]{:S(2)}) %collective-permute-start.54) | collective-permute-done | bytes 393248 | tf_op jit(solution)/shard_map/ppermute | solution.py:724
  458.1 12.2 %collective-permute-done.55 = bf16[2,128,768]{1,2,0:T(8,128)(2,1)} collective-permute-done((bf16[2,128,768]{1,2,0:T(8,128)(2,1)}, bf16[2,128,768]{1,2,0:T(8,128)(2,1)}, u32[]{:S(2)}, u32[]{:S(2)}) %collective-permute-start.55) | collective-permute-done | bytes 393248 | tf_op jit(solution)/shard_map/ppermute | solution.py:724
  502.8 10.0 %collective-permute-done.56 = bf16[384,512]{1,0:T(8,128)(2,1)S(1)} collective-permute-done((bf16[384,512]{1,0:T(8,128)(2,1)}, bf16[384,512]{1,0:T(8,128)(2,1)S(1)}, u32[]{:S(2)}, u32[]{:S(2)}) %collective-permute-start.56) | collective-permute-done | bytes 393248 | tf_op jit(solution)/shard_map/ppermute | solution.py:1030
  514.1 25.4 %collective-permute-done.57 = bf16[384,512]{1,0:T(8,128)(2,1)S(1)} collective-permute-done((bf16[384,512]{1,0:T(8,128)(2,1)}, bf16[384,512]{1,0:T(8,128)(2,1)S(1)}, u32[]{:S(2)}, u32[]{:S(2)}) %collective-permute-start.57) | collective-permute-done | bytes 393248 | tf_op jit(solution)/shard_map/ppermute | solution.py:1030
  540.8 32.3 %collective-permute-done.60 = bf16[384,512]{1,0:T(8,128)(2,1)S(1)} collective-permute-done((bf16[384,512]{1,0:T(8,128)(2,1)}, bf16[384,512]{1,0:T(8,128)(2,1)S(1)}, u32[]{:S(2)}, u32[]{:S(2)}) %collective-permute-start.60) | collective-permute-done | bytes 393248 | tf_op jit(solution)/shard_map/ppermute | solution.py:1030
  600.0 6.8 collective-permute-done.64
  619.1 44.9 %psum.15 = f32[10,768]{1,0:T(8,128)S(1)} all-reduce(f32[10,768]{1,0:T(8,128)S(1)} %pad_maximum_fusion.18), channel_id=1, replica_groups=mesh['dp'=2,'seq'=4,'tensor'=4] {'dp','seq','tensor'}, use_global_device_ids=true, to_apply=%region_22.23 | all-reduce | flops 7680 | bytes 61440 | tf_op jit(solution)/shard_map/psum | solution.py:1081
  671.0 52.4 %reduce-scatter.6.cloned.1.call-done = bf16[1,3,768,512]{3,2,1,0:T(8,128)(2,1)} async-done(((bf16[4,3,768,512]{3,2,1,0:T(8,128)(2,1)}), bf16[1,3,768,512]{3,2,1,0:T(8,128)(2,1)}) %reduce-scatter.6.cloned.1.call-update) | async-done | bytes 2359312 | tf_op jit(solution)/shard_map/reduce_scatter | solution.py:949
  733.2 7.0 collective-permute-done.68
  741.8 8.9 %collective-permute-done.69 = bf16[3,96,512]{2,1,0:T(8,128)(2,1)S(1)} collective-permute-done((bf16[3,96,512]{2,1,0:T(8,128)(2,1)S(1)}, bf16[3,96,512]{2,1,0:T(8,128)(2,1)S(1)}, u32[]{:S(2)}, u32[]{:S(2)}) %collective-permute-start.69) | collective-permute-done | bytes 294944 | tf_op jit(solution)/shard_map/ppermute | solution.py:724
  754.1 22.8 %collective-permute-done.73 = bf16[3,96,512]{2,1,0:T(8,128)(2,1)S(1)} collective-permute-done((bf16[3,96,512]{2,1,0:T(8,128)(2,1)S(1)}, bf16[3,96,512]{2,1,0:T(8,128)(2,1)S(1)}, u32[]{:S(2)}, u32[]{:S(2)}) %collective-permute-start.73) | collective-permute-done | bytes 294944 | tf_op jit(solution)/shard_map/ppermute | solution.py:724
  (513 shorter events, 337.9 us)
Async XLA Ops:
  7.2 124.0 %all-gather.5.cloned.1.call-start = ((), (), s32[]{:S(2)}) async-start(), calls=%async_computation.3 | async-start | bytes 1548288 | tf_op jit(solution)/shard_map/all_gather | solution.py:822
  11.5 275.5 %all-gather.7.cloned.1.call-start = ((), (), s32[]{:S(2)}) async-start(), calls=%async_computation.4 | async-start | bytes 2654208 | tf_op jit(solution)/shard_map/all_gather | solution.py:828
  13.3 295.7 %all-gather.9.cloned.1.call-start = ((), (), s32[]{:S(2)}) async-start(), calls=%async_computation.8 | async-start | bytes 11796480 | tf_op jit(solution)/shard_map/all_gather | solution.py:840
  37.0 47.9 %collective-permute-start.34 = (bf16[3,96,512]{2,1,0:T(8,128)(2,1)}, bf16[3,96,512]{2,1,0:T(8,128)(2,1)S(1)}, u32[]{:S(2)}, u32[]{:S(2)}) collective-permute-start(bf16[3,96,512]{2,1,0:T(8,128)(2,1)} %get-tuple-element.148), channel_id=1, source_target_pairs={{0,24},{4,28},{8,16},{12,20},{16,8},{20,12},{24,0},{28,4},{1,25},{... | collective-permute-start | bytes 884744 | tf_op jit(solution)/shard_map/ppermute | solution.py:724
  92.1 500.4 %reduce-scatter.8.cloned.1.call-start = ((), (), s32[]{:S(2)}) async-start(), calls=%async_computation.7 | async-start | bytes 2654208 | tf_op jit(solution)/shard_map/reduce_scatter | solution.py:961
  145.4 51.0 %collective-permute-start.1 = (bf16[384,512]{1,0:T(8,128)(2,1)S(1)}, bf16[384,512]{1,0:T(8,128)(2,1)}, u32[]{:S(2)}, u32[]{:S(2)}) collective-permute-start(bf16[384,512]{1,0:T(8,128)(2,1)S(1)} %get-tuple-element.200.refs_0_), channel_id=1, source_target_pairs={{0,8},{4,12},{1,9},{5,13},{2,10},{6,14},{3,11},{7,15},{16,24},{20,... | collective-permute-start | bytes 1179656 | tf_op jit(solution)/shard_map/ppermute | solution.py:906
  147.5 49.0 %collective-permute-start.2 = (bf16[384,512]{1,0:T(8,128)(2,1)S(1)}, bf16[384,512]{1,0:T(8,128)(2,1)}, u32[]{:S(2)}, u32[]{:S(2)}) collective-permute-start(bf16[384,512]{1,0:T(8,128)(2,1)S(1)} %get-tuple-element.200.refs_0_), channel_id=1, source_target_pairs={{0,12},{1,13},{2,14},{3,15},{16,28},{17,29},{18,30},{19,31}} | collective-permute-start | bytes 1179656 | tf_op jit(solution)/shard_map/ppermute | solution.py:906
  151.5 50.8 %collective-permute-start.10 = (bf16[384,512]{1,0:T(8,128)(2,1)S(1)}, bf16[384,512]{1,0:T(8,128)(2,1)}, u32[]{:S(2)}, u32[]{:S(2)}) collective-permute-start(bf16[384,512]{1,0:T(8,128)(2,1)S(1)} %get-tuple-element.201.refs_0_), channel_id=1, source_target_pairs={{0,8},{4,12},{1,9},{5,13},{2,10},{6,14},{3,11},{7,15},{16,24},{20,... | collective-permute-start | bytes 1179656 | tf_op jit(solution)/shard_map/ppermute | solution.py:906
  156.2 46.4 %collective-permute-start.11 = (bf16[384,512]{1,0:T(8,128)(2,1)S(1)}, bf16[384,512]{1,0:T(8,128)(2,1)}, u32[]{:S(2)}, u32[]{:S(2)}) collective-permute-start(bf16[384,512]{1,0:T(8,128)(2,1)S(1)} %get-tuple-element.201.refs_0_), channel_id=1, source_target_pairs={{0,12},{1,13},{2,14},{3,15},{16,28},{17,29},{18,30},{19,31}} | collective-permute-start | bytes 1179656 | tf_op jit(solution)/shard_map/ppermute | solution.py:906
  158.4 45.8 %collective-permute-start.9 = (bf16[384,512]{1,0:T(8,128)(2,1)S(1)}, bf16[384,512]{1,0:T(8,128)(2,1)S(1)}, u32[]{:S(2)}, u32[]{:S(2)}) collective-permute-start(bf16[384,512]{1,0:T(8,128)(2,1)S(1)} %get-tuple-element.201.refs_0_), channel_id=1, source_target_pairs={{0,4},{4,8},{8,12},{1,5},{5,9},{9,13},{2,6},{6,10},{10,14},{3,7},{... | collective-permute-start | bytes 1179656 | tf_op jit(solution)/shard_map/ppermute | solution.py:906
  308.5 304.9 %all-reduce.3.cloned.1.call-start = ((), (), s32[]{:S(2)}) async-start(), calls=%async_computation.5 | async-start | bytes 3145728 | tf_op jit(solution)/shard_map/psum | solution.py:967
  349.3 49.2 %collective-permute-start.43 = (bf16[2,48,896]{2,1,0:T(8,128)(2,1)S(1)}, bf16[2,48,896]{2,1,0:T(8,128)(2,1)S(1)}, u32[]{:S(2)}, u32[]{:S(2)}) collective-permute-start(bf16[2,48,896]{2,1,0:T(8,128)(2,1)S(1)} %bitcast.443), channel_id=1, source_target_pairs={{0,4},{4,0},{8,12},{12,8},{16,20},{20,16},{24,28},{28,24},{1,5},{5... | collective-permute-start | bytes 516104 | tf_op jit(solution)/shard_map/ppermute | solution.py:724
  352.4 51.5 %collective-permute-start.44 = (bf16[2,48,896]{2,1,0:T(8,128)(2,1)S(1)}, bf16[2,48,896]{2,1,0:T(8,128)(2,1)S(1)}, u32[]{:S(2)}, u32[]{:S(2)}) collective-permute-start(bf16[2,48,896]{2,1,0:T(8,128)(2,1)S(1)} %bitcast.442), channel_id=1, source_target_pairs={{0,8},{4,12},{8,0},{12,4},{16,24},{20,28},{24,16},{28,20},{1,9},{5... | collective-permute-start | bytes 516104 | tf_op jit(solution)/shard_map/ppermute | solution.py:724
  353.4 50.6 %collective-permute-start.45 = (bf16[2,48,896]{2,1,0:T(8,128)(2,1)S(1)}, bf16[2,48,896]{2,1,0:T(8,128)(2,1)S(1)}, u32[]{:S(2)}, u32[]{:S(2)}) collective-permute-start(bf16[2,48,896]{2,1,0:T(8,128)(2,1)S(1)} %bitcast.441), channel_id=1, source_target_pairs={{0,12},{4,8},{8,4},{12,0},{16,28},{20,24},{24,20},{28,16},{1,13},{... | collective-permute-start | bytes 516104 | tf_op jit(solution)/shard_map/ppermute | solution.py:724
  354.8 50.8 %collective-permute-start.46 = (bf16[2,48,896]{2,1,0:T(8,128)(2,1)S(1)}, bf16[2,48,896]{2,1,0:T(8,128)(2,1)S(1)}, u32[]{:S(2)}, u32[]{:S(2)}) collective-permute-start(bf16[2,48,896]{2,1,0:T(8,128)(2,1)S(1)} %bitcast.440), channel_id=1, source_target_pairs={{0,16},{4,20},{8,24},{12,28},{16,0},{20,4},{24,8},{28,12},{1,17},{... | collective-permute-start | bytes 516104 | tf_op jit(solution)/shard_map/ppermute | solution.py:724
  449.7 219.2 %reduce-scatter.10.cloned.1.call-start = ((), (), s32[]{:S(2)}) async-start(), calls=%async_computation.9 | async-start | bytes 1327104
  489.6 49.9 %collective-permute-start.57 = (bf16[384,512]{1,0:T(8,128)(2,1)}, bf16[384,512]{1,0:T(8,128)(2,1)S(1)}, u32[]{:S(2)}, u32[]{:S(2)}) collective-permute-start(bf16[384,512]{1,0:T(8,128)(2,1)} %get-tuple-element.40), channel_id=1, source_target_pairs={{8,0},{12,4},{9,1},{13,5},{10,2},{14,6},{11,3},{15,7},{24,16},{28,... | collective-permute-start | bytes 1179656 | tf_op jit(solution)/shard_map/ppermute | solution.py:1030
  490.9 48.6 %collective-permute-start.58 = (bf16[384,512]{1,0:T(8,128)(2,1)}, bf16[384,512]{1,0:T(8,128)(2,1)S(1)}, u32[]{:S(2)}, u32[]{:S(2)}) collective-permute-start(bf16[384,512]{1,0:T(8,128)(2,1)} %get-tuple-element.41), channel_id=1, source_target_pairs={{12,0},{13,1},{14,2},{15,3},{28,16},{29,17},{30,18},{31,19}} | collective-permute-start | bytes 1179656 | tf_op jit(solution)/shard_map/ppermute | solution.py:1030
  500.4 72.7 %collective-permute-start.60 = (bf16[384,512]{1,0:T(8,128)(2,1)}, bf16[384,512]{1,0:T(8,128)(2,1)S(1)}, u32[]{:S(2)}, u32[]{:S(2)}) collective-permute-start(bf16[384,512]{1,0:T(8,128)(2,1)} %get-tuple-element.46), channel_id=1, source_target_pairs={{8,0},{12,4},{9,1},{13,5},{10,2},{14,6},{11,3},{15,7},{24,16},{28,... | collective-permute-start | bytes 1179656 | tf_op jit(solution)/shard_map/ppermute | solution.py:1030
  512.8 60.4 %collective-permute-start.61 = (bf16[384,512]{1,0:T(8,128)(2,1)S(1)}, bf16[384,512]{1,0:T(8,128)(2,1)S(1)}, u32[]{:S(2)}, u32[]{:S(2)}) collective-permute-start(bf16[384,512]{1,0:T(8,128)(2,1)S(1)} %copy-done.69), channel_id=1, source_target_pairs={{12,0},{13,1},{14,2},{15,3},{28,16},{29,17},{30,18},{31,19}} | collective-permute-start | bytes 1179656 | tf_op jit(solution)/shard_map/ppermute | solution.py:1030
  580.6 142.7 %reduce-scatter.6.cloned.1.call-start = ((), (), s32[]{:S(2)}) async-start(), calls=%async_computation.6 | async-start | bytes 11796480 | tf_op jit(solution)/shard_map/reduce_scatter | solution.py:949
  610.7 54.7 %collective-permute-start.65 = (bf16[2,128,768]{1,2,0:T(8,128)(2,1)S(1)}, bf16[2,128,768]{1,2,0:T(8,128)(2,1)}, u32[]{:S(2)}, u32[]{:S(2)}) collective-permute-start(bf16[2,128,768]{1,2,0:T(8,128)(2,1)S(1)} %add_convert_fusion.3), channel_id=1, source_target_pairs={{0,1},{1,0},{2,3},{3,2},{4,5},{5,4},{6,7},{7,6},{8,9},{9,8},{10,11... | collective-permute-start | bytes 1179656 | tf_op jit(solution)/shard_map/ppermute | solution.py:724
  611.5 53.9 %collective-permute-start.66 = (bf16[2,128,768]{1,2,0:T(8,128)(2,1)S(1)}, bf16[2,128,768]{1,2,0:T(8,128)(2,1)}, u32[]{:S(2)}, u32[]{:S(2)}) collective-permute-start(bf16[2,128,768]{1,2,0:T(8,128)(2,1)S(1)} %add_convert_fusion.3), channel_id=1, source_target_pairs={{0,2},{1,3},{2,0},{3,1},{4,6},{5,7},{6,4},{7,5},{8,10},{9,11},{10,... | collective-permute-start | bytes 1179656 | tf_op jit(solution)/shard_map/ppermute | solution.py:724
  613.4 52.0 %collective-permute-start.67 = (bf16[2,128,768]{1,2,0:T(8,128)(2,1)S(1)}, bf16[2,128,768]{1,2,0:T(8,128)(2,1)}, u32[]{:S(2)}, u32[]{:S(2)}) collective-permute-start(bf16[2,128,768]{1,2,0:T(8,128)(2,1)S(1)} %add_convert_fusion.3), channel_id=1, source_target_pairs={{0,3},{1,2},{2,1},{3,0},{4,7},{5,6},{6,5},{7,4},{8,11},{9,10},{10,... | collective-permute-start | bytes 1179656 | tf_op jit(solution)/shard_map/ppermute | solution.py:724
  (132 other events, 1986.4 us)
Sparse Core Ops, SparseCore 0:
  11.6 70.7 all-gather.4
  85.2 66.2 all-gather.6
  153.0 81.4 all-gather.8
  308.6 76.1 reduce-scatter.7
  449.8 54.3 all-reduce.2
  580.7 62.5 reduce-scatter.9
  645.9 77.4 reduce-scatter.5

commit v2 on v1

--- a/solution.py
+++ b/solution.py
@@ -497,6 +497,14 @@
     )
 
 
+def spans(head, width):
+    if isinstance(head, int):
+        start = head * HEAD_DIM
+    else:
+        start = pl.multiple_of(head * HEAD_DIM, HEAD_DIM)
+    return (pl.ds(start, HEAD_DIM), pl.ds(width + start, HEAD_DIM), pl.ds(head, 1))
+
+
 def scores_of(keys, queries, seen):
     return jnp.where(seen, contract(keys, queries, 0, 0), -1e30)
 
@@ -511,23 +519,23 @@
     return seen
 
 
-def attend_kernel(count, heads, place_ref, query_ref, key_bits_ref, query_bits_ref, *refs):
-    pair_refs = refs[:count]
-    out_ref, log_ref, peak_ref, total_ref, mixed_ref = refs[count:]
+def attend_kernel(number, final, heads, place_ref, query_ref, key_bits_ref, query_bits_ref, *refs):
+    pair_ref = refs[0]
+    if number:
+        old_peak_ref, old_total_ref, old_mixed_ref = refs[1:4]
+    peak_ref, total_ref, mixed_ref = refs[-3:]
     length = query_ref.shape[1]
     width = heads * HEAD_DIM
 
-    def block(number):
-        pair_ref = pair_refs[number]
+    def block():
         seen = seen_block(number, place_ref, key_bits_ref, query_bits_ref[...], length)
-        for head in range(heads):
-            span = slice(head * HEAD_DIM, (head + 1) * HEAD_DIM)
-            value_span = slice(width + head * HEAD_DIM, width + (head + 1) * HEAD_DIM)
-            row = slice(head, head + 1)
+
+        def one(head, _):
+            span, value_span, row = spans(head, width)
             scores = scores_of(pair_ref[span, :], query_ref[span, :], seen)
             peak = jnp.max(scores, 0, keepdims=True)
             if number:
-                before = peak_ref[row, :]
+                before = old_peak_ref[row, :]
                 peak = jnp.maximum(before, peak)
                 shrink = jnp.exp(before - peak)
             expo = jnp.exp(scores - peak)
@@ -538,24 +546,35 @@
                 preferred_element_type=jnp.float32,
             )
             if number:
-                total = total + shrink * total_ref[row, :]
-                mixed = mixed + shrink * mixed_ref[span, :]
+                total = total + shrink * old_total_ref[row, :]
+                mixed = mixed + shrink * old_mixed_ref[span, :]
             peak_ref[row, :] = peak
             total_ref[row, :] = total
             mixed_ref[span, :] = mixed
-
-    block(0)
-    for number in range(1, count):
-        pl.when(place_ref[0] >= number)(lambda number=number: block(number))
-    for head in range(heads):
-        span = slice(head * HEAD_DIM, (head + 1) * HEAD_DIM)
-        row = slice(head, head + 1)
-        out_ref[span, :] = (mixed_ref[span, :] / total_ref[row, :]).astype(out_ref.dtype)
-        log_ref[row, :] = peak_ref[row, :] + jnp.log(total_ref[row, :])
+            return 0
+
+        lax.fori_loop(0, heads, one, 0)
+
+    def keep():
+        peak_ref[...] = old_peak_ref[...]
+        total_ref[...] = old_total_ref[...]
+        mixed_ref[...] = old_mixed_ref[...]
+
+    if number:
+        pl.when(place_ref[0] >= number)(block)
+        pl.when(place_ref[0] < number)(keep)
+    else:
+        block()
+    if final:
+        out_ref, log_ref = refs[4:6]
+        for head in range(heads):
+            span, _, row = spans(head, width)
+            out_ref[span, :] = (mixed_ref[span, :] / total_ref[row, :]).astype(out_ref.dtype)
+            log_ref[row, :] = peak_ref[row, :] + jnp.log(total_ref[row, :])
 
 
 def attend_back_kernel(
-    count,
+    number,
     heads,
     place_ref,
     query_ref,
@@ -564,22 +583,18 @@
     log_ref,
     key_bits_ref,
     query_bits_ref,
+    pair_ref,
     *refs
 ):
-    pair_refs = refs[:count]
-    query_grad_ref = refs[count]
-    pair_grad_refs = refs[count + 1 : 2 * count + 1]
+    query_grad_ref, pair_grad_ref = refs[-2:]
     length = query_ref.shape[1]
     width = heads * HEAD_DIM
 
-    def block(number):
-        pair_ref = pair_refs[number]
-        pair_grad_ref = pair_grad_refs[number]
+    def block():
         seen = seen_block(number, place_ref, key_bits_ref, query_bits_ref[...], length)
-        for head in range(heads):
-            span = slice(head * HEAD_DIM, (head + 1) * HEAD_DIM)
-            value_span = slice(width + head * HEAD_DIM, width + (head + 1) * HEAD_DIM)
-            row = slice(head, head + 1)
+
+        def one(head, _):
+            span, value_span, row = spans(head, width)
             queries = query_ref[span, :]
             grads = grad_ref[span, :]
             keys = pair_ref[span, :]
@@ -594,70 +609,81 @@
             query_grad = jnp.dot(keys, score_grad, preferred_element_type=jnp.float32)
             pair_grad_ref[span, :] = key_grad.astype(pair_grad_ref.dtype)
             pair_grad_ref[value_span, :] = value_grad.astype(pair_grad_ref.dtype)
-            if number:
-                query_grad = query_grad + query_grad_ref[span, :]
+            if len(refs) > 2:
+                query_grad = query_grad + refs[0][span, :]
             query_grad_ref[span, :] = query_grad
-
-    block(0)
-    for number in range(1, count):
-        pl.when(place_ref[0] >= number)(lambda number=number: block(number))
-
-
-def whole():
-    return pl.BlockSpec(memory_space=pltpu.VMEM)
-
-
-def scalars():
-    return pl.BlockSpec(memory_space=pltpu.SMEM)
-
-
-def attend(place, queries, key_bits, query_bits, pairs):
-    width, length = queries.shape
-    heads = width // HEAD_DIM
-    count = len(pairs)
+            return 0
+
+        lax.fori_loop(0, heads, one, 0)
+
+    def empty():
+        pair_grad_ref[...] = jnp.zeros_like(pair_grad_ref)
+        if len(refs) > 2:
+            query_grad_ref[...] = refs[0][...]
+        else:
+            query_grad_ref[...] = jnp.zeros_like(query_grad_ref)
+
+    if number:
+        pl.when(place_ref[0] >= number)(block)
+        pl.when(place_ref[0] < number)(empty)
+    else:
+        block()
+
+
+def per_tree(array):
+    return pl.BlockSpec((None,) + array.shape[1:], lambda tree: (tree, 0, 0))
+
+
+def attend_call(kernel, name, place, operands, results, flops):
+    trees, width, length = operands[0].shape
     return pl.pallas_call(
-        functools.partial(attend_kernel, count, heads),
-        out_shape=(
-            jax.ShapeDtypeStruct((width, length), jnp.bfloat16),
-            jax.ShapeDtypeStruct((heads, length), jnp.float32),
-        ),
-        in_specs=[scalars()] + [whole()] * (3 + count),
-        out_specs=(whole(), whole()),
-        scratch_shapes=[
-            pltpu.VMEM((heads, length), jnp.float32),
-            pltpu.VMEM((heads, length), jnp.float32),
-            pltpu.VMEM((width, length), jnp.float32),
-        ],
+        kernel,
+        grid=(trees,),
+        out_shape=results,
+        in_specs=[pl.BlockSpec(memory_space=pltpu.SMEM)] + [per_tree(value) for value in operands],
+        out_specs=tuple(per_tree(value) for value in results),
         compiler_params=pltpu.CompilerParams(vmem_limit_bytes=VMEM_BYTES),
         cost_estimate=pl.CostEstimate(
-            flops=16 * count * width * length * length,
-            transcendentals=count * heads * length * length,
-            bytes_accessed=4 * (count + 2) * width * length,
+            flops=flops * trees * width * length * length,
+            transcendentals=trees * width * length * length // HEAD_DIM,
+            bytes_accessed=16 * trees * width * length,
         ),
-        name="attend",
-    )(place, queries, key_bits, query_bits, *pairs)
-
-
-def attend_back(place, queries, outs, grads, logs, key_bits, query_bits, pairs):
-    width, length = queries.shape
+        name=name,
+    )(place, *operands)
+
+
+def attend(number, final, place, queries, key_bits, query_bits, pair, state):
+    trees, width, length = queries.shape
     heads = width // HEAD_DIM
-    count = len(pairs)
-    results = pl.pallas_call(
-        functools.partial(attend_back_kernel, count, heads),
-        out_shape=(jax.ShapeDtypeStruct((width, length), jnp.float32),)
-        + (jax.ShapeDtypeStruct((2 * width, length), jnp.float32),)
-        + (jax.ShapeDtypeStruct((2 * width, length), jnp.bfloat16),) * (count - 1),
-        in_specs=[scalars()] + [whole()] * (6 + count),
-        out_specs=(whole(),) * (count + 1),
-        compiler_params=pltpu.CompilerParams(vmem_limit_bytes=VMEM_BYTES),
-        cost_estimate=pl.CostEstimate(
-            flops=40 * count * width * length * length,
-            transcendentals=count * heads * length * length,
-            bytes_accessed=8 * (count + 2) * width * length,
+    row = jax.ShapeDtypeStruct((trees, heads, length), jnp.float32)
+    field = jax.ShapeDtypeStruct(queries.shape, jnp.float32)
+    results = (row, row, field)
+    if final:
+        results = (jax.ShapeDtypeStruct(queries.shape, jnp.bfloat16), row) + results
+    return attend_call(
+        functools.partial(attend_kernel, number, final, heads),
+        "attend",
+        place,
+        (queries, key_bits, query_bits, pair) + tuple(state),
+        results,
+        16,
+    )
+
+
+def attend_back(number, kind, place, operands):
+    trees, width, length = operands[0].shape
+    heads = width // HEAD_DIM
+    return attend_call(
+        functools.partial(attend_back_kernel, number, heads),
+        "attend_back",
+        place,
+        operands,
+        (
+            jax.ShapeDtypeStruct((trees, width, length), jnp.float32),
+            jax.ShapeDtypeStruct((trees, 2 * width, length), kind),
         ),
-        name="attend_back",
-    )(place, queries, outs, grads, logs, key_bits, query_bits, *pairs)
-    return (results[0], results[1:])
+        40,
+    )
 
 
 def gated_kernel(rows_ref, grads_ref, weights_ref, lowered_ref, routed_ref, parts_ref):
@@ -735,6 +761,14 @@
 def natural(pieces, index):
     stacked = jnp.stack(pieces)
     return [pick(stacked, index ^ other) for other in range(len(pieces))]
+
+
+def tied(*values):
+    return lax.optimization_barrier(values)
+
+
+def route(blocks):
+    return lax.all_to_all(blocks, GROUP, split_axis=0, concat_axis=0)
 
 
 def turned(field, cosine, sine, backward):
@@ -825,21 +859,7 @@
     router_all = small[:, 4 * part_width : 4 * part_width + EXPERTS]
     gains = small[:, 4 * part_width + EXPERTS : 4 * part_width + extra].T.astype(f32)
     mixing_all = jnp.concatenate(share(mixing_own, TENSOR, shards), 0)
-    shared_weights = lax.all_gather(
-        jnp.concatenate([spreader, collector.T[None]], 0), GROUP, axis=1, tiled=True
-    )
-
-    bundles = jnp.concatenate([expander, reducer.transpose(0, 2, 1)[:, None]], 1)
-    arrived = [
-        pick(bundles, member_index ^ step)
-        if step == 0
-        else swap(pick(bundles, member_index ^ step), GROUP, group_size, step)
-        for step in range(group_size)
-    ]
-    own_expert = jnp.concatenate(natural(arrived, member_index), 1)
-    expert_weights = lax.all_gather(own_expert, TENSOR, axis=0, tiled=False)
-
-    labels = member_index ^ jnp.arange(EXPERTS, dtype=jnp.int32)
+    labels = jnp.arange(EXPERTS, dtype=jnp.int32)
     named = jnp.any(routes[:, None, :, :] == labels[None, :, None, None], 3)
     earlier = (
         jnp.arange(rows, dtype=jnp.int32)[:, None] < jnp.arange(rows, dtype=jnp.int32)[None, :]
@@ -856,22 +876,13 @@
 
     def send_rows(field):
         picked = jnp.einsum("bst,btd->bsd", chosen, field, preferred_element_type=f32).astype(bf16)
-        picked = picked.reshape(trees, EXPERTS, slots, field.shape[-1])
-        pieces = [picked[:, step] for step in range(EXPERTS)]
-        pieces = pieces[:1] + [
-            swap(pieces[step], GROUP, group_size, step) for step in range(1, EXPERTS)
-        ]
-        return jnp.stack(pieces).reshape(EXPERTS * trees * slots, field.shape[-1])
+        picked = picked.reshape(trees, EXPERTS, slots, field.shape[-1]).swapaxes(0, 1)
+        return route(picked).reshape(EXPERTS * trees * slots, field.shape[-1])
 
     def return_rows(field):
-        pieces = field.reshape(EXPERTS, trees, slots, field.shape[-1])
-        pieces = [pieces[0]] + [
-            swap(pieces[step], GROUP, group_size, step) for step in range(1, EXPERTS)
-        ]
-        stacked = jnp.stack(pieces, 1).reshape(trees, EXPERTS * slots, field.shape[-1])
-        return jnp.einsum("bst,bsd->btd", chosen, stacked, preferred_element_type=f32)
-
-    upstream_rows = send_rows(cotangent)
+        back = route(field.reshape(EXPERTS, trees, slots, field.shape[-1])).swapaxes(0, 1)
+        back = back.reshape(trees, EXPERTS * slots, field.shape[-1])
+        return jnp.einsum("bst,bsd->btd", chosen, back, preferred_element_type=f32)
 
     place, paths, key_bits = tree_tables(segments, parents)
     offset = seq_index * rows
@@ -896,44 +907,56 @@
         ],
         1,
     )
-    pairs = []
-    outs = []
-    logs = []
-    for tree in range(trees):
-        pairs.append(
-            [pairs_own[tree]]
-            + [
-                lax.ppermute(
-                    pairs_own[tree], SEQ, [(i, i + step) for i in range(seq_size - step)]
-                )
-                for step in range(1, seq_size)
-            ]
-        )
-        out, log = attend(
-            place_arg, queries[tree], key_bits[tree][:, None], own_paths[tree][None], pairs[tree]
-        )
-        outs.append(out)
-        logs.append(log)
-    heads = [jnp.concatenate(share(out, TENSOR, shards), 0) for out in outs]
-    second = inputs + jnp.stack(
-        [
-            jnp.einsum("ht,hd->td", head, mixing_all, preferred_element_type=f32)
-            for head in heads
-        ]
-    )
+    pairs = [pairs_own]
+    for _ in range(1, seq_size):
+        pairs.append(lax.ppermute(pairs[-1], SEQ, [(i, i + 1) for i in range(seq_size - 1)]))
+    key_column = key_bits[:, :, None]
+    path_row = own_paths[:, None, :]
+    state = ()
+    for number in range(seq_size):
+        state = attend(
+            number,
+            number == seq_size - 1,
+            place_arg,
+            queries,
+            key_column,
+            path_row,
+            pairs[number],
+            state,
+        )
+    outs, logs = state[:2]
+
+    bundles = jnp.concatenate([expander, reducer.transpose(0, 2, 1)[:, None]], 1)
+    own_expert = route(bundles).swapaxes(0, 1).reshape(3, model_width, hidden)
+    expert_weights = lax.all_gather(own_expert, TENSOR, axis=0, tiled=False)
+    shared_bundle = jnp.concatenate([spreader, collector.T[None]], 0)
+    shared_bundle, expert_weights = tied(shared_bundle, expert_weights)
+    shared_weights = lax.all_gather(
+        shared_bundle, GROUP, axis=1, tiled=True
+    )
+    heads = jnp.concatenate(
+        [outs] + [swap(outs, TENSOR, shards, step) for step in range(1, shards)], 1
+    )
+    upstream_rows = send_rows(cotangent)
+    heads, upstream_rows = tied(heads, upstream_rows)
+    second = inputs + jnp.einsum("bht,hd->btd", heads, mixing_all, preferred_element_type=f32)
 
     scale_two = lax.rsqrt(jnp.mean(second * second, -1, keepdims=True) + epsilon)
     hidden_in = (second * scale_two * gains[1]).astype(bf16)
-    expert_rows = send_rows(hidden_in)
-    flat = (trees * rows, model_width)
-    shared_out, shared_back, shared_parts = gated(
-        hidden_in.reshape(flat), cotangent.reshape(flat), shared_weights[None], 256
-    )
+    expert_rows, shared_weights = tied(send_rows(hidden_in), shared_weights)
     row_chances = jax.nn.softmax(jnp.dot(expert_rows, router_all, preferred_element_type=f32), -1)
     own_label = jnp.arange(EXPERTS, dtype=jnp.int32) == member_index
     row_gates = jnp.sum(jnp.where(own_label[None], row_chances, 0.0), -1, keepdims=True)
     row_grads = (row_gates * upstream_rows.astype(f32)).astype(bf16)
     lowered, routed_back, expert_parts = gated(expert_rows, row_grads, expert_weights, 256)
+    flat = (trees * rows, model_width)
+    shared_out, shared_back, shared_parts = gated(
+        hidden_in.reshape(flat),
+        cotangent.reshape(flat),
+        shared_weights[None],
+        256,
+    )
+    expert_own = lax.psum_scatter(expert_parts, TENSOR, scatter_dimension=0, tiled=False)
     gate_grads = jnp.sum(upstream_rows.astype(f32) * lowered, -1, keepdims=True)
     lanes = jnp.arange(128, dtype=jnp.int32)[None]
     back_rows = jnp.concatenate(
@@ -944,31 +967,6 @@
         1,
     )
     returned_back = return_rows(back_rows)
-    returned_out = return_rows((row_gates * lowered).astype(bf16))
-
-    expert_own = lax.psum_scatter(expert_parts, TENSOR, scatter_dimension=0, tiled=False)
-    blocks = expert_own.reshape(3, group_size, owned, hidden)
-    blocks = [
-        lax.dynamic_index_in_dim(blocks, member_index ^ step, 1, keepdims=False)
-        for step in range(group_size)
-    ]
-    blocks = blocks[:1] + [
-        swap(blocks[step], GROUP, group_size, step) for step in range(1, group_size)
-    ]
-    expert_grads = jnp.stack(natural(blocks, member_index)).astype(f32)
-    expander_grad = expert_grads[:, :2]
-    reducer_grad = expert_grads[:, 2].transpose(0, 2, 1)
-    shared_grads = lax.psum_scatter(
-        shared_parts[0], GROUP, scatter_dimension=1, tiled=True
-    ).astype(f32)
-    spreader_grad = shared_grads[:2]
-    collector_grad = shared_grads[2].T
-
-    branches = lax.psum(
-        (returned_out + shared_out.reshape(trees, rows, model_width)).astype(bf16), TENSOR
-    ).astype(f32)
-    output = (second + branches).astype(bf16)
-
     def own_rows(field):
         return lax.dynamic_slice_in_dim(field, shard * quarter, quarter, 1)
 
@@ -987,6 +985,7 @@
         returned_back
         + jnp.pad(shared_back.reshape(trees, rows, model_width), ((0, 0), (0, 0), (0, 128)))
     )
+    summed, expert_own = tied(summed, expert_own)
     chance_grad = summed[..., model_width : model_width + EXPERTS]
     quarter_second = own_rows(second)
     quarter_scale = own_rows(scale_two)
@@ -999,7 +998,7 @@
         "bte,de->btd", logit_grad, router_all.astype(f32), precision=highest
     )
     router_part = jnp.einsum(
-        "btd,bte->ed", quarter_hidden.astype(f32), logit_grad, precision=highest
+        "btd,bte->de", quarter_hidden.astype(f32), logit_grad, precision=highest
     )
     gain_two = jnp.sum(hidden_grad * quarter_normed, (0, 1))
     scaled_two = hidden_grad * gains[1]
@@ -1007,57 +1006,59 @@
         scaled_two - quarter_normed * jnp.mean(scaled_two * quarter_normed, -1, keepdims=True)
     )
     branch_grad = spread_shards(second_grad.astype(bf16))
+    returned_out = return_rows((row_gates * lowered).astype(bf16))
+    branch_grad, returned_out = tied(branch_grad, returned_out)
+    partial_out = (returned_out + shared_out.reshape(trees, rows, model_width)).astype(bf16)
+    branches = lax.psum(partial_out, TENSOR).astype(f32)
+    branches, shared_parts = tied(branches, shared_parts)
+    shared_grads = lax.psum_scatter(
+        shared_parts[0], GROUP, scatter_dimension=1, tiled=True
+    ).astype(f32)
+    spreader_grad = shared_grads[:2]
+    collector_grad = shared_grads[2].T
+    output = (second + branches).astype(bf16)
 
     heads_grad = jnp.einsum(
         "hd,btd->bht", mixing_own, branch_grad, preferred_element_type=f32
     ).astype(bf16)
-    outs_all = jnp.stack(outs)
-    mixing_part = jnp.einsum("btd,bht->dh", branch_grad, outs_all, preferred_element_type=f32)
-    mapped_grads = []
-    for tree in range(trees):
-        query_grad, pair_grads = attend_back(
+    mixing_part = jnp.einsum("btd,bht->dh", branch_grad, outs, preferred_element_type=f32)
+    query_grad = ()
+    pair_grads = []
+    for number in range(seq_size - 1, -1, -1):
+        query_grad, pair_grad = attend_back(
+            number,
+            bf16 if number == seq_size - 1 else f32,
             place_arg,
-            queries[tree],
-            outs[tree],
-            heads_grad[tree],
-            logs[tree],
-            key_bits[tree][:, None],
-            own_paths[tree][None],
-            pairs[tree],
-        )
-        pair_grad = pair_grads[0]
-        for step in range(1, seq_size):
-            pair_grad = pair_grad + lax.ppermute(
-                pair_grads[step], SEQ, [(i + step, i) for i in range(seq_size - step)]
-            ).astype(f32)
-        mapped_grads.append(
-            jnp.concatenate(
-                [
-                    turned(
-                        query_grad[None] * HEAD_DIM ** (-0.5),
-                        cosine[tree : tree + 1],
-                        sine[tree : tree + 1],
-                        True,
-                    ),
-                    turned(
-                        pair_grad[None, :part_width],
-                        cosine[tree : tree + 1],
-                        sine[tree : tree + 1],
-                        True,
-                    ),
-                    pair_grad[None, part_width:],
-                ],
-                1,
-            ).astype(bf16)
-        )
-    mapped_grad = jnp.concatenate(mapped_grads, 0)
+            (queries, outs, heads_grad, logs, key_column, path_row, pairs[number])
+            + ((query_grad,) if pair_grads else ()),
+        )
+        pair_grads.append(pair_grad)
+    blocks = expert_own.reshape(3, group_size, owned, hidden).swapaxes(0, 1)
+    expert_home = route(blocks)
+    pair_grad, expert_home = tied(pair_grads[0], expert_home)
+    expert_grads = expert_home.astype(f32)
+    for addend in pair_grads[1:]:
+        moved = lax.ppermute(
+            pair_grad.astype(bf16), SEQ, [(i + 1, i) for i in range(seq_size - 1)]
+        )
+        pair_grad = addend + moved.astype(f32)
+    expander_grad = expert_grads[:, :2]
+    reducer_grad = expert_grads[:, 2].transpose(0, 2, 1)
+    query_grad = query_grad * HEAD_DIM ** (-0.5)
+    mapped_grad = jnp.concatenate(
+        [
+            turned(query_grad, cosine, sine, True),
+            turned(pair_grad[:, :part_width], cosine, sine, True),
+            pair_grad[:, part_width:],
+        ],
+        1,
+    ).astype(bf16)
     project_part = jnp.einsum("btd,bht->dh", first_in, mapped_grad, preferred_element_type=f32)
     first_grad = add_shards(
         jnp.einsum("bht,dh->btd", mapped_grad, project_all, preferred_element_type=f32)
     )
     quarter_scale_one = own_rows(scale_one)
     quarter_normed_one = own_rows(inputs) * quarter_scale_one
-    gain_one = jnp.sum(first_grad * quarter_normed_one, (0, 1))
     scaled_one = first_grad * gains[0]
     input_grad = spread_shards(
         (
@@ -1070,21 +1071,32 @@
         ).astype(bf16)
     )
 
-    small_parts = jnp.concatenate([project_part, mixing_part], 1).astype(bf16)
-    small_grads = lax.psum_scatter(
-        small_parts, GROUP, scatter_dimension=0, tiled=True
-    ).astype(f32)
+    small_parts = jnp.concatenate(
+        [
+            project_part,
+            mixing_part,
+            router_part,
+            gain_two[:, None],
+            jnp.zeros((model_width, -(4 * part_width + EXPERTS + 1) % 128), f32),
+        ],
+        1,
+    ).astype(bf16)
+    small_grads = jnp.sum(
+        route(small_parts.reshape(group_size, owned, -1)).astype(f32),
+        0,
+    )
     project_grad = (
         small_grads[:, : 3 * part_width].reshape(owned, 3, part_width).transpose(1, 0, 2)
     )
-    mixing_grad = small_grads[:, 3 * part_width :].T
+    mixing_grad = small_grads[:, 3 * part_width : 4 * part_width].T
+    rest = small_grads[:, 4 * part_width : 4 * part_width + EXPERTS + 1]
+    gain_one = jnp.sum(project_grad * project.astype(f32), (0, 2)) / norm_gains[0].astype(f32)
     tiny = lax.psum(
-        jnp.concatenate([router_part, gain_one[None], gain_two[None]], 0),
-        (DP, SEQ, TENSOR),
-    )
-    tiny = lax.dynamic_slice_in_dim(tiny, member_index * owned, owned, 1)
+        jnp.concatenate([rest.T, gain_one[None]], 0),
+        TENSOR,
+    )
     router_grad = tiny[:EXPERTS].T
-    gain_grad = tiny[EXPERTS:]
+    gain_grad = jnp.stack([tiny[EXPERTS + 1], tiny[EXPERTS]])
     return (
         output,
         input_grad,

time: 801 us -> 650 us (0.81)
  waiting for transfers between devices: 342 us -> 265 us
  starting transfers between devices: 155 us -> 78.9 us
  local copies, waits for them, and re-layouts: 97.5 us -> 66.7 us
  other arithmetic: 36.1 us -> 58.1 us
  Pallas kernels: 71.5 us -> 84.6 us
    ppermute x63 -> x18, waiting for transfers between devices: 220 us -> 72.5 us  [swap(): return lax.ppermute(piece, axes, [(i, i ^ step) for i in range(size)])]
    all_to_all x0 -> x6, waiting for transfers between devices: none -> 105 us  [route(): return lax.all_to_all(blocks, GROUP, split_axis=0, concat_axis=0)]
    ppermute x63 -> x18, starting transfers between devices: 96.4 us -> 12 us  [swap(): return lax.ppermute(piece, axes, [(i, i ^ step) for i in range(size)])]
    reduce_scatter x1, waiting for transfers between devices: 52.4 us -> 0.01 us  [local_fast(): lax.psum_scatter(expert_parts, TENSOR, scatter_dimension=0, tiled=False)]
    psum x1, blocking collectives: 44.9 us -> 7.57 us  [local_fast(): tiny = lax.psum(jnp.concatenate([rest.T, gain_one[None]], 0), TENSOR)]
    all_to_all x0 -> x1, blocking collectives: none -> 37.1 us  [route(): return lax.all_to_all(blocks, GROUP, split_axis=0, concat_axis=0)]
    all_to_all x0 -> x6, starting transfers between devices: none -> 36.5 us  [route(): return lax.all_to_all(blocks, GROUP, split_axis=0, concat_axis=0)]
    unnamed x214 -> x121, local copies, waits for them, and re-layouts: 50 us -> 15.5 us
  transfers between devices with their start and end apart: 82 -> 36, of which waited for: 32 -> 21; matrix products, arithmetic and copies ran while one was open for 18% -> 21% of each run, Pallas kernels for 9% -> 7%
where the time goes in v2:
time: 650 us; the launch traced here: 642 us
  waiting for transfers between devices  265 us (41%)
  Pallas kernels  84.6 us (13%)
  starting transfers between devices  78.9 us (12%)
  local copies, waits for them, and re-layouts  66.7 us (10%)
  other arithmetic  58.1 us (9%)
  blocking collectives  44.6 us (7%)
  matrix products  28.5 us (4%)
  between operations  15.4 us (2%)
    all_to_all x6, waiting for transfers between devices, route(): return lax.all_to_all(blocks, GROUP, split_axis=0, concat_axis=0)  105 us
    ppermute x18, waiting for transfers between devices, swap(): return lax.ppermute(piece, axes, [(i, i ^ step) for i in range(size)])  72.5 us
    pallas_call x2, Pallas kernels, gated(): pl.pallas_call(gated_kernel, grid=(chunks * tiles,), out_shape=(jax.Shape...  51.1 us
    ppermute x3, waiting for transfers between devices, local_fast(): lax.ppermute(pair_grad.astype(bf16), SEQ, [(i + 1, i) for i in range(seq_...  39.4 us
    all_to_all x1, blocking collectives, route(): return lax.all_to_all(blocks, GROUP, split_axis=0, concat_axis=0)  37.1 us
    all_to_all x6, starting transfers between devices, route(): return lax.all_to_all(blocks, GROUP, split_axis=0, concat_axis=0)  36.5 us
    pallas_call x8, Pallas kernels, attend_call(): pl.pallas_call(kernel, grid=(trees,), out_shape=results, in_specs=[pl.Blo...  33.5 us
    ppermute x3, starting transfers between devices, local_fast(): lax.ppermute(pairs[-1], SEQ, [(i, i + 1) for i in range(seq_size - 1)])  25.6 us
  transfers between devices with their start and end apart: 36, of which 21 were waited for; matrix products, arithmetic and copies ran while one was open for 21% of the time, Pallas kernels for 7%

profile of v2, /device:TPU:0, one launch (start us, length us, event | category | flops | bytes accessed | tf_op | source)
XLA Modules:
  0.0 641.8 jit_solution(10114212428226731131)
XLA Ops:
  10.5 7.4 %all-to-all-start.2 = ((bf16[8,3,96,512]{3,2,1,0:T(8,128)(2,1)}), bf16[8,3,96,512]{3,2,1,0:T(8,128)(2,1)S(1)}, u32[]{:S(2)}, u32[]{:S(2)}) async-start(bf16[8,3,96,512]{3,2,1,0:T(8,128)(2,1)} %pad_maximum_fusion), calls=%async_computation.2 | async-start | bytes 4718592 | tf_op jit(solution)/shard_map/all_to_all | solution.py:771
  19.2 64.0 %all-to-all-done.2 = bf16[8,3,96,512]{3,2,1,0:T(8,128)(2,1)S(1)} async-done(((bf16[8,3,96,512]{3,2,1,0:T(8,128)(2,1)}), bf16[8,3,96,512]{3,2,1,0:T(8,128)(2,1)S(1)}, u32[]{:S(2)}, u32[]{:S(2)}) %all-to-all-start.2) | async-done | bytes 2359328 | tf_op jit(solution)/shard_map/all_to_all | solution.py:771
  101.8 15.4 %collective-permute-done.refs_0_.pair_ref = bf16[2,384,512]{2,1,0:T(8,128)(2,1)} collective-permute-done((bf16[2,384,512]{2,1,0:T(8,128)(2,1)S(1)}, bf16[2,384,512]{2,1,0:T(8,128)(2,1)}, u32[]{:S(2)}, u32[]{:S(2)}) %collective-permute-start) | collective-permute-done | bytes 786464 | tf_op jit(solution)/shard_map/ppermute | solution.py:912
  130.7 9.4 %collective-permute-done.1.refs_0_.pair_ref = bf16[2,384,512]{2,1,0:T(8,128)(2,1)} collective-permute-done((bf16[2,384,512]{2,1,0:T(8,128)(2,1)}, bf16[2,384,512]{2,1,0:T(8,128)(2,1)}, u32[]{:S(2)}, u32[]{:S(2)}) %collective-permute-start.1) | collective-permute-done | bytes 786464 | tf_op jit(solution)/shard_map/ppermute | solution.py:912
  140.1 15.7 %collective-permute-start.2 = (bf16[2,384,512]{2,1,0:T(8,128)(2,1)}, bf16[2,384,512]{2,1,0:T(8,128)(2,1)}, u32[]{:S(2)}, u32[]{:S(2)}) collective-permute-start(bf16[2,384,512]{2,1,0:T(8,128)(2,1)} %collective-permute-done.1.refs_0_.pair_ref), channel_id=1, source_target_pairs={{0,4},{4,8},{8,12},{1,5},{5,9},{9,13},{2,6},{6,10},{10,14},{3,7},{... | collective-permute-start | bytes 2359304 | tf_op jit(solution)/shard_map/ppermute | solution.py:912
  163.2 6.0 attend.4
  184.2 6.4 %collective-permute-done.4 = bf16[2,192,512]{2,1,0:T(8,128)(2,1)} collective-permute-done((bf16[2,192,512]{2,1,0:T(8,128)(2,1)}, bf16[2,192,512]{2,1,0:T(8,128)(2,1)}, u32[]{:S(2)}, u32[]{:S(2)}) %collective-permute-start.4) | collective-permute-done | bytes 393248 | tf_op jit(solution)/shard_map/ppermute | solution.py:750
  190.6 7.5 %collective-permute-done.5 = bf16[2,192,512]{2,1,0:T(8,128)(2,1)} collective-permute-done((bf16[2,192,512]{2,1,0:T(8,128)(2,1)}, bf16[2,192,512]{2,1,0:T(8,128)(2,1)}, u32[]{:S(2)}, u32[]{:S(2)}) %collective-permute-start.5) | collective-permute-done | bytes 393248 | tf_op jit(solution)/shard_map/ppermute | solution.py:750
  217.7 11.0 %all-to-all-start.1 = ((bf16[8,2,48,768]{3,2,1,0:T(8,128)(2,1)}), bf16[8,2,48,768]{3,2,1,0:T(8,128)(2,1)}, u32[]{:S(2)}, u32[]{:S(2)}) async-start(bf16[8,2,48,768]{3,2,1,0:T(8,128)(2,1)} %bitcast.169), calls=%async_computation.1 | async-start | bytes 2359296 | tf_op jit(solution)/shard_map/all_to_all | solution.py:771
  229.1 30.3 %all-to-all-done.1 = bf16[8,2,48,768]{3,2,1,0:T(8,128)(2,1)} async-done(((bf16[8,2,48,768]{3,2,1,0:T(8,128)(2,1)}), bf16[8,2,48,768]{3,2,1,0:T(8,128)(2,1)}, u32[]{:S(2)}, u32[]{:S(2)}) %all-to-all-start.1) | async-done | bytes 1179680 | tf_op jit(solution)/shard_map/all_to_all | solution.py:771
  262.5 36.8 %gated.2 = (f32[768,768]{1,0:T(8,128)}, f32[768,768]{1,0:T(8,128)}, bf16[4,3,768,512]{3,2,1,0:T(8,128)(2,1)}) custom-call(bf16[768,768]{1,0:T(8,128)(2,1)} %bitcast.24.rows_ref, bf16[768,768]{1,0:T(8,128)(2,1)} %fusion.1.grads_ref, bf16[4,3,768,512]{3,2,1,0:T(8,128)(2,1)} %all-gather.6.cloned.1.call-done.weights_ref), custom_call_target="tpu_custom_call" | custom-call | flops 21743271936 | bytes 25952256 | tf_op jit(solution)/shard_map/gated/pallas_call | solution.py:729
  303.5 37.1 %all_to_all.35 = bf16[8,2,48,896]{3,2,1,0:T(8,128)(2,1)} all-to-all(bf16[8,2,48,896]{3,2,1,0:T(8,128)(2,1)S(1)} %bitcast.167), channel_id=1, replica_groups=mesh['dp'=2,'seq'=4,'tensor'=4] {'dp','seq'}, dimensions={0} | all-to-all | bytes 2752512 | tf_op jit(solution)/shard_map/all_to_all | solution.py:771
  346.9 14.3 %gated.3 = (f32[1024,768]{1,0:T(8,128)}, f32[1024,768]{1,0:T(8,128)}, bf16[1,3,768,512]{3,2,1,0:T(8,128)(2,1)}) custom-call(bf16[1024,768]{1,0:T(8,128)(2,1)} %bitcast.183, bf16[1024,768]{1,0:T(8,128)(2,1)} %bitcast.222, bf16[1,3,768,512]{3,2,1,0:T(8,128)(2,1)} %bitcast.223), custom_call_target="tpu_custom_call" | custom-call | flops 7247757312 | bytes 14155776 | tf_op jit(solution)/shard_map/gated/pallas_call | solution.py:729
  370.0 14.7 %collective-permute-done.10 = bf16[2,128,896]{1,2,0:T(8,128)(2,1)S(1)} collective-permute-done((bf16[2,128,896]{1,2,0:T(8,128)(2,1)S(1)}, bf16[2,128,896]{1,2,0:T(8,128)(2,1)S(1)}, u32[]{:S(2)}, u32[]{:S(2)}) %collective-permute-start.10) | collective-permute-done | bytes 458784 | tf_op jit(solution)/shard_map/ppermute | solution.py:750
  384.7 8.3 %collective-permute-done.11 = bf16[2,128,896]{1,2,0:T(8,128)(2,1)S(1)} collective-permute-done((bf16[2,128,896]{1,2,0:T(8,128)(2,1)S(1)}, bf16[2,128,896]{1,2,0:T(8,128)(2,1)S(1)}, u32[]{:S(2)}, u32[]{:S(2)}) %collective-permute-start.11) | collective-permute-done | bytes 458784 | tf_op jit(solution)/shard_map/ppermute | solution.py:750
  424.5 6.8 %collective-permute-done.14 = bf16[2,128,768]{1,2,0:T(8,128)(2,1)} collective-permute-done((bf16[2,128,768]{1,2,0:T(8,128)(2,1)S(1)}, bf16[2,128,768]{1,2,0:T(8,128)(2,1)}, u32[]{:S(2)}, u32[]{:S(2)}) %collective-permute-start.14) | collective-permute-done | bytes 393248 | tf_op jit(solution)/shard_map/ppermute | solution.py:750
  449.1 10.4 %all-to-all-done.5 = bf16[8,3,96,512]{3,2,1,0:T(8,128)(2,1)S(1)} async-done(((bf16[8,3,96,512]{3,2,1,0:T(8,128)(2,1)}), bf16[8,3,96,512]{3,2,1,0:T(8,128)(2,1)S(1)}, u32[]{:S(2)}, u32[]{:S(2)}) %all-to-all-start.5) | async-done | bytes 2359328 | tf_op jit(solution)/shard_map/all_to_all | solution.py:771
  469.0 11.7 %collective-permute-done.15 = bf16[2,384,512]{2,1,0:T(8,128)(2,1)S(1)} collective-permute-done((bf16[2,384,512]{2,1,0:T(8,128)(2,1)}, bf16[2,384,512]{2,1,0:T(8,128)(2,1)S(1)}, u32[]{:S(2)}, u32[]{:S(2)}) %collective-permute-start.15) | collective-permute-done | bytes 786464 | tf_op jit(solution)/shard_map/ppermute | solution.py:1041
  492.4 14.5 %all-reduce.3.cloned.1.call-done = bf16[2,512,768]{1,2,0:T(8,128)(2,1)} async-done(((bf16[2,512,768]{1,2,0:T(8,128)(2,1)}), bf16[2,512,768]{1,2,0:T(8,128)(2,1)}) %all-reduce.3.cloned.1.call-update) | async-done | bytes 1572880 | tf_op jit(solution)/shard_map/psum | solution.py:1012
  519.9 8.1 %attend_back.7 = (f32[2,192,512]{2,1,0:T(8,128)}, f32[2,384,512]{2,1,0:T(8,128)}) custom-call(s32[1]{0:T(128)} %bitcast.place_ref, bf16[2,192,512]{2,1,0:T(8,128)(2,1)} %bitcast.214, bf16[2,192,512]{2,1,0:T(8,128)(2,1)} %get-tuple-element.58.out_ref, bf16[2,192,512]{2,1,0:T(8,128)(2,1)} %fusion.5.grad_ref, f32[2,3,512]{2,1,0:T(4,128)} %get-tuple-element.75.log_ref, ...), custom_call_target="tpu_custom_call" | custom-call | flops 4026531840 | bytes 3145728 | tf_op jit(solution)/shard_map/attend_back/pallas_call | solution.py:639
  529.3 27.7 %collective-permute-done.17 = bf16[2,384,512]{2,1,0:T(8,128)(2,1)} collective-permute-done((bf16[2,384,512]{2,1,0:T(8,128)(2,1)}, bf16[2,384,512]{2,1,0:T(8,128)(2,1)}, u32[]{:S(2)}, u32[]{:S(2)}) %collective-permute-start.17) | collective-permute-done | bytes 786464 | tf_op jit(solution)/shard_map/ppermute | solution.py:1041
  590.8 7.6 %collective-permute-done.20 = bf16[2,128,768]{1,2,0:T(8,128)(2,1)S(1)} collective-permute-done((bf16[2,128,768]{1,2,0:T(8,128)(2,1)}, bf16[2,128,768]{1,2,0:T(8,128)(2,1)S(1)}, u32[]{:S(2)}, u32[]{:S(2)}) %collective-permute-start.20) | collective-permute-done | bytes 393248 | tf_op jit(solution)/shard_map/ppermute | solution.py:750
  604.1 7.5 %reduce-scatter.5.cloned.1.call-done = bf16[3,96,512]{2,1,0:T(8,128)(2,1)} async-done(((bf16[3,768,512]{2,1,0:T(8,128)(2,1)}), bf16[3,96,512]{2,1,0:T(8,128)(2,1)}) %reduce-scatter.5.cloned.1.call-update) | async-done | bytes 294928 | tf_op jit(solution)/shard_map/reduce_scatter | solution.py:1014
  625.1 7.6 %psum.15 = f32[10,96]{1,0:T(8,128)S(1)} all-reduce(f32[10,96]{1,0:T(8,128)S(1)} %pad_maximum_fusion.15), channel_id=1, replica_groups=mesh['dp'=2,'seq'=4,'tensor'=4] {'tensor'}, use_global_device_ids=true, to_apply=%region_24.25 | all-reduce | flops 960 | bytes 7680 | tf_op jit(solution)/shard_map/psum | solution.py:1094
  (323 shorter events, 240.2 us)
Async XLA Ops:
  10.5 72.7 %all-to-all-start.2 = ((bf16[8,3,96,512]{3,2,1,0:T(8,128)(2,1)}), bf16[8,3,96,512]{3,2,1,0:T(8,128)(2,1)S(1)}, u32[]{:S(2)}, u32[]{:S(2)}) async-start(bf16[8,3,96,512]{3,2,1,0:T(8,128)(2,1)} %pad_maximum_fusion), calls=%async_computation.2 | async-start | bytes 4718592 | tf_op jit(solution)/shard_map/all_to_all | solution.py:771
  17.9 73.5 %all-gather.4.cloned.1.call-start = ((), (), s32[]{:S(2)}) async-start(), calls=%async_computation.9 | async-start | bytes 1548288 | tf_op jit(solution)/shard_map/all_gather | solution.py:856
  19.1 156.1 %all-gather.6.cloned.1.call-start = ((), (), s32[]{:S(2)}) async-start(), calls=%async_computation.10 | async-start | bytes 11796480 | tf_op jit(solution)/shard_map/all_gather | solution.py:931
  97.1 20.2 %collective-permute-start = (bf16[2,384,512]{2,1,0:T(8,128)(2,1)S(1)}, bf16[2,384,512]{2,1,0:T(8,128)(2,1)}, u32[]{:S(2)}, u32[]{:S(2)}) collective-permute-start(bf16[2,384,512]{2,1,0:T(8,128)(2,1)S(1)} %pad_maximum_fusion.8.refs_0_.pair_ref), channel_id=1, source_target_pairs={{0,4},{4,8},{8,12},{1,5},{5,9},{9,13},{2,6},{6,10},{10,14},{3,7},{... | collective-permute-start | bytes 2359304 | tf_op jit(solution)/shard_map/ppermute | solution.py:912
  117.3 22.8 %collective-permute-start.1 = (bf16[2,384,512]{2,1,0:T(8,128)(2,1)}, bf16[2,384,512]{2,1,0:T(8,128)(2,1)}, u32[]{:S(2)}, u32[]{:S(2)}) collective-permute-start(bf16[2,384,512]{2,1,0:T(8,128)(2,1)} %collective-permute-done.refs_0_.pair_ref), channel_id=1, source_target_pairs={{0,4},{4,8},{8,12},{1,5},{5,9},{9,13},{2,6},{6,10},{10,14},{3,7},{... | collective-permute-start | bytes 2359304 | tf_op jit(solution)/shard_map/ppermute | solution.py:912
  126.4 74.3 %all-to-all-start = ((bf16[8,2,48,768]{3,2,1,0:T(8,128)(2,1)}), bf16[8,2,48,768]{3,2,1,0:T(8,128)(2,1)S(1)}, u32[]{:S(2)}, u32[]{:S(2)}) async-start(bf16[8,2,48,768]{3,2,1,0:T(8,128)(2,1)} %bitcast.168), calls=%async_computation | async-start | bytes 2359296 | tf_op jit(solution)/shard_map/all_to_all | solution.py:771
  130.0 129.4 %all-gather.8.cloned.1.call-start = ((), (), s32[]{:S(2)}) async-start(), calls=%async_computation.11 | async-start | bytes 2654208 | tf_op jit(solution)/shard_map/all_gather | solution.py:934
  140.1 35.1 %collective-permute-start.2 = (bf16[2,384,512]{2,1,0:T(8,128)(2,1)}, bf16[2,384,512]{2,1,0:T(8,128)(2,1)}, u32[]{:S(2)}, u32[]{:S(2)}) collective-permute-start(bf16[2,384,512]{2,1,0:T(8,128)(2,1)} %collective-permute-done.1.refs_0_.pair_ref), channel_id=1, source_target_pairs={{0,4},{4,8},{8,12},{1,5},{5,9},{9,13},{2,6},{6,10},{10,14},{3,7},{... | collective-permute-start | bytes 2359304 | tf_op jit(solution)/shard_map/ppermute | solution.py:912
  179.9 18.2 %collective-permute-start.5 = (bf16[2,192,512]{2,1,0:T(8,128)(2,1)}, bf16[2,192,512]{2,1,0:T(8,128)(2,1)}, u32[]{:S(2)}, u32[]{:S(2)}) collective-permute-start(bf16[2,192,512]{2,1,0:T(8,128)(2,1)} %get-tuple-element.58.out_ref), channel_id=1, source_target_pairs={{0,3},{1,2},{2,1},{3,0},{4,7},{5,6},{6,5},{7,4},{8,11},{9,10},{10,... | collective-permute-start | bytes 1179656 | tf_op jit(solution)/shard_map/ppermute | solution.py:750
  182.3 18.4 %collective-permute-start.6 = (bf16[192,768]{1,0:T(8,128)(2,1)}, bf16[192,768]{1,0:T(8,128)(2,1)}, u32[]{:S(2)}, u32[]{:S(2)}) collective-permute-start(bf16[192,768]{1,0:T(8,128)(2,1)} %bitcast.215), channel_id=1, source_target_pairs={{0,1},{1,0},{2,3},{3,2},{4,5},{5,4},{6,7},{7,6},{8,9},{9,8},{10,11... | collective-permute-start | bytes 884744 | tf_op jit(solution)/shard_map/ppermute | solution.py:750
  182.7 22.7 %collective-permute-start.7 = (bf16[192,768]{1,0:T(8,128)(2,1)}, bf16[192,768]{1,0:T(8,128)(2,1)}, u32[]{:S(2)}, u32[]{:S(2)}) collective-permute-start(bf16[192,768]{1,0:T(8,128)(2,1)} %bitcast.216), channel_id=1, source_target_pairs={{0,2},{1,3},{2,0},{3,1},{4,6},{5,7},{6,4},{7,5},{8,10},{9,11},{10,... | collective-permute-start | bytes 884744 | tf_op jit(solution)/shard_map/ppermute | solution.py:750
  184.2 26.6 %collective-permute-start.8 = (bf16[192,768]{1,0:T(8,128)(2,1)}, bf16[192,768]{1,0:T(8,128)(2,1)}, u32[]{:S(2)}, u32[]{:S(2)}) collective-permute-start(bf16[192,768]{1,0:T(8,128)(2,1)} %bitcast.217), channel_id=1, source_target_pairs={{0,3},{1,2},{2,1},{3,0},{4,7},{5,6},{6,5},{7,4},{8,11},{9,10},{10,... | collective-permute-start | bytes 884744 | tf_op jit(solution)/shard_map/ppermute | solution.py:750
  217.7 41.7 %all-to-all-start.1 = ((bf16[8,2,48,768]{3,2,1,0:T(8,128)(2,1)}), bf16[8,2,48,768]{3,2,1,0:T(8,128)(2,1)}, u32[]{:S(2)}, u32[]{:S(2)}) async-start(bf16[8,2,48,768]{3,2,1,0:T(8,128)(2,1)} %bitcast.169), calls=%async_computation.1 | async-start | bytes 2359296 | tf_op jit(solution)/shard_map/all_to_all | solution.py:771
  228.7 166.5 %reduce-scatter.3.cloned.1.call-start = ((), (), s32[]{:S(2)}) async-start(), calls=%async_computation.12 | async-start | bytes 11796480 | tf_op jit(solution)/shard_map/reduce_scatter | solution.py:959
  340.6 58.0 %all-to-all-start.4 = ((bf16[8,2,48,768]{3,2,1,0:T(8,128)(2,1)}), bf16[8,2,48,768]{3,2,1,0:T(8,128)(2,1)}, u32[]{:S(2)}, u32[]{:S(2)}) async-start(bf16[8,2,48,768]{3,2,1,0:T(8,128)(2,1)} %bitcast.49), calls=%async_computation.5 | async-start | bytes 2359296 | tf_op jit(solution)/shard_map/all_to_all | solution.py:771
  369.4 23.7 %collective-permute-start.11 = (bf16[2,128,896]{1,2,0:T(8,128)(2,1)S(1)}, bf16[2,128,896]{1,2,0:T(8,128)(2,1)S(1)}, u32[]{:S(2)}, u32[]{:S(2)}) collective-permute-start(bf16[2,128,896]{1,2,0:T(8,128)(2,1)S(1)} %get-tuple-element.192), channel_id=1, source_target_pairs={{0,3},{1,2},{2,1},{3,0},{4,7},{5,6},{6,5},{7,4},{8,11},{9,10},{10,... | collective-permute-start | bytes 1376264 | tf_op jit(solution)/shard_map/ppermute | solution.py:750
  369.4 23.7 %collective-permute-start.9 = (bf16[2,128,896]{1,2,0:T(8,128)(2,1)S(1)}, bf16[2,128,896]{1,2,0:T(8,128)(2,1)S(1)}, u32[]{:S(2)}, u32[]{:S(2)}) collective-permute-start(bf16[2,128,896]{1,2,0:T(8,128)(2,1)S(1)} %get-tuple-element.191), channel_id=1, source_target_pairs={{0,1},{1,0},{2,3},{3,2},{4,5},{5,4},{6,7},{7,6},{8,9},{9,8},{10,11... | collective-permute-start | bytes 1376264 | tf_op jit(solution)/shard_map/ppermute | solution.py:750
  398.5 61.0 %all-to-all-start.5 = ((bf16[8,3,96,512]{3,2,1,0:T(8,128)(2,1)}), bf16[8,3,96,512]{3,2,1,0:T(8,128)(2,1)S(1)}, u32[]{:S(2)}, u32[]{:S(2)}) async-start(bf16[8,3,96,512]{3,2,1,0:T(8,128)(2,1)} %bitcast.163), calls=%async_computation.6 | async-start | bytes 4718592 | tf_op jit(solution)/shard_map/all_to_all | solution.py:771
  403.9 103.0 %all-reduce.3.cloned.1.call-start = ((), (), s32[]{:S(2)}) async-start(), calls=%async_computation.13 | async-start | bytes 3145728 | tf_op jit(solution)/shard_map/psum | solution.py:1012
  459.5 21.2 %collective-permute-start.15 = (bf16[2,384,512]{2,1,0:T(8,128)(2,1)}, bf16[2,384,512]{2,1,0:T(8,128)(2,1)S(1)}, u32[]{:S(2)}, u32[]{:S(2)}) collective-permute-start(bf16[2,384,512]{2,1,0:T(8,128)(2,1)} %get-tuple-element.85), channel_id=1, source_target_pairs={{4,0},{8,4},{12,8},{5,1},{9,5},{13,9},{6,2},{10,6},{14,10},{7,3},{... | collective-permute-start | bytes 2359304 | tf_op jit(solution)/shard_map/ppermute | solution.py:1041
  465.3 146.3 %reduce-scatter.5.cloned.1.call-start = ((), (), s32[]{:S(2)}) async-start(), calls=%async_computation.14 | async-start | bytes 2654208 | tf_op jit(solution)/shard_map/reduce_scatter | solution.py:1014
  483.5 30.5 %collective-permute-start.16 = (bf16[2,384,512]{2,1,0:T(8,128)(2,1)S(1)}, bf16[2,384,512]{2,1,0:T(8,128)(2,1)}, u32[]{:S(2)}, u32[]{:S(2)}) collective-permute-start(bf16[2,384,512]{2,1,0:T(8,128)(2,1)S(1)} %add_convert_fusion.4), channel_id=1, source_target_pairs={{4,0},{8,4},{12,8},{5,1},{9,5},{13,9},{6,2},{10,6},{14,10},{7,3},{... | collective-permute-start | bytes 2359304 | tf_op jit(solution)/shard_map/ppermute | solution.py:1041
  517.0 40.0 %collective-permute-start.17 = (bf16[2,384,512]{2,1,0:T(8,128)(2,1)}, bf16[2,384,512]{2,1,0:T(8,128)(2,1)}, u32[]{:S(2)}, u32[]{:S(2)}) collective-permute-start(bf16[2,384,512]{2,1,0:T(8,128)(2,1)} %add_convert_fusion.3), channel_id=1, source_target_pairs={{4,0},{8,4},{12,8},{5,1},{9,5},{13,9},{6,2},{10,6},{14,10},{7,3},{... | collective-permute-start | bytes 2359304 | tf_op jit(solution)/shard_map/ppermute | solution.py:1041
  569.1 53.1 %all-to-all-start.6 = ((bf16[8,96,896]{2,1,0:T(8,128)(2,1)}), bf16[8,96,896]{2,1,0:T(8,128)(2,1)}, u32[]{:S(2)}, u32[]{:S(2)}) async-start(bf16[8,96,896]{2,1,0:T(8,128)(2,1)} %concatenate.61), calls=%async_computation.7 | async-start | bytes 2752512 | tf_op jit(solution)/shard_map/all_to_all | solution.py:771
  (67 other events, 744.3 us)
Sparse Core Ops, SparseCore 0:
  21.4 69.9 all-gather.3
  93.5 63.3 all-gather.5
  175.3 58.5 all-gather.7
  299.4 80.6 reduce-scatter.2
  465.5 41.3 all-reduce.2
  510.6 101.0 reduce-scatter.4

commit v3 on v2

--- a/solution.py
+++ b/solution.py
@@ -6,6 +6,7 @@
 import jax.numpy as jnp
 from jax import lax
 from jax.experimental import pallas as pl
+from jax.experimental.layout import Layout, with_layout_constraint
 from jax.experimental.pallas import tpu as pltpu
 from jax.sharding import PartitionSpec as P
 
@@ -489,6 +490,8 @@
 
 
 VMEM_BYTES = 56 << 20
+TILE = 256
+ROWS = 256
 
 
 def contract(left, right, left_dim, right_dim):
@@ -686,36 +689,41 @@
     )
 
 
-def gated_kernel(rows_ref, grads_ref, weights_ref, lowered_ref, routed_ref, parts_ref):
-    rows = rows_ref[...]
-    grads = grads_ref[...]
-    gate_weights = weights_ref[0, 0]
-    up_weights = weights_ref[0, 1]
-    down_weights = weights_ref[0, 2]
-    first = jnp.dot(rows, gate_weights, preferred_element_type=jnp.float32)
-    second = jnp.dot(rows, up_weights, preferred_element_type=jnp.float32)
-    sigma = 1.0 / (1.0 + jnp.exp(-first))
-    swish = first * sigma
-    activated = (swish * second).astype(jnp.bfloat16)
-    activated_grad = jnp.dot(grads, down_weights, preferred_element_type=jnp.float32)
-    first_grad = (activated_grad * second * (sigma + swish * (1.0 - sigma))).astype(jnp.bfloat16)
-    second_grad = (activated_grad * swish).astype(jnp.bfloat16)
-    lowered = contract(activated, down_weights, 1, 1)
-    routed = contract(first_grad, gate_weights, 1, 1) + contract(second_grad, up_weights, 1, 1)
-
+def gated_kernel(
+    rows_ref, grads_ref, weights_ref, lowered_ref, routed_ref, first_ref, second_ref, active_ref
+):
     @pl.when(pl.program_id(0) == 0)
     def _():
-        lowered_ref[...] = lowered
-        routed_ref[...] = routed
-
-    @pl.when(pl.program_id(0) > 0)
-    def _():
-        lowered_ref[...] += lowered
-        routed_ref[...] += routed
-
-    parts_ref[0, 0] = contract(rows, first_grad, 0, 0).astype(jnp.bfloat16)
-    parts_ref[0, 1] = contract(rows, second_grad, 0, 0).astype(jnp.bfloat16)
-    parts_ref[0, 2] = contract(grads, activated, 0, 0).astype(jnp.bfloat16)
+        lowered_ref[...] = jnp.zeros_like(lowered_ref)
+        routed_ref[...] = jnp.zeros_like(routed_ref)
+
+    def some(index, _):
+        part = (pl.ds(pl.multiple_of(index * ROWS, ROWS), ROWS), slice(None))
+        rows = rows_ref[part]
+        grads = grads_ref[part]
+        gate_weights = weights_ref[0, 0]
+        up_weights = weights_ref[0, 1]
+        down_weights = weights_ref[0, 2]
+        first = jnp.dot(rows, gate_weights, preferred_element_type=jnp.float32)
+        second = jnp.dot(rows, up_weights, preferred_element_type=jnp.float32)
+        sigma = 1.0 / (1.0 + jnp.exp(-first))
+        swish = first * sigma
+        activated = (swish * second).astype(jnp.bfloat16)
+        activated_grad = jnp.dot(grads, down_weights, preferred_element_type=jnp.float32)
+        first_grad = (activated_grad * second * (sigma + swish * (1.0 - sigma))).astype(
+            jnp.bfloat16
+        )
+        second_grad = (activated_grad * swish).astype(jnp.bfloat16)
+        lowered_ref[part] += contract(activated, down_weights, 1, 1)
+        routed_ref[part] += contract(first_grad, gate_weights, 1, 1) + contract(
+            second_grad, up_weights, 1, 1
+        )
+        first_ref[part] = first_grad
+        second_ref[part] = second_grad
+        active_ref[part] = activated
+        return 0
+
+    lax.fori_loop(0, rows_ref.shape[0] // ROWS, some, 0)
 
 
 def gated(rows, grads, weights, tile):
@@ -726,24 +734,70 @@
     moving = pl.BlockSpec(
         (1, 3, model_width, tile), lambda step: (step // tiles, 0, 0, step % tiles)
     )
-    return pl.pallas_call(
+    column = pl.BlockSpec((count, tile), lambda step: (0, step))
+    field = jax.ShapeDtypeStruct((count, model_width), jnp.float32)
+    wide = jax.ShapeDtypeStruct((count, chunks * hidden), jnp.bfloat16)
+    results = pl.pallas_call(
         gated_kernel,
         grid=(chunks * tiles,),
-        out_shape=(
-            jax.ShapeDtypeStruct((count, model_width), jnp.float32),
-            jax.ShapeDtypeStruct((count, model_width), jnp.float32),
-            jax.ShapeDtypeStruct(weights.shape, jnp.bfloat16),
-        ),
+        out_shape=(field, field, wide, wide, wide),
         in_specs=[fixed, fixed, moving],
-        out_specs=(fixed, fixed, moving),
+        out_specs=(fixed, fixed, column, column, column),
         compiler_params=pltpu.CompilerParams(vmem_limit_bytes=VMEM_BYTES),
         cost_estimate=pl.CostEstimate(
-            flops=18 * count * model_width * chunks * hidden,
+            flops=12 * count * model_width * chunks * hidden,
             transcendentals=count * chunks * hidden,
-            bytes_accessed=12 * count * model_width + 12 * chunks * model_width * hidden,
+            bytes_accessed=12 * count * model_width + 6 * (count + model_width) * chunks * hidden,
         ),
         name="gated",
     )(rows, grads, weights)
+    return (results[0], results[1], results[2:])
+
+
+def parts_kernel(
+    rows_ref, grads_ref, first_ref, second_ref, active_ref, parts_ref, turned_rows, turned_grads
+):
+    @pl.when(pl.program_id(0) == 0)
+    def _():
+        turned_rows[...] = rows_ref[...].T
+        turned_grads[...] = grads_ref[...].T
+
+    def some(index, _):
+        part = (pl.ds(pl.multiple_of(index * ROWS, ROWS), ROWS), slice(None))
+        rows = turned_rows[part]
+        parts_ref[(0, 0) + part] = contract(rows, first_ref[...], 1, 0).astype(jnp.bfloat16)
+        parts_ref[(0, 1) + part] = contract(rows, second_ref[...], 1, 0).astype(jnp.bfloat16)
+        parts_ref[(0, 2) + part] = contract(turned_grads[part], active_ref[...], 1, 0).astype(
+            jnp.bfloat16
+        )
+        return 0
+
+    lax.fori_loop(0, turned_rows.shape[0] // ROWS, some, 0)
+
+
+def weight_parts(rows, grads, wide, chunks, tile):
+    count, model_width = rows.shape
+    hidden = wide[0].shape[1] // chunks
+    tiles = hidden // tile
+    fixed = pl.BlockSpec((count, model_width), lambda step: (0, 0))
+    column = pl.BlockSpec((count, tile), lambda step: (0, step))
+    return pl.pallas_call(
+        parts_kernel,
+        grid=(chunks * tiles,),
+        out_shape=jax.ShapeDtypeStruct((chunks, 3, model_width, hidden), jnp.bfloat16),
+        in_specs=[fixed, fixed, column, column, column],
+        out_specs=pl.BlockSpec(
+            (1, 3, model_width, tile), lambda step: (step // tiles, 0, 0, step % tiles)
+        ),
+        scratch_shapes=[pltpu.VMEM((model_width, count), jnp.bfloat16)] * 2,
+        compiler_params=pltpu.CompilerParams(vmem_limit_bytes=VMEM_BYTES),
+        cost_estimate=pl.CostEstimate(
+            flops=6 * count * model_width * chunks * hidden,
+            transcendentals=0,
+            bytes_accessed=4 * count * model_width + 6 * (count + model_width) * chunks * hidden,
+        ),
+        name="weight_parts",
+    )(rows, grads, *wide)
 
 
 def swap(piece, axes, size, step):
@@ -754,13 +808,17 @@
     return lax.dynamic_index_in_dim(stacked, index, 0, keepdims=False)
 
 
-def share(piece, axes, size):
-    return [piece] + [swap(piece, axes, size, step) for step in range(1, size)]
-
-
-def natural(pieces, index):
-    stacked = jnp.stack(pieces)
-    return [pick(stacked, index ^ other) for other in range(len(pieces))]
+def share(piece, axes, size, dim):
+    step = size // 2
+    while step:
+        piece = jnp.concatenate([piece, swap(piece, axes, size, step)], dim)
+        step //= 2
+    return piece
+
+
+def reversed_bits(index, size):
+    bits = size.bit_length() - 1
+    return sum(((index >> bit) & 1) << (bits - 1 - bit) for bit in range(bits))
 
 
 def tied(*values):
@@ -769,6 +827,11 @@
 
 def route(blocks):
     return lax.all_to_all(blocks, GROUP, split_axis=0, concat_axis=0)
+
+
+def by_rows(field):
+    order = tuple(range(field.ndim))
+    return with_layout_constraint(field, Layout(major_to_minor=order))
 
 
 def turned(field, cosine, sine, backward):
@@ -858,7 +921,7 @@
     mixing_own = small[:, 3 * part_width : 4 * part_width].T
     router_all = small[:, 4 * part_width : 4 * part_width + EXPERTS]
     gains = small[:, 4 * part_width + EXPERTS : 4 * part_width + extra].T.astype(f32)
-    mixing_all = jnp.concatenate(share(mixing_own, TENSOR, shards), 0)
+    mixing_all = share(mixing_own, TENSOR, shards, 0)
     labels = jnp.arange(EXPERTS, dtype=jnp.int32)
     named = jnp.any(routes[:, None, :, :] == labels[None, :, None, None], 3)
     earlier = (
@@ -874,15 +937,19 @@
         .reshape(trees, EXPERTS * slots, rows)
     )
 
-    def send_rows(field):
+    def pick_rows(field):
         picked = jnp.einsum("bst,btd->bsd", chosen, field, preferred_element_type=f32).astype(bf16)
-        picked = picked.reshape(trees, EXPERTS, slots, field.shape[-1]).swapaxes(0, 1)
-        return route(picked).reshape(EXPERTS * trees * slots, field.shape[-1])
-
-    def return_rows(field):
+        return picked.reshape(trees, EXPERTS, slots, field.shape[-1]).swapaxes(0, 1)
+
+    def send_rows(picked):
+        return route(picked).reshape(EXPERTS * trees * slots, picked.shape[-1])
+
+    def bring_rows(field):
         back = route(field.reshape(EXPERTS, trees, slots, field.shape[-1])).swapaxes(0, 1)
-        back = back.reshape(trees, EXPERTS * slots, field.shape[-1])
-        return jnp.einsum("bst,bsd->btd", chosen, back, preferred_element_type=f32)
+        return back.reshape(trees, EXPERTS * slots, field.shape[-1])
+
+    def combine_rows(chosen, back):
+        return by_rows(jnp.einsum("bst,bsd->btd", chosen, back, preferred_element_type=f32))
 
     place, paths, key_bits = tree_tables(segments, parents)
     offset = seq_index * rows
@@ -907,13 +974,20 @@
         ],
         1,
     )
-    pairs = [pairs_own]
-    for _ in range(1, seq_size):
-        pairs.append(lax.ppermute(pairs[-1], SEQ, [(i, i + 1) for i in range(seq_size - 1)]))
     key_column = key_bits[:, :, None]
     path_row = own_paths[:, None, :]
+    pairs = [pairs_own]
+    links = [pairs_own[tree : tree + 1] for tree in range(trees)]
+    shared_bundle = jnp.concatenate([spreader, collector.T[None]], 0)
     state = ()
     for number in range(seq_size):
+        if number + 1 < seq_size:
+            links = [
+                lax.ppermute(link, SEQ, [(i, i + 1) for i in range(seq_size - 1)])
+                for link in links
+            ]
+        else:
+            picked_cotangent, pairs[-1] = tied(pick_rows(cotangent), pairs[-1])
         state = attend(
             number,
             number == seq_size - 1,
@@ -924,39 +998,38 @@
             pairs[number],
             state,
         )
+        if number + 1 < seq_size:
+            *links, first_state = tied(*links, state[0])
+            state = (first_state,) + tuple(state[1:])
+            pairs.append(jnp.concatenate(links, 0))
     outs, logs = state[:2]
 
     bundles = jnp.concatenate([expander, reducer.transpose(0, 2, 1)[:, None]], 1)
     own_expert = route(bundles).swapaxes(0, 1).reshape(3, model_width, hidden)
     expert_weights = lax.all_gather(own_expert, TENSOR, axis=0, tiled=False)
-    shared_bundle = jnp.concatenate([spreader, collector.T[None]], 0)
-    shared_bundle, expert_weights = tied(shared_bundle, expert_weights)
+    outs, expert_weights = tied(outs, expert_weights)
+    heads = share(outs, TENSOR, shards, 1)
+    upstream_rows = send_rows(picked_cotangent)
+    heads, upstream_rows = tied(heads, upstream_rows)
+    second = inputs + by_rows(
+        jnp.einsum("bht,hd->btd", heads, mixing_all, preferred_element_type=f32)
+    )
+
+    scale_two = lax.rsqrt(jnp.mean(second * second, -1, keepdims=True) + epsilon)
+    hidden_in = (second * scale_two * gains[1]).astype(bf16)
+    flat = (trees * rows, model_width)
+    flat_hidden = hidden_in.reshape(flat)
+    flat_cotangent = cotangent.reshape(flat)
+    expert_rows = send_rows(pick_rows(hidden_in))
+    expert_rows, shared_bundle = tied(expert_rows, shared_bundle)
     shared_weights = lax.all_gather(
         shared_bundle, GROUP, axis=1, tiled=True
     )
-    heads = jnp.concatenate(
-        [outs] + [swap(outs, TENSOR, shards, step) for step in range(1, shards)], 1
-    )
-    upstream_rows = send_rows(cotangent)
-    heads, upstream_rows = tied(heads, upstream_rows)
-    second = inputs + jnp.einsum("bht,hd->btd", heads, mixing_all, preferred_element_type=f32)
-
-    scale_two = lax.rsqrt(jnp.mean(second * second, -1, keepdims=True) + epsilon)
-    hidden_in = (second * scale_two * gains[1]).astype(bf16)
-    expert_rows, shared_weights = tied(send_rows(hidden_in), shared_weights)
     row_chances = jax.nn.softmax(jnp.dot(expert_rows, router_all, preferred_element_type=f32), -1)
     own_label = jnp.arange(EXPERTS, dtype=jnp.int32) == member_index
     row_gates = jnp.sum(jnp.where(own_label[None], row_chances, 0.0), -1, keepdims=True)
     row_grads = (row_gates * upstream_rows.astype(f32)).astype(bf16)
-    lowered, routed_back, expert_parts = gated(expert_rows, row_grads, expert_weights, 256)
-    flat = (trees * rows, model_width)
-    shared_out, shared_back, shared_parts = gated(
-        hidden_in.reshape(flat),
-        cotangent.reshape(flat),
-        shared_weights[None],
-        256,
-    )
-    expert_own = lax.psum_scatter(expert_parts, TENSOR, scatter_dimension=0, tiled=False)
+    lowered, routed_back, expert_wide = gated(expert_rows, row_grads, expert_weights, TILE)
     gate_grads = jnp.sum(upstream_rows.astype(f32) * lowered, -1, keepdims=True)
     lanes = jnp.arange(128, dtype=jnp.int32)[None]
     back_rows = jnp.concatenate(
@@ -966,26 +1039,45 @@
         ],
         1,
     )
-    returned_back = return_rows(back_rows)
+    flat_hidden, row_grads, back_rows = tied(flat_hidden, row_grads, back_rows)
+    shared_out, shared_back, shared_wide = gated(
+        flat_hidden, flat_cotangent, shared_weights[None], TILE
+    )
+    expert_parts = weight_parts(expert_rows, row_grads, expert_wide, shards, TILE)
+    back_rows = bring_rows(back_rows)
+    chosen, shared_back, expert_parts = tied(chosen, shared_back, expert_parts)
+    expert_own = lax.psum_scatter(expert_parts, TENSOR, scatter_dimension=0, tiled=False)
+    returned_back = combine_rows(chosen, back_rows)
+    out_rows = (row_gates * lowered).astype(bf16)
+    returned_back, out_rows = tied(returned_back, out_rows)
+    shared_parts = weight_parts(flat_hidden, flat_cotangent, shared_wide, 1, TILE)
+
     def own_rows(field):
         return lax.dynamic_slice_in_dim(field, shard * quarter, quarter, 1)
 
     def add_shards(field):
-        pieces = field.astype(bf16)
-        mine = own_rows(pieces).astype(f32)
-        for step in range(1, shards):
-            sent = lax.dynamic_slice_in_dim(pieces, (shard ^ step) * quarter, quarter, 1)
-            mine = mine + swap(sent, TENSOR, shards, step).astype(f32)
-        return mine
+        held = field.astype(bf16).reshape(trees, shards, quarter, field.shape[-1])
+        step = 1
+        while step < shards:
+            paired = held.reshape(trees, -1, 2, quarter, field.shape[-1])
+            bit = (shard // step) % 2
+            kept = lax.dynamic_index_in_dim(paired, bit, 2, keepdims=False)
+            sent = lax.dynamic_index_in_dim(paired, 1 - bit, 2, keepdims=False)
+            added = kept.astype(f32) + swap(sent, TENSOR, shards, step).astype(f32)
+            step *= 2
+            held = added.astype(bf16) if step < shards else added
+        return held[:, 0]
 
     def spread_shards(field):
-        return jnp.concatenate(natural(share(field, TENSOR, shards), shard), 1)
+        pieces = share(field[None], TENSOR, shards, 0)
+        return jnp.concatenate(
+            [pick(pieces, reversed_bits(shard ^ other, shards)) for other in range(shards)], 1
+        )
 
     summed = add_shards(
         returned_back
         + jnp.pad(shared_back.reshape(trees, rows, model_width), ((0, 0), (0, 0), (0, 128)))
     )
-    summed, expert_own = tied(summed, expert_own)
     chance_grad = summed[..., model_width : model_width + EXPERTS]
     quarter_second = own_rows(second)
     quarter_scale = own_rows(scale_two)
@@ -1006,17 +1098,9 @@
         scaled_two - quarter_normed * jnp.mean(scaled_two * quarter_normed, -1, keepdims=True)
     )
     branch_grad = spread_shards(second_grad.astype(bf16))
-    returned_out = return_rows((row_gates * lowered).astype(bf16))
-    branch_grad, returned_out = tied(branch_grad, returned_out)
+    returned_out = combine_rows(chosen, bring_rows(out_rows))
     partial_out = (returned_out + shared_out.reshape(trees, rows, model_width)).astype(bf16)
-    branches = lax.psum(partial_out, TENSOR).astype(f32)
-    branches, shared_parts = tied(branches, shared_parts)
-    shared_grads = lax.psum_scatter(
-        shared_parts[0], GROUP, scatter_dimension=1, tiled=True
-    ).astype(f32)
-    spreader_grad = shared_grads[:2]
-    collector_grad = shared_grads[2].T
-    output = (second + branches).astype(bf16)
+    branch_grad, partial_out = tied(branch_grad, partial_out)
 
     heads_grad = jnp.einsum(
         "hd,btd->bht", mixing_own, branch_grad, preferred_element_type=f32
@@ -1034,16 +1118,24 @@
         )
         pair_grads.append(pair_grad)
     blocks = expert_own.reshape(3, group_size, owned, hidden).swapaxes(0, 1)
-    expert_home = route(blocks)
-    pair_grad, expert_home = tied(pair_grads[0], expert_home)
-    expert_grads = expert_home.astype(f32)
-    for addend in pair_grads[1:]:
-        moved = lax.ppermute(
-            pair_grad.astype(bf16), SEQ, [(i + 1, i) for i in range(seq_size - 1)]
-        )
-        pair_grad = addend + moved.astype(f32)
-    expander_grad = expert_grads[:, :2]
-    reducer_grad = expert_grads[:, 2].transpose(0, 2, 1)
+    first_home = route(blocks[:, :, : owned // 2])
+    pair_grad, first_home, shared_parts = tied(pair_grads[0], first_home, shared_parts)
+    branches = lax.psum(partial_out, TENSOR)
+    shared_grads = lax.psum_scatter(
+        shared_parts[0], GROUP, scatter_dimension=1, tiled=True
+    ).astype(f32)
+    own_grads = []
+    for tree in range(trees):
+        moving = pair_grad[tree]
+        for step, addend in enumerate(pair_grads[1:]):
+            moved = lax.ppermute(
+                moving.astype(bf16), SEQ, [(i + 1, i) for i in range(seq_size - 1)]
+            )
+            if tree == trees - 1 and step == seq_size - 2:
+                moved, branches = tied(moved, branches)
+            moving = addend[tree] + moved.astype(f32)
+        own_grads.append(moving)
+    pair_grad, blocks = tied(jnp.stack(own_grads), blocks)
     query_grad = query_grad * HEAD_DIM ** (-0.5)
     mapped_grad = jnp.concatenate(
         [
@@ -1053,9 +1145,14 @@
         ],
         1,
     ).astype(bf16)
-    project_part = jnp.einsum("btd,bht->dh", first_in, mapped_grad, preferred_element_type=f32)
-    first_grad = add_shards(
+    first_part = by_rows(
         jnp.einsum("bht,dh->btd", mapped_grad, project_all, preferred_element_type=f32)
+    ).astype(bf16)
+    first_part, mapped_grad = tied(first_part, mapped_grad)
+    first_grad = add_shards(first_part)
+    output = (second + branches.astype(f32)).astype(bf16)
+    project_part = by_rows(
+        jnp.einsum("btd,bht->dh", first_in, mapped_grad, preferred_element_type=f32)
     )
     quarter_scale_one = own_rows(scale_one)
     quarter_normed_one = own_rows(inputs) * quarter_scale_one
@@ -1071,6 +1168,10 @@
         ).astype(bf16)
     )
 
+    input_grad, shared_grads = tied(input_grad, shared_grads)
+    spreader_grad = shared_grads[:2]
+    collector_grad = shared_grads[2].T
+
     small_parts = jnp.concatenate(
         [
             project_part,
@@ -1081,8 +1182,13 @@
         ],
         1,
     ).astype(bf16)
+    second_home, small_parts = tied(route(blocks[:, :, owned // 2 :]), small_parts)
+    expert_grads = jnp.concatenate([first_home, second_home], 2).astype(f32)
+    expander_grad = expert_grads[:, :2]
+    reducer_grad = expert_grads[:, 2].transpose(0, 2, 1)
+    small_home = route(small_parts.reshape(group_size, owned, -1))
     small_grads = jnp.sum(
-        route(small_parts.reshape(group_size, owned, -1)).astype(f32),
+        small_home.astype(f32),
         0,
     )
     project_grad = (

time: 650 us -> 629 us (0.968)
  blocking collectives: 44.6 us -> 6.85 us
  Pallas kernels: 84.6 us -> 96.8 us
  waiting for transfers between devices: 265 us -> 274 us
  local copies, waits for them, and re-layouts: 66.7 us -> 57.9 us
    all_to_all x6 -> x8, waiting for transfers between devices: 105 us -> 154 us  [route(): return lax.all_to_all(blocks, GROUP, split_axis=0, concat_axis=0)]
    all_to_all x1 -> x0, blocking collectives: 37.1 us -> none  [route(): return lax.all_to_all(blocks, GROUP, split_axis=0, concat_axis=0)]
    ppermute x18 -> x12, waiting for transfers between devices: 72.5 us -> 42.1 us  [swap(): return lax.ppermute(piece, axes, [(i, i ^ step) for i in range(size)])]
    ppermute x6 -> x12, waiting for transfers between devices: 64.2 us -> 45.2 us  [the longest x6 26.5 us: local_fast(): lax.ppermute(moving.astype(bf16), SEQ, [(i + 1, i) for i in range(seq_siz...]
    pallas_call x2 -> x4, Pallas kernels: 51.1 us -> 63.1 us  [the longest x2 38.5 us: gated(): pl.pallas_call(gated_kernel, grid=(chunks * tiles,), out_shape=(field, fi...]
    reshape x5 -> x2, local copies, waits for them, and re-layouts: 11.4 us -> 2.19 us  [pick_rows(): return picked.reshape(trees, EXPERTS, slots, field.shape[-1]).swapaxes(0, 1)]
    all_to_all x6 -> x8, starting transfers between devices: 36.5 us -> 43.9 us  [route(): return lax.all_to_all(blocks, GROUP, split_axis=0, concat_axis=0)]
    ppermute x18 -> x12, starting transfers between devices: 12 us -> 5.23 us  [swap(): return lax.ppermute(piece, axes, [(i, i ^ step) for i in range(size)])]
  transfers between devices with their start and end apart: 36 -> 38, of which waited for: 21 -> 23; matrix products, arithmetic and copies ran while one was open for 21% -> 19% of each run, Pallas kernels for 7% -> 14%
where the time goes in v3:
time: 629 us; the launch traced here: 619 us
  waiting for transfers between devices  274 us (44%)
  Pallas kernels  96.8 us (15%)
  starting transfers between devices  76.2 us (12%)
  other arithmetic  62.9 us (10%)
  local copies, waits for them, and re-layouts  57.9 us (9%)
  matrix products  29.3 us (5%)
  between operations  15.7 us (2%)
  blocking collectives  6.85 us (1%)
    all_to_all x8, waiting for transfers between devices, route(): return lax.all_to_all(blocks, GROUP, split_axis=0, concat_axis=0)  154 us
    all_to_all x8, starting transfers between devices, route(): return lax.all_to_all(blocks, GROUP, split_axis=0, concat_axis=0)  43.9 us
    ppermute x12, waiting for transfers between devices, swap(): return lax.ppermute(piece, axes, [(i, i ^ step) for i in range(size)])  42.1 us
    pallas_call x2, Pallas kernels, gated(): pl.pallas_call(gated_kernel, grid=(chunks * tiles,), out_shape=(field, fi...  38.5 us
    pallas_call x8, Pallas kernels, attend_call(): pl.pallas_call(kernel, grid=(trees,), out_shape=results, in_specs=[pl.Blo...  33.8 us
    ppermute x6, waiting for transfers between devices, local_fast(): lax.ppermute(moving.astype(bf16), SEQ, [(i + 1, i) for i in range(seq_siz...  26.5 us
    pallas_call x2, Pallas kernels, weight_parts(): pl.pallas_call(parts_kernel, grid=(chunks * tiles,), out_shape=jax.ShapeD...  24.5 us
    unnamed x120, local copies, waits for them, and re-layouts  19.1 us
  transfers between devices with their start and end apart: 38, of which 23 were waited for; matrix products, arithmetic and copies ran while one was open for 19% of the time, Pallas kernels for 14%

profile of v3, /device:TPU:0, one launch (start us, length us, event | category | flops | bytes accessed | tf_op | source)
XLA Modules:
  0.0 619.2 jit_solution(11143954292048987250)
XLA Ops:
  10.5 7.4 %all-to-all-start = ((bf16[8,3,96,512]{3,2,1,0:T(8,128)(2,1)}), bf16[8,3,96,512]{3,2,1,0:T(8,128)(2,1)S(1)}, u32[]{:S(2)}, u32[]{:S(2)}) async-start(bf16[8,3,96,512]{3,2,1,0:T(8,128)(2,1)} %pad_maximum_fusion), calls=%async_computation | async-start | bytes 4718592 | tf_op jit(solution)/shard_map/all_to_all | solution.py:829
  19.2 64.0 %all-to-all-done = bf16[8,3,96,512]{3,2,1,0:T(8,128)(2,1)S(1)} async-done(((bf16[8,3,96,512]{3,2,1,0:T(8,128)(2,1)}), bf16[8,3,96,512]{3,2,1,0:T(8,128)(2,1)S(1)}, u32[]{:S(2)}, u32[]{:S(2)}) %all-to-all-start) | async-done | bytes 2359328 | tf_op jit(solution)/shard_map/all_to_all | solution.py:829
  104.5 6.2 %attend.4 = (f32[2,3,512]{2,1,0:T(4,128)}, f32[2,3,512]{2,1,0:T(4,128)}, f32[2,192,512]{2,1,0:T(8,128)}) custom-call(s32[1]{0:T(128)} %bitcast.place_ref, bf16[2,192,512]{2,1,0:T(8,128)(2,1)} %bitcast.268, s32[2,2048,1]{2,1,0:T(8,128)} %copy.261.key_bits_ref, s32[2,1,512]{2,1,0:T(1,128)} %broadcast_in_dim.173.query_bits_ref, ...), custom_call_target="tpu_custom_call" | custom-call | flops 1610612736 | bytes 3145728 | tf_op jit(solution)/shard_map/attend/pallas_call | solution.py:642
  154.4 8.1 %all-to-all-start.1 = ((bf16[8,2,48,768]{3,2,1,0:T(8,128)(2,1)}), bf16[8,2,48,768]{3,2,1,0:T(8,128)(2,1)S(1)}, u32[]{:S(2)}, u32[]{:S(2)}) async-start(bf16[8,2,48,768]{3,2,1,0:T(8,128)(2,1)} %bitcast.225), calls=%async_computation.1 | async-start | bytes 2359296 | tf_op jit(solution)/shard_map/all_to_all | solution.py:829
  169.2 8.3 %collective-permute-done.6 = bf16[2,192,512]{2,1,0:T(8,128)(2,1)S(1)} collective-permute-done((bf16[2,192,512]{2,1,0:T(8,128)(2,1)}, bf16[2,192,512]{2,1,0:T(8,128)(2,1)S(1)}, u32[]{:S(2)}, u32[]{:S(2)}) %collective-permute-start.6) | collective-permute-done | bytes 393248 | tf_op jit(solution)/shard_map/ppermute | solution.py:804
  182.8 6.9 %all-to-all-done.1 = bf16[8,2,48,768]{3,2,1,0:T(8,128)(2,1)S(1)} async-done(((bf16[8,2,48,768]{3,2,1,0:T(8,128)(2,1)}), bf16[8,2,48,768]{3,2,1,0:T(8,128)(2,1)S(1)}, u32[]{:S(2)}, u32[]{:S(2)}) %all-to-all-start.1) | async-done | bytes 1179680 | tf_op jit(solution)/shard_map/all_to_all | solution.py:829
  203.1 28.0 %all-to-all-done.2 = bf16[8,2,48,768]{3,2,1,0:T(8,128)(2,1)} async-done(((bf16[8,2,48,768]{3,2,1,0:T(8,128)(2,1)}), bf16[8,2,48,768]{3,2,1,0:T(8,128)(2,1)}, u32[]{:S(2)}, u32[]{:S(2)}) %all-to-all-start.2) | async-done | bytes 1179680 | tf_op jit(solution)/shard_map/all_to_all | solution.py:829
  234.5 25.8 %gated.2 = (f32[768,768]{1,0:T(8,128)}, f32[768,768]{1,0:T(8,128)}, bf16[768,2048]{1,0:T(8,128)(2,1)}, bf16[768,2048]{1,0:T(8,128)(2,1)}, bf16[768,2048]{1,0:T(8,128)(2,1)}) custom-call(bf16[768,768]{1,0:T(8,128)(2,1)} %bitcast.30.rows_ref, bf16[768,768]{1,0:T(8,128)(2,1)} %fusion.1.grads_ref, bf16[4,3,768,512]{3,2,1,0:T(8,128)(2,1)} %all-gather.6.cloned.1.call-done.weights_ref), custom_call_target="tpu_custom_call" | custom-call | flops 14495514624 | bytes 25952256 | tf_op jit(solution)/shard_map/gated/pallas_call | solution.py:740
  265.4 16.3 %weight_parts.2 = bf16[4,3,768,512]{3,2,1,0:T(8,128)(2,1)} custom-call(bf16[768,768]{1,0:T(8,128)(2,1)} %bitcast.30.rows_ref, bf16[768,768]{1,0:T(8,128)(2,1)} %fusion.1.grads_ref, bf16[768,2048]{1,0:T(8,128)(2,1)} %get-tuple-element.111.first_ref, bf16[768,2048]{1,0:T(8,128)(2,1)} %get-tuple-element.112.second_ref, ...), custom_call_target="tpu_custom_call" | custom-call | flops 7247757312 | bytes 21233664 | tf_op jit(solution)/shard_map/weight_parts/pallas_call | solution.py:784
  281.8 12.8 %gated.3 = (f32[1024,768]{1,0:T(8,128)}, f32[1024,768]{1,0:T(8,128)}, bf16[1024,512]{1,0:T(8,128)(2,1)}, bf16[1024,512]{1,0:T(8,128)(2,1)}, bf16[1024,512]{1,0:T(8,128)(2,1)}) custom-call(bf16[1024,768]{1,0:T(8,128)(2,1)} %bitcast.243, bf16[1024,768]{1,0:T(8,128)(2,1)} %bitcast.266, bf16[1,3,768,512]{3,2,1,0:T(8,128)(2,1)} %bitcast.279), custom_call_target="tpu_custom_call" | custom-call | flops 4831838208 | bytes 14942208 | tf_op jit(solution)/shard_map/gated/pallas_call | solution.py:740
  298.9 31.7 %all-to-all-done.3 = bf16[8,2,48,896]{3,2,1,0:T(8,128)(2,1)} async-done(((bf16[8,2,48,896]{3,2,1,0:T(8,128)(2,1)}), bf16[8,2,48,896]{3,2,1,0:T(8,128)(2,1)}, u32[]{:S(2)}, u32[]{:S(2)}) %all-to-all-start.3) | async-done | bytes 1376288 | tf_op jit(solution)/shard_map/all_to_all | solution.py:829
  346.7 21.4 %collective-permute-done.11 = bf16[2,1,128,896]{3,2,0,1:T(8,128)(2,1)} collective-permute-done((bf16[2,1,128,896]{3,2,0,1:T(8,128)(2,1)}, bf16[2,1,128,896]{3,2,0,1:T(8,128)(2,1)}, u32[]{:S(2)}, u32[]{:S(2)}) %collective-permute-start.11) | collective-permute-done | bytes 458784 | tf_op jit(solution)/shard_map/ppermute | solution.py:804
  374.6 6.3 %reduce-scatter.3.cloned.1.call-done = bf16[1,3,768,512]{3,2,1,0:T(8,128)(2,1)} async-done(((bf16[4,3,768,512]{3,2,1,0:T(8,128)(2,1)}), bf16[1,3,768,512]{3,2,1,0:T(8,128)(2,1)}) %reduce-scatter.3.cloned.1.call-update) | async-done | bytes 2359312 | tf_op jit(solution)/shard_map/reduce_scatter | solution.py:1049
  392.7 8.2 %weight_parts.3 = bf16[1,3,768,512]{3,2,1,0:T(8,128)(2,1)} custom-call(bf16[1024,768]{1,0:T(8,128)(2,1)} %bitcast.244, bf16[1024,768]{1,0:T(8,128)(2,1)} %bitcast.267, bf16[1024,512]{1,0:T(8,128)(2,1)} %get-tuple-element.128.first_ref, bf16[1024,512]{1,0:T(8,128)(2,1)} %get-tuple-element.129.second_ref, bf16[1024,512]{1,0:T(8,128)(2,1)} %get-tuple-element.130.active_ref), custom_call_target="tpu_custom_call" | custom-call | flops 2415919104 | bytes 8650752 | tf_op jit(solution)/shard_map/weight_parts/pallas_call | solution.py:784
  413.2 6.5 %all-to-all-done.5 = bf16[8,3,48,512]{3,2,1,0:T(8,128)(2,1)} async-done(((bf16[8,3,48,512]{3,2,1,0:T(8,128)(2,1)}), bf16[8,3,48,512]{3,2,1,0:T(8,128)(2,1)}, u32[]{:S(2)}, u32[]{:S(2)}) %all-to-all-start.5) | async-done | bytes 1179680 | tf_op jit(solution)/shard_map/all_to_all | solution.py:829
  427.1 7.7 %collective-permute-done.14 = bf16[384,512]{1,0:T(8,128)(2,1)S(1)} collective-permute-done((bf16[384,512]{1,0:T(8,128)(2,1)S(1)}, bf16[384,512]{1,0:T(8,128)(2,1)S(1)}, u32[]{:S(2)}, u32[]{:S(2)}) %collective-permute-start.14) | collective-permute-done | bytes 393248 | tf_op jit(solution)/shard_map/ppermute | solution.py:1131
  448.8 8.0 %collective-permute-done.15 = bf16[384,512]{1,0:T(8,128)(2,1)} collective-permute-done((bf16[384,512]{1,0:T(8,128)(2,1)}, bf16[384,512]{1,0:T(8,128)(2,1)}, u32[]{:S(2)}, u32[]{:S(2)}) %collective-permute-start.15) | collective-permute-done | bytes 393248 | tf_op jit(solution)/shard_map/ppermute | solution.py:1131
  456.8 5.5 collective-permute-done.18
  467.8 8.1 %attend_back.7 = (f32[2,192,512]{2,1,0:T(8,128)}, f32[2,384,512]{2,1,0:T(8,128)}) custom-call(s32[1]{0:T(128)} %bitcast.place_ref, bf16[2,192,512]{2,1,0:T(8,128)(2,1)} %bitcast.275, bf16[2,192,512]{2,1,0:T(8,128)(2,1)} %get-tuple-element.99.out_ref, bf16[2,192,512]{2,1,0:T(8,128)(2,1)} %fusion.7.grad_ref, f32[2,3,512]{2,1,0:T(4,128)} %get-tuple-element.121.log_ref, ...), custom_call_target="tpu_custom_call" | custom-call | flops 4026531840 | bytes 3145728 | tf_op jit(solution)/shard_map/attend_back/pallas_call | solution.py:642
  478.0 13.3 %all-reduce.3.cloned.1.call-done = bf16[2,512,768]{2,1,0:T(8,128)(2,1)} async-done(((bf16[2,512,768]{2,1,0:T(8,128)(2,1)}), bf16[2,512,768]{2,1,0:T(8,128)(2,1)}) %all-reduce.3.cloned.1.call-update) | async-done | bytes 1572880 | tf_op jit(solution)/shard_map/psum | solution.py:1123
  534.5 16.4 %all-to-all-done.6 = bf16[8,3,48,512]{3,2,1,0:T(8,128)(2,1)} async-done(((bf16[8,3,48,512]{3,2,1,0:T(8,128)(2,1)}), bf16[8,3,48,512]{3,2,1,0:T(8,128)(2,1)}, u32[]{:S(2)}, u32[]{:S(2)}) %all-to-all-start.6) | async-done | bytes 1179680 | tf_op jit(solution)/shard_map/all_to_all | solution.py:829
  559.3 9.5 %collective-permute-done.22 = bf16[1,2,128,768]{3,2,1,0:T(8,128)(2,1)S(1)} collective-permute-done((bf16[1,2,128,768]{3,2,1,0:T(8,128)(2,1)S(1)}, bf16[1,2,128,768]{3,2,1,0:T(8,128)(2,1)S(1)}, u32[]{:S(2)}, u32[]{:S(2)}) %collective-permute-start.22) | collective-permute-done | bytes 393248 | tf_op jit(solution)/shard_map/ppermute | solution.py:804
  584.7 13.0 %reduce-scatter.5.cloned.1.call-done = bf16[3,96,512]{2,1,0:T(8,128)(2,1)} async-done(((bf16[3,768,512]{2,1,0:T(8,128)(2,1)}), bf16[3,96,512]{2,1,0:T(8,128)(2,1)}) %reduce-scatter.5.cloned.1.call-update) | async-done | bytes 294928 | tf_op jit(solution)/shard_map/reduce_scatter | solution.py:1124
  603.1 6.9 %psum.15 = f32[10,96]{1,0:T(8,128)S(1)} all-reduce(f32[10,96]{1,0:T(8,128)S(1)} %pad_maximum_fusion.19), channel_id=1, replica_groups=mesh['dp'=2,'seq'=4,'tensor'=4] {'tensor'}, use_global_device_ids=true, to_apply=%region_25.26 | all-reduce | flops 960 | bytes 7680 | tf_op jit(solution)/shard_map/psum | solution.py:1200
  (333 shorter events, 257.3 us)
Async XLA Ops:
  10.5 72.7 %all-to-all-start = ((bf16[8,3,96,512]{3,2,1,0:T(8,128)(2,1)}), bf16[8,3,96,512]{3,2,1,0:T(8,128)(2,1)S(1)}, u32[]{:S(2)}, u32[]{:S(2)}) async-start(bf16[8,3,96,512]{3,2,1,0:T(8,128)(2,1)} %pad_maximum_fusion), calls=%async_computation | async-start | bytes 4718592 | tf_op jit(solution)/shard_map/all_to_all | solution.py:829
  17.9 77.6 %all-gather.4.cloned.1.call-start = ((), (), s32[]{:S(2)}) async-start(), calls=%async_computation.10 | async-start | bytes 1548288 | tf_op jit(solution)/shard_map/all_gather | solution.py:919
  19.1 146.5 %all-gather.6.cloned.1.call-start = ((), (), s32[]{:S(2)}) async-start(), calls=%async_computation.11 | async-start | bytes 11796480 | tf_op jit(solution)/shard_map/all_gather | solution.py:1009
  101.4 14.7 %collective-permute-start.1 = (bf16[1,384,512]{2,1,0:T(8,128)(2,1)S(1)}, bf16[1,384,512]{2,1,0:T(8,128)(2,1)S(1)}, u32[]{:S(2)}, u32[]{:S(2)}) collective-permute-start(bf16[1,384,512]{2,1,0:T(8,128)(2,1)S(1)} %get-tuple-element.259), channel_id=1, source_target_pairs={{0,4},{4,8},{8,12},{1,5},{5,9},{9,13},{2,6},{6,10},{10,14},{3,7},{... | collective-permute-start | bytes 1179656 | tf_op jit(solution)/shard_map/ppermute | solution.py:986
  134.4 14.0 %collective-permute-start.4 = (bf16[1,384,512]{2,1,0:T(8,128)(2,1)S(1)}, bf16[1,384,512]{2,1,0:T(8,128)(2,1)S(1)}, u32[]{:S(2)}, u32[]{:S(2)}) collective-permute-start(bf16[1,384,512]{2,1,0:T(8,128)(2,1)S(1)} %collective-permute-done.2), channel_id=1, source_target_pairs={{0,4},{4,8},{8,12},{1,5},{5,9},{9,13},{2,6},{6,10},{10,14},{3,7},{... | collective-permute-start | bytes 1179656 | tf_op jit(solution)/shard_map/ppermute | solution.py:986
  138.9 14.6 %collective-permute-start.5 = (bf16[1,384,512]{2,1,0:T(8,128)(2,1)S(1)}, bf16[1,384,512]{2,1,0:T(8,128)(2,1)S(1)}, u32[]{:S(2)}, u32[]{:S(2)}) collective-permute-start(bf16[1,384,512]{2,1,0:T(8,128)(2,1)S(1)} %collective-permute-done.3), channel_id=1, source_target_pairs={{0,4},{4,8},{8,12},{1,5},{5,9},{9,13},{2,6},{6,10},{10,14},{3,7},{... | collective-permute-start | bytes 1179656 | tf_op jit(solution)/shard_map/ppermute | solution.py:986
  154.4 35.3 %all-to-all-start.1 = ((bf16[8,2,48,768]{3,2,1,0:T(8,128)(2,1)}), bf16[8,2,48,768]{3,2,1,0:T(8,128)(2,1)S(1)}, u32[]{:S(2)}, u32[]{:S(2)}) async-start(bf16[8,2,48,768]{3,2,1,0:T(8,128)(2,1)} %bitcast.225), calls=%async_computation.1 | async-start | bytes 2359296 | tf_op jit(solution)/shard_map/all_to_all | solution.py:829
  197.9 33.3 %all-to-all-start.2 = ((bf16[8,2,48,768]{3,2,1,0:T(8,128)(2,1)}), bf16[8,2,48,768]{3,2,1,0:T(8,128)(2,1)}, u32[]{:S(2)}, u32[]{:S(2)}) async-start(bf16[8,2,48,768]{3,2,1,0:T(8,128)(2,1)} %bitcast.240), calls=%async_computation.2 | async-start | bytes 2359296 | tf_op jit(solution)/shard_map/all_to_all | solution.py:829
  202.3 79.5 %all-gather.8.cloned.1.call-start = ((), (), s32[]{:S(2)}) async-start(), calls=%async_computation.12 | async-start | bytes 2654208 | tf_op jit(solution)/shard_map/all_gather | solution.py:1025
  231.2 149.7 %reduce-scatter.3.cloned.1.call-start = ((), (), s32[]{:S(2)}) async-start(), calls=%async_computation.13 | async-start | bytes 11796480 | tf_op jit(solution)/shard_map/reduce_scatter | solution.py:1049
  294.6 36.0 %all-to-all-start.3 = ((bf16[8,2,48,896]{3,2,1,0:T(8,128)(2,1)}), bf16[8,2,48,896]{3,2,1,0:T(8,128)(2,1)}, u32[]{:S(2)}, u32[]{:S(2)}) async-start(bf16[8,2,48,896]{3,2,1,0:T(8,128)(2,1)} %bitcast.236), calls=%async_computation.3 | async-start | bytes 2752512 | tf_op jit(solution)/shard_map/all_to_all | solution.py:829
  336.8 48.5 %all-to-all-start.4 = ((bf16[8,2,48,768]{3,2,1,0:T(8,128)(2,1)}), bf16[8,2,48,768]{3,2,1,0:T(8,128)(2,1)}, u32[]{:S(2)}, u32[]{:S(2)}) async-start(bf16[8,2,48,768]{3,2,1,0:T(8,128)(2,1)} %bitcast.238), calls=%async_computation.4 | async-start | bytes 2359296 | tf_op jit(solution)/shard_map/all_to_all | solution.py:829
  344.7 23.3 %collective-permute-start.11 = (bf16[2,1,128,896]{3,2,0,1:T(8,128)(2,1)}, bf16[2,1,128,896]{3,2,0,1:T(8,128)(2,1)}, u32[]{:S(2)}, u32[]{:S(2)}) collective-permute-start(bf16[2,1,128,896]{3,2,0,1:T(8,128)(2,1)} %constant_dynamic-slice_fusion.4), channel_id=1, source_target_pairs={{0,2},{1,3},{2,0},{3,1},{4,6},{5,7},{6,4},{7,5},{8,10},{9,11},{10,... | collective-permute-start | bytes 1376264 | tf_op jit(solution)/shard_map/ppermute | solution.py:804
  374.1 16.6 %collective-permute-start.12 = (bf16[1,2,128,768]{3,2,1,0:T(8,128)(2,1)S(1)}, bf16[1,2,128,768]{3,2,1,0:T(8,128)(2,1)}, u32[]{:S(2)}, u32[]{:S(2)}) collective-permute-start(bf16[1,2,128,768]{3,2,1,0:T(8,128)(2,1)S(1)} %convert_bitcast_fusion.2), channel_id=1, source_target_pairs={{0,2},{1,3},{2,0},{3,1},{4,6},{5,7},{6,4},{7,5},{8,10},{9,11},{10,... | collective-permute-start | bytes 1179656 | tf_op jit(solution)/shard_map/ppermute | solution.py:804
  385.3 34.5 %all-to-all-start.5 = ((bf16[8,3,48,512]{3,2,1,0:T(8,128)(2,1)}), bf16[8,3,48,512]{3,2,1,0:T(8,128)(2,1)}, u32[]{:S(2)}, u32[]{:S(2)}) async-start(bf16[8,3,48,512]{3,2,1,0:T(8,128)(2,1)} %slice.211), calls=%async_computation.6 | async-start | bytes 2359296 | tf_op jit(solution)/shard_map/all_to_all | solution.py:829
  390.7 100.7 %all-reduce.3.cloned.1.call-start = ((), (), s32[]{:S(2)}) async-start(), calls=%async_computation.14 | async-start | bytes 3145728 | tf_op jit(solution)/shard_map/psum | solution.py:1123
  422.2 17.9 %collective-permute-start.17 = (bf16[384,512]{1,0:T(8,128)(2,1)S(1)}, bf16[384,512]{1,0:T(8,128)(2,1)S(1)}, u32[]{:S(2)}, u32[]{:S(2)}) collective-permute-start(bf16[384,512]{1,0:T(8,128)(2,1)S(1)} %get-tuple-element.257), channel_id=1, source_target_pairs={{4,0},{8,4},{12,8},{5,1},{9,5},{13,9},{6,2},{10,6},{14,10},{7,3},{... | collective-permute-start | bytes 1179656 | tf_op jit(solution)/shard_map/ppermute | solution.py:1131
  442.5 14.2 %collective-permute-start.15 = (bf16[384,512]{1,0:T(8,128)(2,1)}, bf16[384,512]{1,0:T(8,128)(2,1)}, u32[]{:S(2)}, u32[]{:S(2)}) collective-permute-start(bf16[384,512]{1,0:T(8,128)(2,1)} %get-tuple-element.244), channel_id=1, source_target_pairs={{4,0},{8,4},{12,8},{5,1},{9,5},{13,9},{6,2},{10,6},{14,10},{7,3},{... | collective-permute-start | bytes 1179656 | tf_op jit(solution)/shard_map/ppermute | solution.py:1131
  443.8 18.5 %collective-permute-start.18 = (bf16[384,512]{1,0:T(8,128)(2,1)S(1)}, bf16[384,512]{1,0:T(8,128)(2,1)}, u32[]{:S(2)}, u32[]{:S(2)}) collective-permute-start(bf16[384,512]{1,0:T(8,128)(2,1)S(1)} %get-tuple-element.243), channel_id=1, source_target_pairs={{4,0},{8,4},{12,8},{5,1},{9,5},{13,9},{6,2},{10,6},{14,10},{7,3},{... | collective-permute-start | bytes 1179656 | tf_op jit(solution)/shard_map/ppermute | solution.py:1131
  445.1 152.6 %reduce-scatter.5.cloned.1.call-start = ((), (), s32[]{:S(2)}) async-start(), calls=%async_computation.15 | async-start | bytes 2654208 | tf_op jit(solution)/shard_map/reduce_scatter | solution.py:1124
  464.9 26.4 %collective-permute-start.16 = (bf16[384,512]{1,0:T(8,128)(2,1)}, bf16[384,512]{1,0:T(8,128)(2,1)}, u32[]{:S(2)}, u32[]{:S(2)}) collective-permute-start(bf16[384,512]{1,0:T(8,128)(2,1)} %get-tuple-element.242), channel_id=1, source_target_pairs={{4,0},{8,4},{12,8},{5,1},{9,5},{13,9},{6,2},{10,6},{14,10},{7,3},{... | collective-permute-start | bytes 1179656 | tf_op jit(solution)/shard_map/ppermute | solution.py:1131
  466.2 25.1 %collective-permute-start.19 = (bf16[384,512]{1,0:T(8,128)(2,1)S(1)}, bf16[384,512]{1,0:T(8,128)(2,1)}, u32[]{:S(2)}, u32[]{:S(2)}) collective-permute-start(bf16[384,512]{1,0:T(8,128)(2,1)S(1)} %get-tuple-element.241), channel_id=1, source_target_pairs={{4,0},{8,4},{12,8},{5,1},{9,5},{13,9},{6,2},{10,6},{14,10},{7,3},{... | collective-permute-start | bytes 1179656 | tf_op jit(solution)/shard_map/ppermute | solution.py:1131
  500.3 50.5 %all-to-all-start.6 = ((bf16[8,3,48,512]{3,2,1,0:T(8,128)(2,1)}), bf16[8,3,48,512]{3,2,1,0:T(8,128)(2,1)}, u32[]{:S(2)}, u32[]{:S(2)}) async-start(bf16[8,3,48,512]{3,2,1,0:T(8,128)(2,1)} %slice.180), calls=%async_computation.8 | async-start | bytes 2359296 | tf_op jit(solution)/shard_map/all_to_all | solution.py:829
  550.8 49.4 %all-to-all-start.7 = ((bf16[8,96,896]{2,1,0:T(8,128)(2,1)}), bf16[8,96,896]{2,1,0:T(8,128)(2,1)}, u32[]{:S(2)}, u32[]{:S(2)}) async-start(bf16[8,96,896]{2,1,0:T(8,128)(2,1)} %bitcast.235), calls=%async_computation.9 | async-start | bytes 2752512 | tf_op jit(solution)/shard_map/all_to_all | solution.py:829
  (69 other events, 387.5 us)
Sparse Core Ops, SparseCore 0:
  21.4 69.9 all-gather.3
  93.5 63.3 all-gather.5
  231.3 48.3 all-gather.7
  294.7 86.1 reduce-scatter.2
  445.3 46.0 all-reduce.2
  494.7 102.9 reduce-scatter.4

commit v4 on v3

--- a/solution.py
+++ b/solution.py
@@ -757,37 +757,44 @@
 def parts_kernel(
     rows_ref, grads_ref, first_ref, second_ref, active_ref, parts_ref, turned_rows, turned_grads
 ):
+    owned = parts_ref.shape[3]
+
     @pl.when(pl.program_id(0) == 0)
     def _():
         turned_rows[...] = rows_ref[...].T
         turned_grads[...] = grads_ref[...].T
 
     def some(index, _):
-        part = (pl.ds(pl.multiple_of(index * ROWS, ROWS), ROWS), slice(None))
+        part = (pl.ds(pl.multiple_of(index * 2 * owned, 2 * owned), 2 * owned), slice(None))
         rows = turned_rows[part]
-        parts_ref[(0, 0) + part] = contract(rows, first_ref[...], 1, 0).astype(jnp.bfloat16)
-        parts_ref[(0, 1) + part] = contract(rows, second_ref[...], 1, 0).astype(jnp.bfloat16)
-        parts_ref[(0, 2) + part] = contract(turned_grads[part], active_ref[...], 1, 0).astype(
-            jnp.bfloat16
-        )
+        results = (
+            contract(rows, first_ref[...], 1, 0),
+            contract(rows, second_ref[...], 1, 0),
+            contract(turned_grads[part], active_ref[...], 1, 0),
+        )
+        for kind, result in enumerate(results):
+            for half in range(2):
+                piece = result[half * owned : (half + 1) * owned]
+                parts_ref[0, 2 * index + half, kind] = piece.astype(jnp.bfloat16)
         return 0
 
-    lax.fori_loop(0, turned_rows.shape[0] // ROWS, some, 0)
-
-
-def weight_parts(rows, grads, wide, chunks, tile):
+    lax.fori_loop(0, parts_ref.shape[1] // 2, some, 0)
+
+
+def weight_parts(rows, grads, wide, chunks, owners, tile):
     count, model_width = rows.shape
     hidden = wide[0].shape[1] // chunks
     tiles = hidden // tile
+    owned = model_width // owners
     fixed = pl.BlockSpec((count, model_width), lambda step: (0, 0))
     column = pl.BlockSpec((count, tile), lambda step: (0, step))
     return pl.pallas_call(
         parts_kernel,
         grid=(chunks * tiles,),
-        out_shape=jax.ShapeDtypeStruct((chunks, 3, model_width, hidden), jnp.bfloat16),
+        out_shape=jax.ShapeDtypeStruct((chunks, owners, 3, owned, hidden), jnp.bfloat16),
         in_specs=[fixed, fixed, column, column, column],
         out_specs=pl.BlockSpec(
-            (1, 3, model_width, tile), lambda step: (step // tiles, 0, 0, step % tiles)
+            (1, owners, 3, owned, tile), lambda step: (step // tiles, 0, 0, 0, step % tiles)
         ),
         scratch_shapes=[pltpu.VMEM((model_width, count), jnp.bfloat16)] * 2,
         compiler_params=pltpu.CompilerParams(vmem_limit_bytes=VMEM_BYTES),
@@ -1043,14 +1050,16 @@
     shared_out, shared_back, shared_wide = gated(
         flat_hidden, flat_cotangent, shared_weights[None], TILE
     )
-    expert_parts = weight_parts(expert_rows, row_grads, expert_wide, shards, TILE)
+    expert_parts = weight_parts(
+        expert_rows, row_grads, expert_wide, shards, group_size, TILE
+    )
     back_rows = bring_rows(back_rows)
-    chosen, shared_back, expert_parts = tied(chosen, shared_back, expert_parts)
-    expert_own = lax.psum_scatter(expert_parts, TENSOR, scatter_dimension=0, tiled=False)
+    chosen, shared_back = tied(chosen, shared_back)
     returned_back = combine_rows(chosen, back_rows)
     out_rows = (row_gates * lowered).astype(bf16)
-    returned_back, out_rows = tied(returned_back, out_rows)
-    shared_parts = weight_parts(flat_hidden, flat_cotangent, shared_wide, 1, TILE)
+    shared_parts = weight_parts(
+        flat_hidden, flat_cotangent, shared_wide, 1, group_size, TILE
+    )
 
     def own_rows(field):
         return lax.dynamic_slice_in_dim(field, shard * quarter, quarter, 1)
@@ -1078,6 +1087,7 @@
         returned_back
         + jnp.pad(shared_back.reshape(trees, rows, model_width), ((0, 0), (0, 0), (0, 128)))
     )
+    summed, shared_parts, out_rows = tied(summed, shared_parts, out_rows)
     chance_grad = summed[..., model_width : model_width + EXPERTS]
     quarter_second = own_rows(second)
     quarter_scale = own_rows(scale_two)
@@ -1100,7 +1110,6 @@
     branch_grad = spread_shards(second_grad.astype(bf16))
     returned_out = combine_rows(chosen, bring_rows(out_rows))
     partial_out = (returned_out + shared_out.reshape(trees, rows, model_width)).astype(bf16)
-    branch_grad, partial_out = tied(branch_grad, partial_out)
 
     heads_grad = jnp.einsum(
         "hd,btd->bht", mixing_own, branch_grad, preferred_element_type=f32
@@ -1117,13 +1126,10 @@
             + ((query_grad,) if pair_grads else ()),
         )
         pair_grads.append(pair_grad)
-    blocks = expert_own.reshape(3, group_size, owned, hidden).swapaxes(0, 1)
-    first_home = route(blocks[:, :, : owned // 2])
-    pair_grad, first_home, shared_parts = tied(pair_grads[0], first_home, shared_parts)
-    branches = lax.psum(partial_out, TENSOR)
+    pair_grad = pair_grads[0]
     shared_grads = lax.psum_scatter(
-        shared_parts[0], GROUP, scatter_dimension=1, tiled=True
-    ).astype(f32)
+        shared_parts[0], GROUP, scatter_dimension=0, tiled=True
+    )[0].astype(f32)
     own_grads = []
     for tree in range(trees):
         moving = pair_grad[tree]
@@ -1131,11 +1137,17 @@
             moved = lax.ppermute(
                 moving.astype(bf16), SEQ, [(i + 1, i) for i in range(seq_size - 1)]
             )
-            if tree == trees - 1 and step == seq_size - 2:
-                moved, branches = tied(moved, branches)
+            if tree == 0 and step == 0:
+                moved, expert_parts = tied(moved, expert_parts)
+                expert_own = lax.psum_scatter(
+                    expert_parts, TENSOR, scatter_dimension=0, tiled=False
+                )
             moving = addend[tree] + moved.astype(f32)
         own_grads.append(moving)
-    pair_grad, blocks = tied(jnp.stack(own_grads), blocks)
+    pair_grad, shared_grads, partial_out = tied(jnp.stack(own_grads), shared_grads, partial_out)
+    output = spread_shards((quarter_second + add_shards(partial_out)).astype(bf16))
+    spreader_grad = shared_grads[:2]
+    collector_grad = shared_grads[2].T
     query_grad = query_grad * HEAD_DIM ** (-0.5)
     mapped_grad = jnp.concatenate(
         [
@@ -1150,7 +1162,6 @@
     ).astype(bf16)
     first_part, mapped_grad = tied(first_part, mapped_grad)
     first_grad = add_shards(first_part)
-    output = (second + branches.astype(f32)).astype(bf16)
     project_part = by_rows(
         jnp.einsum("btd,bht->dh", first_in, mapped_grad, preferred_element_type=f32)
     )
@@ -1168,9 +1179,6 @@
         ).astype(bf16)
     )
 
-    input_grad, shared_grads = tied(input_grad, shared_grads)
-    spreader_grad = shared_grads[:2]
-    collector_grad = shared_grads[2].T
 
     small_parts = jnp.concatenate(
         [
@@ -1182,11 +1190,11 @@
         ],
         1,
     ).astype(bf16)
-    second_home, small_parts = tied(route(blocks[:, :, owned // 2 :]), small_parts)
-    expert_grads = jnp.concatenate([first_home, second_home], 2).astype(f32)
+    small_home = route(small_parts.reshape(group_size, owned, -1))
+    small_home, expert_own = tied(small_home, expert_own)
+    expert_grads = route(expert_own).astype(f32)
     expander_grad = expert_grads[:, :2]
     reducer_grad = expert_grads[:, 2].transpose(0, 2, 1)
-    small_home = route(small_parts.reshape(group_size, owned, -1))
     small_grads = jnp.sum(
         small_home.astype(f32),
         0,
@@ -1201,6 +1209,7 @@
         jnp.concatenate([rest.T, gain_one[None]], 0),
         TENSOR,
     )
+    tiny, input_grad = tied(tiny, input_grad)
     router_grad = tiny[:EXPERTS].T
     gain_grad = jnp.stack([tiny[EXPERTS + 1], tiny[EXPERTS]])
     return (

time: 629 us -> 609 us (0.968)
  local copies, waits for them, and re-layouts: 57.9 us -> 43 us
  other arithmetic: 62.9 us -> 48.6 us
  waiting for transfers between devices: 274 us -> 285 us
    ppermute x6, waiting for transfers between devices: 26.5 us -> 53.2 us  [local_fast(): lax.ppermute(moving.astype(bf16), SEQ, [(i + 1, i) for i in range(seq_siz...]
    psum x1 -> x0, waiting for transfers between devices: 13.3 us -> none  [local_fast(): branches = lax.psum(partial_out, TENSOR)]
    reduce_scatter x1, waiting for transfers between devices: 13 us -> 0.02 us  [local_fast(): lax.psum_scatter(shared_parts[0], GROUP, scatter_dimension=0, tiled=True)[0]]
    all_to_all x8 -> x7, waiting for transfers between devices: 154 us -> 163 us  [route(): return lax.all_to_all(blocks, GROUP, split_axis=0, concat_axis=0)]
    all_to_all x8 -> x7, starting transfers between devices: 43.9 us -> 34.5 us  [route(): return lax.all_to_all(blocks, GROUP, split_axis=0, concat_axis=0)]
    ppermute x12 -> x16, waiting for transfers between devices: 42.1 us -> 49 us  [swap(): return lax.ppermute(piece, axes, [(i, i ^ step) for i in range(size)])]
    reduce_scatter x1, waiting for transfers between devices: 6.31 us -> 0.01 us  [local_fast(): lax.psum_scatter(expert_parts, TENSOR, scatter_dimension=0, tiled=False)]
    unnamed x120 -> x128, local copies, waits for them, and re-layouts: 19.1 us -> 13 us
  transfers between devices with their start and end apart: 38 -> 40, of which waited for: 23 -> 27; matrix products, arithmetic and copies ran while one was open for 19% -> 16% of each run, Pallas kernels for 14% -> 14%
where the time goes in v4:
time: 609 us; the launch traced here: 600 us
  waiting for transfers between devices  285 us (47%)
  Pallas kernels  98.3 us (16%)
  starting transfers between devices  71.8 us (12%)
  other arithmetic  48.6 us (8%)
  local copies, waits for them, and re-layouts  43 us (7%)
  matrix products  30.5 us (5%)
  between operations  15.7 us (3%)
  blocking collectives  6.55 us (1%)
    all_to_all x7, waiting for transfers between devices, route(): return lax.all_to_all(blocks, GROUP, split_axis=0, concat_axis=0)  163 us
    ppermute x6, waiting for transfers between devices, local_fast(): lax.ppermute(moving.astype(bf16), SEQ, [(i + 1, i) for i in range(seq_siz...  53.2 us
    ppermute x16, waiting for transfers between devices, swap(): return lax.ppermute(piece, axes, [(i, i ^ step) for i in range(size)])  49 us
    pallas_call x2, Pallas kernels, gated(): pl.pallas_call(gated_kernel, grid=(chunks * tiles,), out_shape=(field, fi...  38.5 us
    all_to_all x7, starting transfers between devices, route(): return lax.all_to_all(blocks, GROUP, split_axis=0, concat_axis=0)  34.5 us
    pallas_call x8, Pallas kernels, attend_call(): pl.pallas_call(kernel, grid=(trees,), out_shape=results, in_specs=[pl.Blo...  33.9 us
    pallas_call x2, Pallas kernels, weight_parts(): pl.pallas_call(parts_kernel, grid=(chunks * tiles,), out_shape=jax.ShapeD...  25.8 us
    ppermute x6, waiting for transfers between devices, local_fast(): lax.ppermute(link, SEQ, [(i, i + 1) for i in range(seq_size - 1)])  19.7 us
  transfers between devices with their start and end apart: 40, of which 27 were waited for; matrix products, arithmetic and copies ran while one was open for 16% of the time, Pallas kernels for 14%

profile of v4, /device:TPU:0, one launch (start us, length us, event | category | flops | bytes accessed | tf_op | source)
XLA Modules:
  0.0 599.8 jit_solution(15997491238753552153)
XLA Ops:
  10.5 7.4 %all-to-all-start = ((bf16[8,3,96,512]{3,2,1,0:T(8,128)(2,1)}), bf16[8,3,96,512]{3,2,1,0:T(8,128)(2,1)S(1)}, u32[]{:S(2)}, u32[]{:S(2)}) async-start(bf16[8,3,96,512]{3,2,1,0:T(8,128)(2,1)} %pad_maximum_fusion), calls=%async_computation | async-start | bytes 4718592 | tf_op jit(solution)/shard_map/all_to_all | solution.py:836
  19.2 64.0 %all-to-all-done = bf16[8,3,96,512]{3,2,1,0:T(8,128)(2,1)S(1)} async-done(((bf16[8,3,96,512]{3,2,1,0:T(8,128)(2,1)}), bf16[8,3,96,512]{3,2,1,0:T(8,128)(2,1)S(1)}, u32[]{:S(2)}, u32[]{:S(2)}) %all-to-all-start) | async-done | bytes 2359328 | tf_op jit(solution)/shard_map/all_to_all | solution.py:836
  104.5 6.2 %attend.4 = (f32[2,3,512]{2,1,0:T(4,128)}, f32[2,3,512]{2,1,0:T(4,128)}, f32[2,192,512]{2,1,0:T(8,128)}) custom-call(s32[1]{0:T(128)} %bitcast.place_ref, bf16[2,192,512]{2,1,0:T(8,128)(2,1)} %bitcast.299, s32[2,2048,1]{2,1,0:T(8,128)} %copy.269.key_bits_ref, s32[2,1,512]{2,1,0:T(1,128)} %broadcast_in_dim.173.query_bits_ref, ...), custom_call_target="tpu_custom_call" | custom-call | flops 1610612736 | bytes 3145728 | tf_op jit(solution)/shard_map/attend/pallas_call | solution.py:642
  154.6 6.3 %all-to-all-start.1 = ((bf16[8,2,48,768]{3,2,1,0:T(8,128)(2,1)}), bf16[8,2,48,768]{3,2,1,0:T(8,128)(2,1)S(1)}, u32[]{:S(2)}, u32[]{:S(2)}) async-start(bf16[8,2,48,768]{3,2,1,0:T(8,128)(2,1)} %bitcast.263), calls=%async_computation.1 | async-start | bytes 2359296 | tf_op jit(solution)/shard_map/all_to_all | solution.py:836
  170.0 5.6 collective-permute-done.6
  181.9 6.1 %all-to-all-done.1 = bf16[8,2,48,768]{3,2,1,0:T(8,128)(2,1)S(1)} async-done(((bf16[8,2,48,768]{3,2,1,0:T(8,128)(2,1)}), bf16[8,2,48,768]{3,2,1,0:T(8,128)(2,1)S(1)}, u32[]{:S(2)}, u32[]{:S(2)}) %all-to-all-start.1) | async-done | bytes 1179680 | tf_op jit(solution)/shard_map/all_to_all | solution.py:836
  200.2 29.2 %all-to-all-done.2 = bf16[8,2,48,768]{3,2,1,0:T(8,128)(2,1)S(1)} async-done(((bf16[8,2,48,768]{3,2,1,0:T(8,128)(2,1)}), bf16[8,2,48,768]{3,2,1,0:T(8,128)(2,1)S(1)}, u32[]{:S(2)}, u32[]{:S(2)}) %all-to-all-start.2) | async-done | bytes 1179680 | tf_op jit(solution)/shard_map/all_to_all | solution.py:836
  232.5 25.8 %gated.2 = (f32[768,768]{1,0:T(8,128)}, f32[768,768]{1,0:T(8,128)}, bf16[768,2048]{1,0:T(8,128)(2,1)}, bf16[768,2048]{1,0:T(8,128)(2,1)}, bf16[768,2048]{1,0:T(8,128)(2,1)}) custom-call(bf16[768,768]{1,0:T(8,128)(2,1)} %bitcast.261, bf16[768,768]{1,0:T(8,128)(2,1)} %fusion.1.grads_ref, bf16[4,3,768,512]{3,2,1,0:T(8,128)(2,1)} %all-gather.6.cloned.1.call-done.weights_ref), custom_call_target="tpu_custom_call" | custom-call | flops 14495514624 | bytes 25952256 | tf_op jit(solution)/shard_map/gated/pallas_call | solution.py:740
  267.4 39.7 %all-to-all-done.3 = bf16[8,2,48,896]{3,2,1,0:T(8,128)(2,1)S(1)} async-done(((bf16[8,2,48,896]{3,2,1,0:T(8,128)(2,1)}), bf16[8,2,48,896]{3,2,1,0:T(8,128)(2,1)S(1)}, u32[]{:S(2)}, u32[]{:S(2)}) %all-to-all-start.3) | async-done | bytes 1376288 | tf_op jit(solution)/shard_map/all_to_all | solution.py:836
  307.2 12.7 %gated.3 = (f32[1024,768]{1,0:T(8,128)}, f32[1024,768]{1,0:T(8,128)}, bf16[1024,512]{1,0:T(8,128)(2,1)}, bf16[1024,512]{1,0:T(8,128)(2,1)}, bf16[1024,512]{1,0:T(8,128)(2,1)}) custom-call(bf16[1024,768]{1,0:T(8,128)(2,1)} %bitcast.268, bf16[1024,768]{1,0:T(8,128)(2,1)} %bitcast.297, bf16[1,3,768,512]{3,2,1,0:T(8,128)(2,1)} %bitcast.310), custom_call_target="tpu_custom_call" | custom-call | flops 4831838208 | bytes 14942208 | tf_op jit(solution)/shard_map/gated/pallas_call | solution.py:740
  327.6 8.5 %weight_parts.2 = bf16[1,8,3,96,512]{4,3,2,1,0:T(8,128)(2,1)} custom-call(bf16[1024,768]{1,0:T(8,128)(2,1)} %bitcast.269, bf16[1024,768]{1,0:T(8,128)(2,1)} %bitcast.298, bf16[1024,512]{1,0:T(8,128)(2,1)} %get-tuple-element.109.first_ref, bf16[1024,512]{1,0:T(8,128)(2,1)} %get-tuple-element.110.second_ref, bf16[1024,512]{1,0:T(8,128)(2,1)} %get-tuple-element.111.active_ref), custom_call_target="tpu_custom_call" | custom-call | flops 2415919104 | bytes 8650752 | tf_op jit(solution)/shard_map/weight_parts/pallas_call | solution.py:791
  348.2 9.0 %collective-permute-done.12 = bf16[1,2,128,768]{3,2,1,0:T(8,128)(2,1)S(1)} collective-permute-done((bf16[1,2,128,768]{3,2,1,0:T(8,128)(2,1)S(1)}, bf16[1,2,128,768]{3,2,1,0:T(8,128)(2,1)S(1)}, u32[]{:S(2)}, u32[]{:S(2)}) %collective-permute-start.12) | collective-permute-done | bytes 393248 | tf_op jit(solution)/shard_map/ppermute | solution.py:811
  368.6 17.4 %weight_parts.3 = bf16[4,8,3,96,512]{4,3,2,1,0:T(8,128)(2,1)} custom-call(bf16[768,768]{1,0:T(8,128)(2,1)} %bitcast.262, bf16[768,768]{1,0:T(8,128)(2,1)} %fusion.1.grads_ref, bf16[768,2048]{1,0:T(8,128)(2,1)} %get-tuple-element.122.first_ref, bf16[768,2048]{1,0:T(8,128)(2,1)} %get-tuple-element.123.second_ref, bf16[768,2048]{1,0:T(8,128)(2,1)} %get-tuple-element.124.active_ref), custom_call_target="tpu_custom_call" | custom-call | flops 7247757312 | bytes 21233664 | tf_op jit(solution)/shard_map/weight_parts/pallas_call | solution.py:791
  403.0 8.2 %attend_back.7 = (f32[2,192,512]{2,1,0:T(8,128)}, f32[2,384,512]{2,1,0:T(8,128)}) custom-call(s32[1]{0:T(128)} %bitcast.place_ref, bf16[2,192,512]{2,1,0:T(8,128)(2,1)} %bitcast.306, bf16[2,192,512]{2,1,0:T(8,128)(2,1)} %get-tuple-element.95.out_ref, bf16[2,192,512]{2,1,0:T(8,128)(2,1)} %fusion.8.grad_ref, f32[2,3,512]{2,1,0:T(4,128)} %get-tuple-element.113.log_ref, ...), custom_call_target="tpu_custom_call" | custom-call | flops 4026531840 | bytes 3145728 | tf_op jit(solution)/shard_map/attend_back/pallas_call | solution.py:642
  411.2 18.9 %collective-permute-done.17 = bf16[384,512]{1,0:T(8,128)(2,1)S(1)} collective-permute-done((bf16[384,512]{1,0:T(8,128)(2,1)S(1)}, bf16[384,512]{1,0:T(8,128)(2,1)S(1)}, u32[]{:S(2)}, u32[]{:S(2)}) %collective-permute-start.17) | collective-permute-done | bytes 393248 | tf_op jit(solution)/shard_map/ppermute | solution.py:1137
  438.5 12.7 %collective-permute-done.15 = bf16[384,512]{1,0:T(8,128)(2,1)S(1)} collective-permute-done((bf16[384,512]{1,0:T(8,128)(2,1)}, bf16[384,512]{1,0:T(8,128)(2,1)S(1)}, u32[]{:S(2)}, u32[]{:S(2)}) %collective-permute-start.15) | collective-permute-done | bytes 393248 | tf_op jit(solution)/shard_map/ppermute | solution.py:1137
  451.2 7.3 %collective-permute-done.18 = bf16[384,512]{1,0:T(8,128)(2,1)} collective-permute-done((bf16[384,512]{1,0:T(8,128)(2,1)}, bf16[384,512]{1,0:T(8,128)(2,1)}, u32[]{:S(2)}, u32[]{:S(2)}) %collective-permute-start.18) | collective-permute-done | bytes 393248 | tf_op jit(solution)/shard_map/ppermute | solution.py:1137
  466.8 8.1 %collective-permute-done.16 = bf16[384,512]{1,0:T(8,128)(2,1)S(1)} collective-permute-done((bf16[384,512]{1,0:T(8,128)(2,1)}, bf16[384,512]{1,0:T(8,128)(2,1)S(1)}, u32[]{:S(2)}, u32[]{:S(2)}) %collective-permute-start.16) | collective-permute-done | bytes 393248 | tf_op jit(solution)/shard_map/ppermute | solution.py:1137
  474.9 6.2 %collective-permute-done.19 = bf16[384,512]{1,0:T(8,128)(2,1)S(1)} collective-permute-done((bf16[384,512]{1,0:T(8,128)(2,1)}, bf16[384,512]{1,0:T(8,128)(2,1)S(1)}, u32[]{:S(2)}, u32[]{:S(2)}) %collective-permute-start.19) | collective-permute-done | bytes 393248 | tf_op jit(solution)/shard_map/ppermute | solution.py:1137
  506.8 9.0 %collective-permute-done.25 = bf16[2,1,128,768]{3,2,0,1:T(8,128)(2,1)S(1)} collective-permute-done((bf16[2,1,128,768]{3,2,0,1:T(8,128)(2,1)S(1)}, bf16[2,1,128,768]{3,2,0,1:T(8,128)(2,1)S(1)}, u32[]{:S(2)}, u32[]{:S(2)}) %collective-permute-start.25) | collective-permute-done | bytes 393248 | tf_op jit(solution)/shard_map/ppermute | solution.py:811
  517.1 14.4 %all-to-all-done.5 = bf16[8,96,896]{2,1,0:T(8,128)(2,1)} async-done(((bf16[8,96,896]{2,1,0:T(8,128)(2,1)}), bf16[8,96,896]{2,1,0:T(8,128)(2,1)}, u32[]{:S(2)}, u32[]{:S(2)}) %all-to-all-start.5) | async-done | bytes 1376288 | tf_op jit(solution)/shard_map/all_to_all | solution.py:836
  540.2 10.0 %collective-permute-done.26 = bf16[1,2,128,768]{3,2,1,0:T(8,128)(2,1)S(1)} collective-permute-done((bf16[1,2,128,768]{3,2,1,0:T(8,128)(2,1)S(1)}, bf16[1,2,128,768]{3,2,1,0:T(8,128)(2,1)S(1)}, u32[]{:S(2)}, u32[]{:S(2)}) %collective-permute-start.26) | collective-permute-done | bytes 393248 | tf_op jit(solution)/shard_map/ppermute | solution.py:811
  570.1 6.6 %psum.7 = f32[10,96]{1,0:T(8,128)S(1)} all-reduce(f32[10,96]{1,0:T(8,128)S(1)} %pad_maximum_fusion.24), channel_id=1, replica_groups=mesh['dp'=2,'seq'=4,'tensor'=4] {'tensor'}, use_global_device_ids=true, to_apply=%region_23.24 | all-reduce | flops 960 | bytes 7680 | tf_op jit(solution)/shard_map/psum | solution.py:1208
  578.7 10.0 %all-to-all-done.6 = bf16[8,3,96,512]{3,2,1,0:T(8,128)(2,1)S(1)} async-done(((bf16[8,3,96,512]{3,2,1,0:T(8,128)(2,1)}), bf16[8,3,96,512]{3,2,1,0:T(8,128)(2,1)S(1)}, u32[]{:S(2)}, u32[]{:S(2)}) %all-to-all-start.6) | async-done | bytes 2359328 | tf_op jit(solution)/shard_map/all_to_all | solution.py:836
  (346 shorter events, 234.9 us)
Async XLA Ops:
  10.5 72.7 %all-to-all-start = ((bf16[8,3,96,512]{3,2,1,0:T(8,128)(2,1)}), bf16[8,3,96,512]{3,2,1,0:T(8,128)(2,1)S(1)}, u32[]{:S(2)}, u32[]{:S(2)}) async-start(bf16[8,3,96,512]{3,2,1,0:T(8,128)(2,1)} %pad_maximum_fusion), calls=%async_computation | async-start | bytes 4718592 | tf_op jit(solution)/shard_map/all_to_all | solution.py:836
  17.9 76.7 %all-gather.4.cloned.1.call-start = ((), (), s32[]{:S(2)}) async-start(), calls=%async_computation.9 | async-start | bytes 1548288 | tf_op jit(solution)/shard_map/all_gather | solution.py:926
  19.1 144.9 %all-gather.6.cloned.1.call-start = ((), (), s32[]{:S(2)}) async-start(), calls=%async_computation.10 | async-start | bytes 11796480 | tf_op jit(solution)/shard_map/all_gather | solution.py:1016
  100.5 15.6 %collective-permute-start.1 = (bf16[1,384,512]{2,1,0:T(8,128)(2,1)S(1)}, bf16[1,384,512]{2,1,0:T(8,128)(2,1)S(1)}, u32[]{:S(2)}, u32[]{:S(2)}) collective-permute-start(bf16[1,384,512]{2,1,0:T(8,128)(2,1)S(1)} %get-tuple-element.239), channel_id=1, source_target_pairs={{0,4},{4,8},{8,12},{1,5},{5,9},{9,13},{2,6},{6,10},{10,14},{3,7},{... | collective-permute-start | bytes 1179656 | tf_op jit(solution)/shard_map/ppermute | solution.py:993
  120.5 14.8 %collective-permute-start.3 = (bf16[1,384,512]{2,1,0:T(8,128)(2,1)S(1)}, bf16[1,384,512]{2,1,0:T(8,128)(2,1)S(1)}, u32[]{:S(2)}, u32[]{:S(2)}) collective-permute-start(bf16[1,384,512]{2,1,0:T(8,128)(2,1)S(1)} %collective-permute-done.1), channel_id=1, source_target_pairs={{0,4},{4,8},{8,12},{1,5},{5,9},{9,13},{2,6},{6,10},{10,14},{3,7},{... | collective-permute-start | bytes 1179656 | tf_op jit(solution)/shard_map/ppermute | solution.py:993
  135.3 13.9 %collective-permute-start.4 = (bf16[1,384,512]{2,1,0:T(8,128)(2,1)S(1)}, bf16[1,384,512]{2,1,0:T(8,128)(2,1)S(1)}, u32[]{:S(2)}, u32[]{:S(2)}) collective-permute-start(bf16[1,384,512]{2,1,0:T(8,128)(2,1)S(1)} %collective-permute-done.2), channel_id=1, source_target_pairs={{0,4},{4,8},{8,12},{1,5},{5,9},{9,13},{2,6},{6,10},{10,14},{3,7},{... | collective-permute-start | bytes 1179656 | tf_op jit(solution)/shard_map/ppermute | solution.py:993
  139.7 14.0 %collective-permute-start.5 = (bf16[1,384,512]{2,1,0:T(8,128)(2,1)S(1)}, bf16[1,384,512]{2,1,0:T(8,128)(2,1)S(1)}, u32[]{:S(2)}, u32[]{:S(2)}) collective-permute-start(bf16[1,384,512]{2,1,0:T(8,128)(2,1)S(1)} %collective-permute-done.3), channel_id=1, source_target_pairs={{0,4},{4,8},{8,12},{1,5},{5,9},{9,13},{2,6},{6,10},{10,14},{3,7},{... | collective-permute-start | bytes 1179656 | tf_op jit(solution)/shard_map/ppermute | solution.py:993
  154.6 33.3 %all-to-all-start.1 = ((bf16[8,2,48,768]{3,2,1,0:T(8,128)(2,1)}), bf16[8,2,48,768]{3,2,1,0:T(8,128)(2,1)S(1)}, u32[]{:S(2)}, u32[]{:S(2)}) async-start(bf16[8,2,48,768]{3,2,1,0:T(8,128)(2,1)} %bitcast.263), calls=%async_computation.1 | async-start | bytes 2359296 | tf_op jit(solution)/shard_map/all_to_all | solution.py:836
  195.3 34.0 %all-to-all-start.2 = ((bf16[8,2,48,768]{3,2,1,0:T(8,128)(2,1)}), bf16[8,2,48,768]{3,2,1,0:T(8,128)(2,1)S(1)}, u32[]{:S(2)}, u32[]{:S(2)}) async-start(bf16[8,2,48,768]{3,2,1,0:T(8,128)(2,1)} %bitcast.265), calls=%async_computation.2 | async-start | bytes 2359296 | tf_op jit(solution)/shard_map/all_to_all | solution.py:836
  199.4 107.9 %all-gather.8.cloned.1.call-start = ((), (), s32[]{:S(2)}) async-start(), calls=%async_computation.11 | async-start | bytes 2654208 | tf_op jit(solution)/shard_map/all_gather | solution.py:1032
  263.5 43.5 %all-to-all-start.3 = ((bf16[8,2,48,896]{3,2,1,0:T(8,128)(2,1)}), bf16[8,2,48,896]{3,2,1,0:T(8,128)(2,1)S(1)}, u32[]{:S(2)}, u32[]{:S(2)}) async-start(bf16[8,2,48,896]{3,2,1,0:T(8,128)(2,1)} %bitcast.35), calls=%async_computation.3 | async-start | bytes 2752512 | tf_op jit(solution)/shard_map/all_to_all | solution.py:836
  267.1 214.4 %reduce-scatter.3.cloned.1.call-start = ((), (), s32[]{:S(2)}) async-start(), calls=%async_computation.12 | async-start | bytes 2654208 | tf_op jit(solution)/shard_map/reduce_scatter | solution.py:1130
  339.8 191.7 %reduce-scatter.5.cloned.1.call-start = ((), (), s32[]{:S(2)}) async-start(), calls=%async_computation.13 | async-start | bytes 11796480 | tf_op jit(solution)/shard_map/reduce_scatter | solution.py:1142
  367.3 18.7 %collective-permute-start.14 = (bf16[384,512]{1,0:T(8,128)(2,1)S(1)}, bf16[384,512]{1,0:T(8,128)(2,1)S(1)}, u32[]{:S(2)}, u32[]{:S(2)}) collective-permute-start(bf16[384,512]{1,0:T(8,128)(2,1)S(1)} %get-tuple-element.237), channel_id=1, source_target_pairs={{4,0},{8,4},{12,8},{5,1},{9,5},{13,9},{6,2},{10,6},{14,10},{7,3},{... | collective-permute-start | bytes 1179656 | tf_op jit(solution)/shard_map/ppermute | solution.py:1137
  386.0 77.3 %all-to-all-start.4 = ((bf16[8,2,48,768]{3,2,1,0:T(8,128)(2,1)}), bf16[8,2,48,768]{3,2,1,0:T(8,128)(2,1)S(1)}, u32[]{:S(2)}, u32[]{:S(2)}) async-start(bf16[8,2,48,768]{3,2,1,0:T(8,128)(2,1)} %bitcast.63), calls=%async_computation.5 | async-start | bytes 2359296 | tf_op jit(solution)/shard_map/all_to_all | solution.py:836
  394.2 35.9 %collective-permute-start.17 = (bf16[384,512]{1,0:T(8,128)(2,1)S(1)}, bf16[384,512]{1,0:T(8,128)(2,1)S(1)}, u32[]{:S(2)}, u32[]{:S(2)}) collective-permute-start(bf16[384,512]{1,0:T(8,128)(2,1)S(1)} %get-tuple-element.238), channel_id=1, source_target_pairs={{4,0},{8,4},{12,8},{5,1},{9,5},{13,9},{6,2},{10,6},{14,10},{7,3},{... | collective-permute-start | bytes 1179656 | tf_op jit(solution)/shard_map/ppermute | solution.py:1137
  431.3 19.9 %collective-permute-start.15 = (bf16[384,512]{1,0:T(8,128)(2,1)}, bf16[384,512]{1,0:T(8,128)(2,1)S(1)}, u32[]{:S(2)}, u32[]{:S(2)}) collective-permute-start(bf16[384,512]{1,0:T(8,128)(2,1)} %get-tuple-element.223), channel_id=1, source_target_pairs={{4,0},{8,4},{12,8},{5,1},{9,5},{13,9},{6,2},{10,6},{14,10},{7,3},{... | collective-permute-start | bytes 1179656 | tf_op jit(solution)/shard_map/ppermute | solution.py:1137
  432.6 25.9 %collective-permute-start.18 = (bf16[384,512]{1,0:T(8,128)(2,1)}, bf16[384,512]{1,0:T(8,128)(2,1)}, u32[]{:S(2)}, u32[]{:S(2)}) collective-permute-start(bf16[384,512]{1,0:T(8,128)(2,1)} %get-tuple-element.224), channel_id=1, source_target_pairs={{4,0},{8,4},{12,8},{5,1},{9,5},{13,9},{6,2},{10,6},{14,10},{7,3},{... | collective-permute-start | bytes 1179656 | tf_op jit(solution)/shard_map/ppermute | solution.py:1137
  460.6 14.3 %collective-permute-start.16 = (bf16[384,512]{1,0:T(8,128)(2,1)}, bf16[384,512]{1,0:T(8,128)(2,1)S(1)}, u32[]{:S(2)}, u32[]{:S(2)}) collective-permute-start(bf16[384,512]{1,0:T(8,128)(2,1)} %get-tuple-element.221), channel_id=1, source_target_pairs={{4,0},{8,4},{12,8},{5,1},{9,5},{13,9},{6,2},{10,6},{14,10},{7,3},{... | collective-permute-start | bytes 1179656 | tf_op jit(solution)/shard_map/ppermute | solution.py:1137
  462.0 19.1 %collective-permute-start.19 = (bf16[384,512]{1,0:T(8,128)(2,1)}, bf16[384,512]{1,0:T(8,128)(2,1)S(1)}, u32[]{:S(2)}, u32[]{:S(2)}) collective-permute-start(bf16[384,512]{1,0:T(8,128)(2,1)} %get-tuple-element.222), channel_id=1, source_target_pairs={{4,0},{8,4},{12,8},{5,1},{9,5},{13,9},{6,2},{10,6},{14,10},{7,3},{... | collective-permute-start | bytes 1179656 | tf_op jit(solution)/shard_map/ppermute | solution.py:1137
  495.0 36.5 %all-to-all-start.5 = ((bf16[8,96,896]{2,1,0:T(8,128)(2,1)}), bf16[8,96,896]{2,1,0:T(8,128)(2,1)}, u32[]{:S(2)}, u32[]{:S(2)}) async-start(bf16[8,96,896]{2,1,0:T(8,128)(2,1)} %concatenate.111), calls=%async_computation.6 | async-start | bytes 2752512 | tf_op jit(solution)/shard_map/all_to_all | solution.py:836
  504.6 31.0 %collective-permute-start.21 = (bf16[2,1,128,768]{3,2,0,1:T(8,128)(2,1)S(1)}, bf16[2,1,128,768]{3,2,0,1:T(8,128)(2,1)}, u32[]{:S(2)}, u32[]{:S(2)}) collective-permute-start(bf16[2,1,128,768]{3,2,0,1:T(8,128)(2,1)S(1)} %constant_dynamic-slice_fusion.4), channel_id=1, source_target_pairs={{0,2},{1,3},{2,0},{3,1},{4,6},{5,7},{6,4},{7,5},{8,10},{9,11},{10,... | collective-permute-start | bytes 1179656 | tf_op jit(solution)/shard_map/ppermute | solution.py:811
  531.5 57.2 %all-to-all-start.6 = ((bf16[8,3,96,512]{3,2,1,0:T(8,128)(2,1)}), bf16[8,3,96,512]{3,2,1,0:T(8,128)(2,1)S(1)}, u32[]{:S(2)}, u32[]{:S(2)}) async-start(bf16[8,3,96,512]{3,2,1,0:T(8,128)(2,1)} %bitcast.278), calls=%async_computation.8 | async-start | bytes 4718592 | tf_op jit(solution)/shard_map/all_to_all | solution.py:836
  538.5 17.2 %collective-permute-start.22 = (bf16[1,2,128,768]{3,2,1,0:T(8,128)(2,1)S(1)}, bf16[1,2,128,768]{3,2,1,0:T(8,128)(2,1)S(1)}, u32[]{:S(2)}, u32[]{:S(2)}) collective-permute-start(bf16[1,2,128,768]{3,2,1,0:T(8,128)(2,1)S(1)} %get-tuple-element.200), channel_id=1, source_target_pairs={{0,2},{1,3},{2,0},{3,1},{4,6},{5,7},{6,4},{7,5},{8,10},{9,11},{10,... | collective-permute-start | bytes 1179656 | tf_op jit(solution)/shard_map/ppermute | solution.py:811
  (75 other events, 678.8 us)
Sparse Core Ops, SparseCore 0:
  21.4 69.9 all-gather.3
  93.5 63.3 all-gather.5
  229.5 52.8 all-gather.7
  339.9 90.4 reduce-scatter.2
  432.9 76.4 reduce-scatter.4

commit v5 on v4

--- a/solution.py
+++ b/solution.py
@@ -1115,35 +1115,32 @@
         "hd,btd->bht", mixing_own, branch_grad, preferred_element_type=f32
     ).astype(bf16)
     mixing_part = jnp.einsum("btd,bht->dh", branch_grad, outs, preferred_element_type=f32)
-    query_grad = ()
-    pair_grads = []
-    for number in range(seq_size - 1, -1, -1):
-        query_grad, pair_grad = attend_back(
+    def block_back(number, query_grad):
+        return attend_back(
             number,
             bf16 if number == seq_size - 1 else f32,
             place_arg,
-            (queries, outs, heads_grad, logs, key_column, path_row, pairs[number])
-            + ((query_grad,) if pair_grads else ()),
-        )
-        pair_grads.append(pair_grad)
-    pair_grad = pair_grads[0]
+            (queries, outs, heads_grad, logs, key_column, path_row, pairs[number]) + query_grad,
+        )
+
+    query_grad, pair_grad = block_back(seq_size - 1, ())
     shared_grads = lax.psum_scatter(
         shared_parts[0], GROUP, scatter_dimension=0, tiled=True
     )[0].astype(f32)
-    own_grads = []
-    for tree in range(trees):
-        moving = pair_grad[tree]
-        for step, addend in enumerate(pair_grads[1:]):
-            moved = lax.ppermute(
-                moving.astype(bf16), SEQ, [(i + 1, i) for i in range(seq_size - 1)]
-            )
-            if tree == 0 and step == 0:
-                moved, expert_parts = tied(moved, expert_parts)
-                expert_own = lax.psum_scatter(
-                    expert_parts, TENSOR, scatter_dimension=0, tiled=False
-                )
-            moving = addend[tree] + moved.astype(f32)
-        own_grads.append(moving)
+    moving = [pair_grad[tree] for tree in range(trees)]
+    for step in range(seq_size - 1):
+        query_grad, pair_grad = block_back(seq_size - 2 - step, (query_grad,))
+        moved = [
+            lax.ppermute(grads.astype(bf16), SEQ, [(i + 1, i) for i in range(seq_size - 1)])
+            for grads in moving
+        ]
+        if step == 0:
+            *moved, expert_parts = tied(*moved, expert_parts)
+            expert_own = lax.psum_scatter(expert_parts, TENSOR, scatter_dimension=0, tiled=False)
+        moving = [pair_grad[tree] + moved[tree].astype(f32) for tree in range(trees)]
+        if step < seq_size - 2:
+            query_grad, *moving = tied(query_grad, *moving)
+    own_grads = moving
     pair_grad, shared_grads, partial_out = tied(jnp.stack(own_grads), shared_grads, partial_out)
     output = spread_shards((quarter_second + add_shards(partial_out)).astype(bf16))
     spreader_grad = shared_grads[:2]

time: 609 us -> 599 us (0.984)
  waiting for transfers between devices: 285 us -> 270 us
    ppermute x6, waiting for transfers between devices: 53.2 us -> 38.7 us  [local_fast(): lax.ppermute(grads.astype(bf16), SEQ, [(i + 1, i) for i in range(seq_size...]
    all_to_all x7, waiting for transfers between devices: 163 us -> 156 us  [route(): return lax.all_to_all(blocks, GROUP, split_axis=0, concat_axis=0)]
    ppermute x16, waiting for transfers between devices: 49 us -> 55.3 us  [swap(): return lax.ppermute(piece, axes, [(i, i ^ step) for i in range(size)])]
  transfers between devices with their start and end apart: 40 -> 40, of which waited for: 27 -> 26; matrix products, arithmetic and copies ran while one was open for 16% -> 17% of each run, Pallas kernels for 14% -> 14%
where the time goes in v5:
time: 599 us; the launch traced here: 589 us
  waiting for transfers between devices  270 us (45%)
  Pallas kernels  98.1 us (16%)
  starting transfers between devices  73.2 us (12%)
  other arithmetic  50.2 us (8%)
  local copies, waits for them, and re-layouts  44 us (7%)
  matrix products  30.4 us (5%)
  between operations  15.7 us (3%)
  blocking collectives  7.33 us (1%)
    all_to_all x7, waiting for transfers between devices, route(): return lax.all_to_all(blocks, GROUP, split_axis=0, concat_axis=0)  156 us
    ppermute x16, waiting for transfers between devices, swap(): return lax.ppermute(piece, axes, [(i, i ^ step) for i in range(size)])  55.3 us
    ppermute x6, waiting for transfers between devices, local_fast(): lax.ppermute(grads.astype(bf16), SEQ, [(i + 1, i) for i in range(seq_size...  38.7 us
    pallas_call x2, Pallas kernels, gated(): pl.pallas_call(gated_kernel, grid=(chunks * tiles,), out_shape=(field, fi...  38.5 us
    all_to_all x7, starting transfers between devices, route(): return lax.all_to_all(blocks, GROUP, split_axis=0, concat_axis=0)  35.5 us
    pallas_call x8, Pallas kernels, attend_call(): pl.pallas_call(kernel, grid=(trees,), out_shape=results, in_specs=[pl.Blo...  33.8 us
    pallas_call x2, Pallas kernels, weight_parts(): pl.pallas_call(parts_kernel, grid=(chunks * tiles,), out_shape=jax.ShapeD...  25.8 us
    ppermute x6, waiting for transfers between devices, local_fast(): lax.ppermute(link, SEQ, [(i, i + 1) for i in range(seq_size - 1)])  19.7 us
  transfers between devices with their start and end apart: 40, of which 26 were waited for; matrix products, arithmetic and copies ran while one was open for 17% of the time, Pallas kernels for 14%

profile of v5, /device:TPU:0, one launch (start us, length us, event | category | flops | bytes accessed | tf_op | source)
XLA Modules:
  0.0 589.1 jit_solution(8541106716001226477)
XLA Ops:
  10.5 7.4 %all-to-all-start = ((bf16[8,3,96,512]{3,2,1,0:T(8,128)(2,1)}), bf16[8,3,96,512]{3,2,1,0:T(8,128)(2,1)S(1)}, u32[]{:S(2)}, u32[]{:S(2)}) async-start(bf16[8,3,96,512]{3,2,1,0:T(8,128)(2,1)} %pad_maximum_fusion), calls=%async_computation | async-start | bytes 4718592 | tf_op jit(solution)/shard_map/all_to_all | solution.py:836
  19.2 64.0 %all-to-all-done = bf16[8,3,96,512]{3,2,1,0:T(8,128)(2,1)S(1)} async-done(((bf16[8,3,96,512]{3,2,1,0:T(8,128)(2,1)}), bf16[8,3,96,512]{3,2,1,0:T(8,128)(2,1)S(1)}, u32[]{:S(2)}, u32[]{:S(2)}) %all-to-all-start) | async-done | bytes 2359328 | tf_op jit(solution)/shard_map/all_to_all | solution.py:836
  104.5 6.2 %attend.4 = (f32[2,3,512]{2,1,0:T(4,128)}, f32[2,3,512]{2,1,0:T(4,128)}, f32[2,192,512]{2,1,0:T(8,128)}) custom-call(s32[1]{0:T(128)} %bitcast.place_ref, bf16[2,192,512]{2,1,0:T(8,128)(2,1)} %bitcast.291, s32[2,2048,1]{2,1,0:T(8,128)} %copy.269.key_bits_ref, s32[2,1,512]{2,1,0:T(1,128)} %broadcast_in_dim.173.query_bits_ref, ...), custom_call_target="tpu_custom_call" | custom-call | flops 1610612736 | bytes 3145728 | tf_op jit(solution)/shard_map/attend/pallas_call | solution.py:642
  110.7 5.4 collective-permute-done.1
  154.6 6.3 %all-to-all-start.1 = ((bf16[8,2,48,768]{3,2,1,0:T(8,128)(2,1)}), bf16[8,2,48,768]{3,2,1,0:T(8,128)(2,1)S(1)}, u32[]{:S(2)}, u32[]{:S(2)}) async-start(bf16[8,2,48,768]{3,2,1,0:T(8,128)(2,1)} %bitcast.255), calls=%async_computation.1 | async-start | bytes 2359296 | tf_op jit(solution)/shard_map/all_to_all | solution.py:836
  170.0 5.6 collective-permute-done.6
  181.9 6.1 %all-to-all-done.1 = bf16[8,2,48,768]{3,2,1,0:T(8,128)(2,1)S(1)} async-done(((bf16[8,2,48,768]{3,2,1,0:T(8,128)(2,1)}), bf16[8,2,48,768]{3,2,1,0:T(8,128)(2,1)S(1)}, u32[]{:S(2)}, u32[]{:S(2)}) %all-to-all-start.1) | async-done | bytes 1179680 | tf_op jit(solution)/shard_map/all_to_all | solution.py:836
  200.2 29.2 %all-to-all-done.2 = bf16[8,2,48,768]{3,2,1,0:T(8,128)(2,1)S(1)} async-done(((bf16[8,2,48,768]{3,2,1,0:T(8,128)(2,1)}), bf16[8,2,48,768]{3,2,1,0:T(8,128)(2,1)S(1)}, u32[]{:S(2)}, u32[]{:S(2)}) %all-to-all-start.2) | async-done | bytes 1179680 | tf_op jit(solution)/shard_map/all_to_all | solution.py:836
  232.5 25.8 %gated.2 = (f32[768,768]{1,0:T(8,128)}, f32[768,768]{1,0:T(8,128)}, bf16[768,2048]{1,0:T(8,128)(2,1)}, bf16[768,2048]{1,0:T(8,128)(2,1)}, bf16[768,2048]{1,0:T(8,128)(2,1)}) custom-call(bf16[768,768]{1,0:T(8,128)(2,1)} %bitcast.253, bf16[768,768]{1,0:T(8,128)(2,1)} %fusion.1.grads_ref, bf16[4,3,768,512]{3,2,1,0:T(8,128)(2,1)} %all-gather.6.cloned.1.call-done.weights_ref), custom_call_target="tpu_custom_call" | custom-call | flops 14495514624 | bytes 25952256 | tf_op jit(solution)/shard_map/gated/pallas_call | solution.py:740
  267.4 39.7 %all-to-all-done.3 = bf16[8,2,48,896]{3,2,1,0:T(8,128)(2,1)S(1)} async-done(((bf16[8,2,48,896]{3,2,1,0:T(8,128)(2,1)}), bf16[8,2,48,896]{3,2,1,0:T(8,128)(2,1)S(1)}, u32[]{:S(2)}, u32[]{:S(2)}) %all-to-all-start.3) | async-done | bytes 1376288 | tf_op jit(solution)/shard_map/all_to_all | solution.py:836
  307.2 12.7 %gated.3 = (f32[1024,768]{1,0:T(8,128)}, f32[1024,768]{1,0:T(8,128)}, bf16[1024,512]{1,0:T(8,128)(2,1)}, bf16[1024,512]{1,0:T(8,128)(2,1)}, bf16[1024,512]{1,0:T(8,128)(2,1)}) custom-call(bf16[1024,768]{1,0:T(8,128)(2,1)} %bitcast.260, bf16[1024,768]{1,0:T(8,128)(2,1)} %bitcast.289, bf16[1,3,768,512]{3,2,1,0:T(8,128)(2,1)} %bitcast.302), custom_call_target="tpu_custom_call" | custom-call | flops 4831838208 | bytes 14942208 | tf_op jit(solution)/shard_map/gated/pallas_call | solution.py:740
  327.6 8.5 %weight_parts.2 = bf16[1,8,3,96,512]{4,3,2,1,0:T(8,128)(2,1)} custom-call(bf16[1024,768]{1,0:T(8,128)(2,1)} %bitcast.261, bf16[1024,768]{1,0:T(8,128)(2,1)} %bitcast.290, bf16[1024,512]{1,0:T(8,128)(2,1)} %get-tuple-element.116.first_ref, bf16[1024,512]{1,0:T(8,128)(2,1)} %get-tuple-element.117.second_ref, bf16[1024,512]{1,0:T(8,128)(2,1)} %get-tuple-element.118.active_ref), custom_call_target="tpu_custom_call" | custom-call | flops 2415919104 | bytes 8650752 | tf_op jit(solution)/shard_map/weight_parts/pallas_call | solution.py:791
  348.2 9.0 %collective-permute-done.12 = bf16[1,2,128,768]{3,2,1,0:T(8,128)(2,1)S(1)} collective-permute-done((bf16[1,2,128,768]{3,2,1,0:T(8,128)(2,1)S(1)}, bf16[1,2,128,768]{3,2,1,0:T(8,128)(2,1)S(1)}, u32[]{:S(2)}, u32[]{:S(2)}) %collective-permute-start.12) | collective-permute-done | bytes 393248 | tf_op jit(solution)/shard_map/ppermute | solution.py:811
  370.1 17.4 %weight_parts.3 = bf16[4,8,3,96,512]{4,3,2,1,0:T(8,128)(2,1)} custom-call(bf16[768,768]{1,0:T(8,128)(2,1)} %bitcast.254, bf16[768,768]{1,0:T(8,128)(2,1)} %fusion.1.grads_ref, bf16[768,2048]{1,0:T(8,128)(2,1)} %get-tuple-element.126.first_ref, bf16[768,2048]{1,0:T(8,128)(2,1)} %get-tuple-element.127.second_ref, bf16[768,2048]{1,0:T(8,128)(2,1)} %get-tuple-element.128.active_ref), custom_call_target="tpu_custom_call" | custom-call | flops 7247757312 | bytes 21233664 | tf_op jit(solution)/shard_map/weight_parts/pallas_call | solution.py:791
  389.0 5.4 all-to-all-start.4
  412.0 19.7 %collective-permute-done.16 = bf16[384,512]{1,0:T(8,128)(2,1)S(1)} collective-permute-done((bf16[384,512]{1,0:T(8,128)(2,1)S(1)}, bf16[384,512]{1,0:T(8,128)(2,1)S(1)}, u32[]{:S(2)}, u32[]{:S(2)}) %collective-permute-start.16) | collective-permute-done | bytes 393248 | tf_op jit(solution)/shard_map/ppermute | solution.py:1134
  431.7 7.5 %collective-permute-done.17 = bf16[384,512]{1,0:T(8,128)(2,1)S(1)} collective-permute-done((bf16[384,512]{1,0:T(8,128)(2,1)S(1)}, bf16[384,512]{1,0:T(8,128)(2,1)S(1)}, u32[]{:S(2)}, u32[]{:S(2)}) %collective-permute-start.17) | collective-permute-done | bytes 393248 | tf_op jit(solution)/shard_map/ppermute | solution.py:1134
  443.8 8.1 %attend_back.7 = (f32[2,192,512]{2,1,0:T(8,128)}, f32[2,384,512]{2,1,0:T(8,128)}) custom-call(s32[1]{0:T(128)} %bitcast.place_ref, bf16[2,192,512]{2,1,0:T(8,128)(2,1)} %bitcast.298, bf16[2,192,512]{2,1,0:T(8,128)(2,1)} %get-tuple-element.102.out_ref, bf16[2,192,512]{2,1,0:T(8,128)(2,1)} %fusion.8.grad_ref, f32[2,3,512]{2,1,0:T(4,128)} %get-tuple-element.120.log_ref, ...), custom_call_target="tpu_custom_call" | custom-call | flops 4026531840 | bytes 3145728 | tf_op jit(solution)/shard_map/attend_back/pallas_call | solution.py:642
  461.0 7.1 %collective-permute-done.19 = bf16[384,512]{1,0:T(8,128)(2,1)} collective-permute-done((bf16[384,512]{1,0:T(8,128)(2,1)S(1)}, bf16[384,512]{1,0:T(8,128)(2,1)}, u32[]{:S(2)}, u32[]{:S(2)}) %collective-permute-start.19) | collective-permute-done | bytes 393248 | tf_op jit(solution)/shard_map/ppermute | solution.py:1134
  495.8 15.5 %collective-permute-done.25 = bf16[2,1,128,768]{3,2,0,1:T(8,128)(2,1)S(1)} collective-permute-done((bf16[2,1,128,768]{3,2,0,1:T(8,128)(2,1)S(1)}, bf16[2,1,128,768]{3,2,0,1:T(8,128)(2,1)S(1)}, u32[]{:S(2)}, u32[]{:S(2)}) %collective-permute-start.25) | collective-permute-done | bytes 393248 | tf_op jit(solution)/shard_map/ppermute | solution.py:811
  512.6 8.2 %all-to-all-done.5 = bf16[8,96,896]{2,1,0:T(8,128)(2,1)} async-done(((bf16[8,96,896]{2,1,0:T(8,128)(2,1)}), bf16[8,96,896]{2,1,0:T(8,128)(2,1)}, u32[]{:S(2)}, u32[]{:S(2)}) %all-to-all-start.5) | async-done | bytes 1376288 | tf_op jit(solution)/shard_map/all_to_all | solution.py:836
  529.5 10.0 %collective-permute-done.26 = bf16[1,2,128,768]{3,2,1,0:T(8,128)(2,1)S(1)} collective-permute-done((bf16[1,2,128,768]{3,2,1,0:T(8,128)(2,1)S(1)}, bf16[1,2,128,768]{3,2,1,0:T(8,128)(2,1)S(1)}, u32[]{:S(2)}, u32[]{:S(2)}) %collective-permute-start.26) | collective-permute-done | bytes 393248 | tf_op jit(solution)/shard_map/ppermute | solution.py:811
  559.4 7.3 %psum.7 = f32[10,96]{1,0:T(8,128)S(1)} all-reduce(f32[10,96]{1,0:T(8,128)S(1)} %pad_maximum_fusion.24), channel_id=1, replica_groups=mesh['dp'=2,'seq'=4,'tensor'=4] {'tensor'}, use_global_device_ids=true, to_apply=%region_23.24 | all-reduce | flops 960 | bytes 7680 | tf_op jit(solution)/shard_map/psum | solution.py:1205
  568.8 9.2 %all-to-all-done.6 = bf16[8,3,96,512]{3,2,1,0:T(8,128)(2,1)S(1)} async-done(((bf16[8,3,96,512]{3,2,1,0:T(8,128)(2,1)}), bf16[8,3,96,512]{3,2,1,0:T(8,128)(2,1)S(1)}, u32[]{:S(2)}, u32[]{:S(2)}) %all-to-all-start.6) | async-done | bytes 2359328 | tf_op jit(solution)/shard_map/all_to_all | solution.py:836
  (346 shorter events, 232.2 us)
Async XLA Ops:
  10.5 72.7 %all-to-all-start = ((bf16[8,3,96,512]{3,2,1,0:T(8,128)(2,1)}), bf16[8,3,96,512]{3,2,1,0:T(8,128)(2,1)S(1)}, u32[]{:S(2)}, u32[]{:S(2)}) async-start(bf16[8,3,96,512]{3,2,1,0:T(8,128)(2,1)} %pad_maximum_fusion), calls=%async_computation | async-start | bytes 4718592 | tf_op jit(solution)/shard_map/all_to_all | solution.py:836
  17.9 76.7 %all-gather.4.cloned.1.call-start = ((), (), s32[]{:S(2)}) async-start(), calls=%async_computation.9 | async-start | bytes 1548288 | tf_op jit(solution)/shard_map/all_gather | solution.py:926
  19.1 144.9 %all-gather.6.cloned.1.call-start = ((), (), s32[]{:S(2)}) async-start(), calls=%async_computation.10 | async-start | bytes 11796480 | tf_op jit(solution)/shard_map/all_gather | solution.py:1016
  100.5 15.6 %collective-permute-start.1 = (bf16[1,384,512]{2,1,0:T(8,128)(2,1)S(1)}, bf16[1,384,512]{2,1,0:T(8,128)(2,1)S(1)}, u32[]{:S(2)}, u32[]{:S(2)}) collective-permute-start(bf16[1,384,512]{2,1,0:T(8,128)(2,1)S(1)} %get-tuple-element.253), channel_id=1, source_target_pairs={{0,4},{4,8},{8,12},{1,5},{5,9},{9,13},{2,6},{6,10},{10,14},{3,7},{... | collective-permute-start | bytes 1179656 | tf_op jit(solution)/shard_map/ppermute | solution.py:993
  120.5 14.8 %collective-permute-start.3 = (bf16[1,384,512]{2,1,0:T(8,128)(2,1)S(1)}, bf16[1,384,512]{2,1,0:T(8,128)(2,1)S(1)}, u32[]{:S(2)}, u32[]{:S(2)}) collective-permute-start(bf16[1,384,512]{2,1,0:T(8,128)(2,1)S(1)} %collective-permute-done.1), channel_id=1, source_target_pairs={{0,4},{4,8},{8,12},{1,5},{5,9},{9,13},{2,6},{6,10},{10,14},{3,7},{... | collective-permute-start | bytes 1179656 | tf_op jit(solution)/shard_map/ppermute | solution.py:993
  139.7 14.0 %collective-permute-start.5 = (bf16[1,384,512]{2,1,0:T(8,128)(2,1)S(1)}, bf16[1,384,512]{2,1,0:T(8,128)(2,1)S(1)}, u32[]{:S(2)}, u32[]{:S(2)}) collective-permute-start(bf16[1,384,512]{2,1,0:T(8,128)(2,1)S(1)} %collective-permute-done.3), channel_id=1, source_target_pairs={{0,4},{4,8},{8,12},{1,5},{5,9},{9,13},{2,6},{6,10},{10,14},{3,7},{... | collective-permute-start | bytes 1179656 | tf_op jit(solution)/shard_map/ppermute | solution.py:993
  154.6 33.3 %all-to-all-start.1 = ((bf16[8,2,48,768]{3,2,1,0:T(8,128)(2,1)}), bf16[8,2,48,768]{3,2,1,0:T(8,128)(2,1)S(1)}, u32[]{:S(2)}, u32[]{:S(2)}) async-start(bf16[8,2,48,768]{3,2,1,0:T(8,128)(2,1)} %bitcast.255), calls=%async_computation.1 | async-start | bytes 2359296 | tf_op jit(solution)/shard_map/all_to_all | solution.py:836
  195.3 34.0 %all-to-all-start.2 = ((bf16[8,2,48,768]{3,2,1,0:T(8,128)(2,1)}), bf16[8,2,48,768]{3,2,1,0:T(8,128)(2,1)S(1)}, u32[]{:S(2)}, u32[]{:S(2)}) async-start(bf16[8,2,48,768]{3,2,1,0:T(8,128)(2,1)} %bitcast.257), calls=%async_computation.2 | async-start | bytes 2359296 | tf_op jit(solution)/shard_map/all_to_all | solution.py:836
  199.4 107.9 %all-gather.8.cloned.1.call-start = ((), (), s32[]{:S(2)}) async-start(), calls=%async_computation.11 | async-start | bytes 2654208 | tf_op jit(solution)/shard_map/all_gather | solution.py:1032
  263.5 43.5 %all-to-all-start.3 = ((bf16[8,2,48,896]{3,2,1,0:T(8,128)(2,1)}), bf16[8,2,48,896]{3,2,1,0:T(8,128)(2,1)S(1)}, u32[]{:S(2)}, u32[]{:S(2)}) async-start(bf16[8,2,48,896]{3,2,1,0:T(8,128)(2,1)} %bitcast.35), calls=%async_computation.3 | async-start | bytes 2752512 | tf_op jit(solution)/shard_map/all_to_all | solution.py:836
  267.1 202.5 %reduce-scatter.3.cloned.1.call-start = ((), (), s32[]{:S(2)}) async-start(), calls=%async_computation.12 | async-start | bytes 2654208 | tf_op jit(solution)/shard_map/reduce_scatter | solution.py:1127
  339.8 181.0 %reduce-scatter.5.cloned.1.call-start = ((), (), s32[]{:S(2)}) async-start(), calls=%async_computation.13 | async-start | bytes 11796480 | tf_op jit(solution)/shard_map/reduce_scatter | solution.py:1139
  367.5 20.0 %collective-permute-start.14 = (bf16[384,512]{1,0:T(8,128)(2,1)S(1)}, bf16[384,512]{1,0:T(8,128)(2,1)S(1)}, u32[]{:S(2)}, u32[]{:S(2)}) collective-permute-start(bf16[384,512]{1,0:T(8,128)(2,1)S(1)} %get-tuple-element.252), channel_id=1, source_target_pairs={{4,0},{8,4},{12,8},{5,1},{9,5},{13,9},{6,2},{10,6},{14,10},{7,3},{... | collective-permute-start | bytes 1179656 | tf_op jit(solution)/shard_map/ppermute | solution.py:1134
  368.8 20.2 %collective-permute-start.15 = (bf16[384,512]{1,0:T(8,128)(2,1)S(1)}, bf16[384,512]{1,0:T(8,128)(2,1)S(1)}, u32[]{:S(2)}, u32[]{:S(2)}) collective-permute-start(bf16[384,512]{1,0:T(8,128)(2,1)S(1)} %get-tuple-element.251), channel_id=1, source_target_pairs={{4,0},{8,4},{12,8},{5,1},{9,5},{13,9},{6,2},{10,6},{14,10},{7,3},{... | collective-permute-start | bytes 1179656 | tf_op jit(solution)/shard_map/ppermute | solution.py:1134
  389.0 65.0 %all-to-all-start.4 = ((bf16[8,2,48,768]{3,2,1,0:T(8,128)(2,1)}), bf16[8,2,48,768]{3,2,1,0:T(8,128)(2,1)S(1)}, u32[]{:S(2)}, u32[]{:S(2)}) async-start(bf16[8,2,48,768]{3,2,1,0:T(8,128)(2,1)} %bitcast.63), calls=%async_computation.5 | async-start | bytes 2359296 | tf_op jit(solution)/shard_map/all_to_all | solution.py:836
  403.1 28.6 %collective-permute-start.16 = (bf16[384,512]{1,0:T(8,128)(2,1)S(1)}, bf16[384,512]{1,0:T(8,128)(2,1)S(1)}, u32[]{:S(2)}, u32[]{:S(2)}) collective-permute-start(bf16[384,512]{1,0:T(8,128)(2,1)S(1)} %get-tuple-element.134), channel_id=1, source_target_pairs={{4,0},{8,4},{12,8},{5,1},{9,5},{13,9},{6,2},{10,6},{14,10},{7,3},{... | collective-permute-start | bytes 1179656 | tf_op jit(solution)/shard_map/ppermute | solution.py:1134
  404.4 34.8 %collective-permute-start.17 = (bf16[384,512]{1,0:T(8,128)(2,1)S(1)}, bf16[384,512]{1,0:T(8,128)(2,1)S(1)}, u32[]{:S(2)}, u32[]{:S(2)}) collective-permute-start(bf16[384,512]{1,0:T(8,128)(2,1)S(1)} %get-tuple-element.135), channel_id=1, source_target_pairs={{4,0},{8,4},{12,8},{5,1},{9,5},{13,9},{6,2},{10,6},{14,10},{7,3},{... | collective-permute-start | bytes 1179656 | tf_op jit(solution)/shard_map/ppermute | solution.py:1134
  441.2 19.8 %collective-permute-start.18 = (bf16[384,512]{1,0:T(8,128)(2,1)S(1)}, bf16[384,512]{1,0:T(8,128)(2,1)}, u32[]{:S(2)}, u32[]{:S(2)}) collective-permute-start(bf16[384,512]{1,0:T(8,128)(2,1)S(1)} %get-tuple-element.138), channel_id=1, source_target_pairs={{4,0},{8,4},{12,8},{5,1},{9,5},{13,9},{6,2},{10,6},{14,10},{7,3},{... | collective-permute-start | bytes 1179656 | tf_op jit(solution)/shard_map/ppermute | solution.py:1134
  442.5 25.6 %collective-permute-start.19 = (bf16[384,512]{1,0:T(8,128)(2,1)S(1)}, bf16[384,512]{1,0:T(8,128)(2,1)}, u32[]{:S(2)}, u32[]{:S(2)}) collective-permute-start(bf16[384,512]{1,0:T(8,128)(2,1)S(1)} %get-tuple-element.139), channel_id=1, source_target_pairs={{4,0},{8,4},{12,8},{5,1},{9,5},{13,9},{6,2},{10,6},{14,10},{7,3},{... | collective-permute-start | bytes 1179656 | tf_op jit(solution)/shard_map/ppermute | solution.py:1134
  483.3 37.5 %all-to-all-start.5 = ((bf16[8,96,896]{2,1,0:T(8,128)(2,1)}), bf16[8,96,896]{2,1,0:T(8,128)(2,1)}, u32[]{:S(2)}, u32[]{:S(2)}) async-start(bf16[8,96,896]{2,1,0:T(8,128)(2,1)} %concatenate.111), calls=%async_computation.6 | async-start | bytes 2752512 | tf_op jit(solution)/shard_map/all_to_all | solution.py:836
  492.2 19.0 %collective-permute-start.25 = (bf16[2,1,128,768]{3,2,0,1:T(8,128)(2,1)S(1)}, bf16[2,1,128,768]{3,2,0,1:T(8,128)(2,1)S(1)}, u32[]{:S(2)}, u32[]{:S(2)}) collective-permute-start(bf16[2,1,128,768]{3,2,0,1:T(8,128)(2,1)S(1)} %constant_dynamic-slice_fusion), channel_id=1, source_target_pairs={{0,2},{1,3},{2,0},{3,1},{4,6},{5,7},{6,4},{7,5},{8,10},{9,11},{10,... | collective-permute-start | bytes 1179656 | tf_op jit(solution)/shard_map/ppermute | solution.py:811
  494.0 30.8 %collective-permute-start.21 = (bf16[2,1,128,768]{3,2,0,1:T(8,128)(2,1)S(1)}, bf16[2,1,128,768]{3,2,0,1:T(8,128)(2,1)}, u32[]{:S(2)}, u32[]{:S(2)}) collective-permute-start(bf16[2,1,128,768]{3,2,0,1:T(8,128)(2,1)S(1)} %constant_dynamic-slice_fusion.4), channel_id=1, source_target_pairs={{0,2},{1,3},{2,0},{3,1},{4,6},{5,7},{6,4},{7,5},{8,10},{9,11},{10,... | collective-permute-start | bytes 1179656 | tf_op jit(solution)/shard_map/ppermute | solution.py:811
  520.8 57.2 %all-to-all-start.6 = ((bf16[8,3,96,512]{3,2,1,0:T(8,128)(2,1)}), bf16[8,3,96,512]{3,2,1,0:T(8,128)(2,1)S(1)}, u32[]{:S(2)}, u32[]{:S(2)}) async-start(bf16[8,3,96,512]{3,2,1,0:T(8,128)(2,1)} %bitcast.270), calls=%async_computation.8 | async-start | bytes 4718592 | tf_op jit(solution)/shard_map/all_to_all | solution.py:836
  528.7 16.3 %collective-permute-start.22 = (bf16[1,2,128,768]{3,2,1,0:T(8,128)(2,1)S(1)}, bf16[1,2,128,768]{3,2,1,0:T(8,128)(2,1)S(1)}, u32[]{:S(2)}, u32[]{:S(2)}) collective-permute-start(bf16[1,2,128,768]{3,2,1,0:T(8,128)(2,1)S(1)} %get-tuple-element.214), channel_id=1, source_target_pairs={{0,2},{1,3},{2,0},{3,1},{4,6},{5,7},{6,4},{7,5},{8,10},{9,11},{10,... | collective-permute-start | bytes 1179656 | tf_op jit(solution)/shard_map/ppermute | solution.py:811
  (75 other events, 655.3 us)
Sparse Core Ops, SparseCore 0:
  21.4 69.9 all-gather.3
  93.5 63.3 all-gather.5
  229.5 52.8 all-gather.7
  339.9 84.9 reduce-scatter.2
  427.4 84.0 reduce-scatter.4

commit v6 on v5

--- a/solution.py
+++ b/solution.py
@@ -1157,7 +1157,6 @@
     first_part = by_rows(
         jnp.einsum("bht,dh->btd", mapped_grad, project_all, preferred_element_type=f32)
     ).astype(bf16)
-    first_part, mapped_grad = tied(first_part, mapped_grad)
     first_grad = add_shards(first_part)
     project_part = by_rows(
         jnp.einsum("btd,bht->dh", first_in, mapped_grad, preferred_element_type=f32)
@@ -1177,16 +1176,18 @@
     )
 
 
-    small_parts = jnp.concatenate(
+    early_width = part_width + EXPERTS + 1
+    early_width += -early_width % 128
+    early_parts = jnp.concatenate(
         [
-            project_part,
             mixing_part,
             router_part,
             gain_two[:, None],
-            jnp.zeros((model_width, -(4 * part_width + EXPERTS + 1) % 128), f32),
+            jnp.zeros((model_width, early_width - part_width - EXPERTS - 1), f32),
         ],
         1,
     ).astype(bf16)
+    small_parts = jnp.concatenate([early_parts, project_part.astype(bf16)], 1)
     small_home = route(small_parts.reshape(group_size, owned, -1))
     small_home, expert_own = tied(small_home, expert_own)
     expert_grads = route(expert_own).astype(f32)
@@ -1197,10 +1198,10 @@
         0,
     )
     project_grad = (
-        small_grads[:, : 3 * part_width].reshape(owned, 3, part_width).transpose(1, 0, 2)
-    )
-    mixing_grad = small_grads[:, 3 * part_width : 4 * part_width].T
-    rest = small_grads[:, 4 * part_width : 4 * part_width + EXPERTS + 1]
+        small_grads[:, early_width:].reshape(owned, 3, part_width).transpose(1, 0, 2)
+    )
+    mixing_grad = small_grads[:, :part_width].T
+    rest = small_grads[:, part_width : part_width + EXPERTS + 1]
     gain_one = jnp.sum(project_grad * project.astype(f32), (0, 2)) / norm_gains[0].astype(f32)
     tiny = lax.psum(
         jnp.concatenate([rest.T, gain_one[None]], 0),

time: 599 us -> 600 us (level)
    unnamed x128 -> x134, local copies, waits for them, and re-layouts: 14.1 us -> 14.4 us
  transfers between devices with their start and end apart: 40 -> 40, of which waited for: 26 -> 27; matrix products, arithmetic and copies ran while one was open for 17% -> 17% of each run, Pallas kernels for 14% -> 14%
where the time goes in v6:
time: 600 us; the launch traced here: 592 us
  waiting for transfers between devices  272 us (45%)
  Pallas kernels  98.5 us (16%)
  starting transfers between devices  74.8 us (12%)
  other arithmetic  51.1 us (9%)
  local copies, waits for them, and re-layouts  42.8 us (7%)
  matrix products  30.7 us (5%)
  between operations  15.7 us (3%)
  blocking collectives  6.55 us (1%)
    all_to_all x7, waiting for transfers between devices, route(): return lax.all_to_all(blocks, GROUP, split_axis=0, concat_axis=0)  154 us
    ppermute x16, waiting for transfers between devices, swap(): return lax.ppermute(piece, axes, [(i, i ^ step) for i in range(size)])  57.8 us
    ppermute x6, waiting for transfers between devices, local_fast(): lax.ppermute(grads.astype(bf16), SEQ, [(i + 1, i) for i in range(seq_size...  38.8 us
    pallas_call x2, Pallas kernels, gated(): pl.pallas_call(gated_kernel, grid=(chunks * tiles,), out_shape=(field, fi...  38.5 us
    all_to_all x7, starting transfers between devices, route(): return lax.all_to_all(blocks, GROUP, split_axis=0, concat_axis=0)  37.3 us
    pallas_call x8, Pallas kernels, attend_call(): pl.pallas_call(kernel, grid=(trees,), out_shape=results, in_specs=[pl.Blo...  34.1 us
    pallas_call x2, Pallas kernels, weight_parts(): pl.pallas_call(parts_kernel, grid=(chunks * tiles,), out_shape=jax.ShapeD...  25.9 us
    ppermute x6, waiting for transfers between devices, local_fast(): lax.ppermute(link, SEQ, [(i, i + 1) for i in range(seq_size - 1)])  19.6 us
  transfers between devices with their start and end apart: 40, of which 27 were waited for; matrix products, arithmetic and copies ran while one was open for 17% of the time, Pallas kernels for 14%

profile of v6, /device:TPU:0, one launch (start us, length us, event | category | flops | bytes accessed | tf_op | source)
XLA Modules:
  0.0 592.2 jit_solution(10027500289334460417)
XLA Ops:
  10.5 7.4 %all-to-all-start = ((bf16[8,3,96,512]{3,2,1,0:T(8,128)(2,1)}), bf16[8,3,96,512]{3,2,1,0:T(8,128)(2,1)S(1)}, u32[]{:S(2)}, u32[]{:S(2)}) async-start(bf16[8,3,96,512]{3,2,1,0:T(8,128)(2,1)} %pad_maximum_fusion), calls=%async_computation | async-start | bytes 4718592 | tf_op jit(solution)/shard_map/all_to_all | solution.py:836
  19.2 64.0 %all-to-all-done = bf16[8,3,96,512]{3,2,1,0:T(8,128)(2,1)S(1)} async-done(((bf16[8,3,96,512]{3,2,1,0:T(8,128)(2,1)}), bf16[8,3,96,512]{3,2,1,0:T(8,128)(2,1)S(1)}, u32[]{:S(2)}, u32[]{:S(2)}) %all-to-all-start) | async-done | bytes 2359328 | tf_op jit(solution)/shard_map/all_to_all | solution.py:836
  104.5 6.2 %attend.4 = (f32[2,3,512]{2,1,0:T(4,128)}, f32[2,3,512]{2,1,0:T(4,128)}, f32[2,192,512]{2,1,0:T(8,128)}) custom-call(s32[1]{0:T(128)} %bitcast.place_ref, bf16[2,192,512]{2,1,0:T(8,128)(2,1)} %bitcast.286, s32[2,2048,1]{2,1,0:T(8,128)} %copy.269.key_bits_ref, s32[2,1,512]{2,1,0:T(1,128)} %broadcast_in_dim.176.query_bits_ref, ...), custom_call_target="tpu_custom_call" | custom-call | flops 1610612736 | bytes 3145728 | tf_op jit(solution)/shard_map/attend/pallas_call | solution.py:642
  154.6 6.4 %all-to-all-start.1 = ((bf16[8,2,48,768]{3,2,1,0:T(8,128)(2,1)}), bf16[8,2,48,768]{3,2,1,0:T(8,128)(2,1)S(1)}, u32[]{:S(2)}, u32[]{:S(2)}) async-start(bf16[8,2,48,768]{3,2,1,0:T(8,128)(2,1)} %bitcast.253), calls=%async_computation.1 | async-start | bytes 2359296 | tf_op jit(solution)/shard_map/all_to_all | solution.py:836
  170.0 5.6 collective-permute-done.6
  181.9 6.1 %all-to-all-done.1 = bf16[8,2,48,768]{3,2,1,0:T(8,128)(2,1)S(1)} async-done(((bf16[8,2,48,768]{3,2,1,0:T(8,128)(2,1)}), bf16[8,2,48,768]{3,2,1,0:T(8,128)(2,1)S(1)}, u32[]{:S(2)}, u32[]{:S(2)}) %all-to-all-start.1) | async-done | bytes 1179680 | tf_op jit(solution)/shard_map/all_to_all | solution.py:836
  200.3 29.2 %all-to-all-done.2 = bf16[8,2,48,768]{3,2,1,0:T(8,128)(2,1)S(1)} async-done(((bf16[8,2,48,768]{3,2,1,0:T(8,128)(2,1)}), bf16[8,2,48,768]{3,2,1,0:T(8,128)(2,1)S(1)}, u32[]{:S(2)}, u32[]{:S(2)}) %all-to-all-start.2) | async-done | bytes 1179680 | tf_op jit(solution)/shard_map/all_to_all | solution.py:836
  232.5 25.8 %gated.2 = (f32[768,768]{1,0:T(8,128)}, f32[768,768]{1,0:T(8,128)}, bf16[768,2048]{1,0:T(8,128)(2,1)}, bf16[768,2048]{1,0:T(8,128)(2,1)}, bf16[768,2048]{1,0:T(8,128)(2,1)}) custom-call(bf16[768,768]{1,0:T(8,128)(2,1)} %bitcast.251, bf16[768,768]{1,0:T(8,128)(2,1)} %fusion.1.grads_ref, bf16[4,3,768,512]{3,2,1,0:T(8,128)(2,1)} %all-gather.6.cloned.1.call-done.weights_ref), custom_call_target="tpu_custom_call" | custom-call | flops 14495514624 | bytes 25952256 | tf_op jit(solution)/shard_map/gated/pallas_call | solution.py:740
  267.5 39.7 %all-to-all-done.3 = bf16[8,2,48,896]{3,2,1,0:T(8,128)(2,1)S(1)} async-done(((bf16[8,2,48,896]{3,2,1,0:T(8,128)(2,1)}), bf16[8,2,48,896]{3,2,1,0:T(8,128)(2,1)S(1)}, u32[]{:S(2)}, u32[]{:S(2)}) %all-to-all-start.3) | async-done | bytes 1376288 | tf_op jit(solution)/shard_map/all_to_all | solution.py:836
  307.3 12.7 %gated.3 = (f32[1024,768]{1,0:T(8,128)}, f32[1024,768]{1,0:T(8,128)}, bf16[1024,512]{1,0:T(8,128)(2,1)}, bf16[1024,512]{1,0:T(8,128)(2,1)}, bf16[1024,512]{1,0:T(8,128)(2,1)}) custom-call(bf16[1024,768]{1,0:T(8,128)(2,1)} %bitcast.258, bf16[1024,768]{1,0:T(8,128)(2,1)} %bitcast.284, bf16[1,3,768,512]{3,2,1,0:T(8,128)(2,1)} %bitcast.297), custom_call_target="tpu_custom_call" | custom-call | flops 4831838208 | bytes 14942208 | tf_op jit(solution)/shard_map/gated/pallas_call | solution.py:740
  327.7 8.5 %weight_parts.2 = bf16[1,8,3,96,512]{4,3,2,1,0:T(8,128)(2,1)} custom-call(bf16[1024,768]{1,0:T(8,128)(2,1)} %bitcast.259, bf16[1024,768]{1,0:T(8,128)(2,1)} %bitcast.285, bf16[1024,512]{1,0:T(8,128)(2,1)} %get-tuple-element.114.first_ref, bf16[1024,512]{1,0:T(8,128)(2,1)} %get-tuple-element.115.second_ref, bf16[1024,512]{1,0:T(8,128)(2,1)} %get-tuple-element.116.active_ref), custom_call_target="tpu_custom_call" | custom-call | flops 2415919104 | bytes 8650752 | tf_op jit(solution)/shard_map/weight_parts/pallas_call | solution.py:791
  348.3 8.9 %collective-permute-done.12 = bf16[1,2,128,768]{3,2,1,0:T(8,128)(2,1)S(1)} collective-permute-done((bf16[1,2,128,768]{3,2,1,0:T(8,128)(2,1)S(1)}, bf16[1,2,128,768]{3,2,1,0:T(8,128)(2,1)S(1)}, u32[]{:S(2)}, u32[]{:S(2)}) %collective-permute-start.12) | collective-permute-done | bytes 393248 | tf_op jit(solution)/shard_map/ppermute | solution.py:811
  370.1 17.4 %weight_parts.3 = bf16[4,8,3,96,512]{4,3,2,1,0:T(8,128)(2,1)} custom-call(bf16[768,768]{1,0:T(8,128)(2,1)} %bitcast.252, bf16[768,768]{1,0:T(8,128)(2,1)} %fusion.1.grads_ref, bf16[768,2048]{1,0:T(8,128)(2,1)} %get-tuple-element.124.first_ref, bf16[768,2048]{1,0:T(8,128)(2,1)} %get-tuple-element.125.second_ref, bf16[768,2048]{1,0:T(8,128)(2,1)} %get-tuple-element.126.active_ref), custom_call_target="tpu_custom_call" | custom-call | flops 7247757312 | bytes 21233664 | tf_op jit(solution)/shard_map/weight_parts/pallas_call | solution.py:791
  389.1 5.4 all-to-all-start.4
  411.8 20.0 %collective-permute-done.16 = bf16[384,512]{1,0:T(8,128)(2,1)S(1)} collective-permute-done((bf16[384,512]{1,0:T(8,128)(2,1)S(1)}, bf16[384,512]{1,0:T(8,128)(2,1)S(1)}, u32[]{:S(2)}, u32[]{:S(2)}) %collective-permute-start.16) | collective-permute-done | bytes 393248 | tf_op jit(solution)/shard_map/ppermute | solution.py:1134
  431.8 7.6 %collective-permute-done.17 = bf16[384,512]{1,0:T(8,128)(2,1)S(1)} collective-permute-done((bf16[384,512]{1,0:T(8,128)(2,1)S(1)}, bf16[384,512]{1,0:T(8,128)(2,1)S(1)}, u32[]{:S(2)}, u32[]{:S(2)}) %collective-permute-start.17) | collective-permute-done | bytes 393248 | tf_op jit(solution)/shard_map/ppermute | solution.py:1134
  445.0 8.4 %attend_back.7 = (f32[2,192,512]{2,1,0:T(8,128)}, f32[2,384,512]{2,1,0:T(8,128)}) custom-call(s32[1]{0:T(128)} %bitcast.place_ref, bf16[2,192,512]{2,1,0:T(8,128)(2,1)} %bitcast.293, bf16[2,192,512]{2,1,0:T(8,128)(2,1)} %get-tuple-element.100.out_ref, bf16[2,192,512]{2,1,0:T(8,128)(2,1)} %fusion.8.grad_ref, f32[2,3,512]{2,1,0:T(4,128)} %get-tuple-element.118.log_ref, ...), custom_call_target="tpu_custom_call" | custom-call | flops 4026531840 | bytes 3145728 | tf_op jit(solution)/shard_map/attend_back/pallas_call | solution.py:642
  462.2 7.3 %collective-permute-done.19 = bf16[384,512]{1,0:T(8,128)(2,1)} collective-permute-done((bf16[384,512]{1,0:T(8,128)(2,1)}, bf16[384,512]{1,0:T(8,128)(2,1)}, u32[]{:S(2)}, u32[]{:S(2)}) %collective-permute-start.19) | collective-permute-done | bytes 393248 | tf_op jit(solution)/shard_map/ppermute | solution.py:1134
  496.4 17.0 %collective-permute-done.25 = bf16[2,1,128,768]{3,2,0,1:T(8,128)(2,1)S(1)} collective-permute-done((bf16[2,1,128,768]{3,2,0,1:T(8,128)(2,1)S(1)}, bf16[2,1,128,768]{3,2,0,1:T(8,128)(2,1)S(1)}, u32[]{:S(2)}, u32[]{:S(2)}) %collective-permute-start.25) | collective-permute-done | bytes 393248 | tf_op jit(solution)/shard_map/ppermute | solution.py:811
  521.4 5.5 all-to-all-start.6
  531.5 10.0 %collective-permute-done.26 = bf16[1,2,128,768]{3,2,1,0:T(8,128)(2,1)S(1)} collective-permute-done((bf16[1,2,128,768]{3,2,1,0:T(8,128)(2,1)S(1)}, bf16[1,2,128,768]{3,2,1,0:T(8,128)(2,1)S(1)}, u32[]{:S(2)}, u32[]{:S(2)}) %collective-permute-start.26) | collective-permute-done | bytes 393248 | tf_op jit(solution)/shard_map/ppermute | solution.py:811
  542.6 5.5 collective-permute-done.22
  562.6 6.6 %psum.7 = f32[10,96]{1,0:T(8,128)S(1)} all-reduce(f32[10,96]{1,0:T(8,128)S(1)} %pad_maximum_fusion.26), channel_id=1, replica_groups=mesh['dp'=2,'seq'=4,'tensor'=4] {'tensor'}, use_global_device_ids=true, to_apply=%region_23.24 | all-reduce | flops 960 | bytes 7680 | tf_op jit(solution)/shard_map/psum | solution.py:1206
  571.1 10.0 %all-to-all-done.6 = bf16[8,3,96,512]{3,2,1,0:T(8,128)(2,1)S(1)} async-done(((bf16[8,3,96,512]{3,2,1,0:T(8,128)(2,1)}), bf16[8,3,96,512]{3,2,1,0:T(8,128)(2,1)S(1)}, u32[]{:S(2)}, u32[]{:S(2)}) %all-to-all-start.6) | async-done | bytes 2359328 | tf_op jit(solution)/shard_map/all_to_all | solution.py:836
  (351 shorter events, 235.3 us)
Async XLA Ops:
  10.5 72.7 %all-to-all-start = ((bf16[8,3,96,512]{3,2,1,0:T(8,128)(2,1)}), bf16[8,3,96,512]{3,2,1,0:T(8,128)(2,1)S(1)}, u32[]{:S(2)}, u32[]{:S(2)}) async-start(bf16[8,3,96,512]{3,2,1,0:T(8,128)(2,1)} %pad_maximum_fusion), calls=%async_computation | async-start | bytes 4718592 | tf_op jit(solution)/shard_map/all_to_all | solution.py:836
  17.9 76.7 %all-gather.4.cloned.1.call-start = ((), (), s32[]{:S(2)}) async-start(), calls=%async_computation.9 | async-start | bytes 1548288 | tf_op jit(solution)/shard_map/all_gather | solution.py:926
  19.1 144.9 %all-gather.6.cloned.1.call-start = ((), (), s32[]{:S(2)}) async-start(), calls=%async_computation.10 | async-start | bytes 11796480 | tf_op jit(solution)/shard_map/all_gather | solution.py:1016
  100.5 15.6 %collective-permute-start.1 = (bf16[1,384,512]{2,1,0:T(8,128)(2,1)S(1)}, bf16[1,384,512]{2,1,0:T(8,128)(2,1)S(1)}, u32[]{:S(2)}, u32[]{:S(2)}) collective-permute-start(bf16[1,384,512]{2,1,0:T(8,128)(2,1)S(1)} %get-tuple-element.249), channel_id=1, source_target_pairs={{0,4},{4,8},{8,12},{1,5},{5,9},{9,13},{2,6},{6,10},{10,14},{3,7},{... | collective-permute-start | bytes 1179656 | tf_op jit(solution)/shard_map/ppermute | solution.py:993
  120.5 14.8 %collective-permute-start.3 = (bf16[1,384,512]{2,1,0:T(8,128)(2,1)S(1)}, bf16[1,384,512]{2,1,0:T(8,128)(2,1)S(1)}, u32[]{:S(2)}, u32[]{:S(2)}) collective-permute-start(bf16[1,384,512]{2,1,0:T(8,128)(2,1)S(1)} %collective-permute-done.1), channel_id=1, source_target_pairs={{0,4},{4,8},{8,12},{1,5},{5,9},{9,13},{2,6},{6,10},{10,14},{3,7},{... | collective-permute-start | bytes 1179656 | tf_op jit(solution)/shard_map/ppermute | solution.py:993
  139.7 14.0 %collective-permute-start.5 = (bf16[1,384,512]{2,1,0:T(8,128)(2,1)S(1)}, bf16[1,384,512]{2,1,0:T(8,128)(2,1)S(1)}, u32[]{:S(2)}, u32[]{:S(2)}) collective-permute-start(bf16[1,384,512]{2,1,0:T(8,128)(2,1)S(1)} %collective-permute-done.3), channel_id=1, source_target_pairs={{0,4},{4,8},{8,12},{1,5},{5,9},{9,13},{2,6},{6,10},{10,14},{3,7},{... | collective-permute-start | bytes 1179656 | tf_op jit(solution)/shard_map/ppermute | solution.py:993
  154.6 33.4 %all-to-all-start.1 = ((bf16[8,2,48,768]{3,2,1,0:T(8,128)(2,1)}), bf16[8,2,48,768]{3,2,1,0:T(8,128)(2,1)S(1)}, u32[]{:S(2)}, u32[]{:S(2)}) async-start(bf16[8,2,48,768]{3,2,1,0:T(8,128)(2,1)} %bitcast.253), calls=%async_computation.1 | async-start | bytes 2359296 | tf_op jit(solution)/shard_map/all_to_all | solution.py:836
  195.4 34.0 %all-to-all-start.2 = ((bf16[8,2,48,768]{3,2,1,0:T(8,128)(2,1)}), bf16[8,2,48,768]{3,2,1,0:T(8,128)(2,1)S(1)}, u32[]{:S(2)}, u32[]{:S(2)}) async-start(bf16[8,2,48,768]{3,2,1,0:T(8,128)(2,1)} %bitcast.255), calls=%async_computation.2 | async-start | bytes 2359296 | tf_op jit(solution)/shard_map/all_to_all | solution.py:836
  199.4 107.9 %all-gather.8.cloned.1.call-start = ((), (), s32[]{:S(2)}) async-start(), calls=%async_computation.11 | async-start | bytes 2654208 | tf_op jit(solution)/shard_map/all_gather | solution.py:1032
  263.6 43.5 %all-to-all-start.3 = ((bf16[8,2,48,896]{3,2,1,0:T(8,128)(2,1)}), bf16[8,2,48,896]{3,2,1,0:T(8,128)(2,1)S(1)}, u32[]{:S(2)}, u32[]{:S(2)}) async-start(bf16[8,2,48,896]{3,2,1,0:T(8,128)(2,1)} %bitcast.35), calls=%async_computation.3 | async-start | bytes 2752512 | tf_op jit(solution)/shard_map/all_to_all | solution.py:836
  267.2 203.9 %reduce-scatter.3.cloned.1.call-start = ((), (), s32[]{:S(2)}) async-start(), calls=%async_computation.12 | async-start | bytes 2654208 | tf_op jit(solution)/shard_map/reduce_scatter | solution.py:1127
  339.9 181.5 %reduce-scatter.5.cloned.1.call-start = ((), (), s32[]{:S(2)}) async-start(), calls=%async_computation.13 | async-start | bytes 11796480 | tf_op jit(solution)/shard_map/reduce_scatter | solution.py:1139
  367.5 20.0 %collective-permute-start.14 = (bf16[384,512]{1,0:T(8,128)(2,1)S(1)}, bf16[384,512]{1,0:T(8,128)(2,1)S(1)}, u32[]{:S(2)}, u32[]{:S(2)}) collective-permute-start(bf16[384,512]{1,0:T(8,128)(2,1)S(1)} %get-tuple-element.248), channel_id=1, source_target_pairs={{4,0},{8,4},{12,8},{5,1},{9,5},{13,9},{6,2},{10,6},{14,10},{7,3},{... | collective-permute-start | bytes 1179656 | tf_op jit(solution)/shard_map/ppermute | solution.py:1134
  368.8 20.2 %collective-permute-start.15 = (bf16[384,512]{1,0:T(8,128)(2,1)S(1)}, bf16[384,512]{1,0:T(8,128)(2,1)S(1)}, u32[]{:S(2)}, u32[]{:S(2)}) collective-permute-start(bf16[384,512]{1,0:T(8,128)(2,1)S(1)} %get-tuple-element.247), channel_id=1, source_target_pairs={{4,0},{8,4},{12,8},{5,1},{9,5},{13,9},{6,2},{10,6},{14,10},{7,3},{... | collective-permute-start | bytes 1179656 | tf_op jit(solution)/shard_map/ppermute | solution.py:1134
  389.1 66.4 %all-to-all-start.4 = ((bf16[8,2,48,768]{3,2,1,0:T(8,128)(2,1)}), bf16[8,2,48,768]{3,2,1,0:T(8,128)(2,1)S(1)}, u32[]{:S(2)}, u32[]{:S(2)}) async-start(bf16[8,2,48,768]{3,2,1,0:T(8,128)(2,1)} %bitcast.63), calls=%async_computation.5 | async-start | bytes 2359296 | tf_op jit(solution)/shard_map/all_to_all | solution.py:836
  403.0 28.8 %collective-permute-start.16 = (bf16[384,512]{1,0:T(8,128)(2,1)S(1)}, bf16[384,512]{1,0:T(8,128)(2,1)S(1)}, u32[]{:S(2)}, u32[]{:S(2)}) collective-permute-start(bf16[384,512]{1,0:T(8,128)(2,1)S(1)} %get-tuple-element.132), channel_id=1, source_target_pairs={{4,0},{8,4},{12,8},{5,1},{9,5},{13,9},{6,2},{10,6},{14,10},{7,3},{... | collective-permute-start | bytes 1179656 | tf_op jit(solution)/shard_map/ppermute | solution.py:1134
  404.3 35.1 %collective-permute-start.17 = (bf16[384,512]{1,0:T(8,128)(2,1)S(1)}, bf16[384,512]{1,0:T(8,128)(2,1)S(1)}, u32[]{:S(2)}, u32[]{:S(2)}) collective-permute-start(bf16[384,512]{1,0:T(8,128)(2,1)S(1)} %get-tuple-element.133), channel_id=1, source_target_pairs={{4,0},{8,4},{12,8},{5,1},{9,5},{13,9},{6,2},{10,6},{14,10},{7,3},{... | collective-permute-start | bytes 1179656 | tf_op jit(solution)/shard_map/ppermute | solution.py:1134
  442.4 19.8 %collective-permute-start.18 = (bf16[384,512]{1,0:T(8,128)(2,1)}, bf16[384,512]{1,0:T(8,128)(2,1)}, u32[]{:S(2)}, u32[]{:S(2)}) collective-permute-start(bf16[384,512]{1,0:T(8,128)(2,1)} %get-tuple-element.136), channel_id=1, source_target_pairs={{4,0},{8,4},{12,8},{5,1},{9,5},{13,9},{6,2},{10,6},{14,10},{7,3},{... | collective-permute-start | bytes 1179656 | tf_op jit(solution)/shard_map/ppermute | solution.py:1134
  443.7 25.8 %collective-permute-start.19 = (bf16[384,512]{1,0:T(8,128)(2,1)}, bf16[384,512]{1,0:T(8,128)(2,1)}, u32[]{:S(2)}, u32[]{:S(2)}) collective-permute-start(bf16[384,512]{1,0:T(8,128)(2,1)} %get-tuple-element.137), channel_id=1, source_target_pairs={{4,0},{8,4},{12,8},{5,1},{9,5},{13,9},{6,2},{10,6},{14,10},{7,3},{... | collective-permute-start | bytes 1179656 | tf_op jit(solution)/shard_map/ppermute | solution.py:1134
  482.2 37.7 %all-to-all-start.5 = ((bf16[8,96,832]{2,1,0:T(8,128)(2,1)}), bf16[8,96,832]{2,1,0:T(8,128)(2,1)}, u32[]{:S(2)}, u32[]{:S(2)}) async-start(bf16[8,96,832]{2,1,0:T(8,128)(2,1)} %bitcast.247), calls=%async_computation.6 | async-start | bytes 2752512 | tf_op jit(solution)/shard_map/all_to_all | solution.py:836
  493.0 20.4 %collective-permute-start.25 = (bf16[2,1,128,768]{3,2,0,1:T(8,128)(2,1)S(1)}, bf16[2,1,128,768]{3,2,0,1:T(8,128)(2,1)S(1)}, u32[]{:S(2)}, u32[]{:S(2)}) collective-permute-start(bf16[2,1,128,768]{3,2,0,1:T(8,128)(2,1)S(1)} %constant_dynamic-slice_fusion), channel_id=1, source_target_pairs={{0,2},{1,3},{2,0},{3,1},{4,6},{5,7},{6,4},{7,5},{8,10},{9,11},{10,... | collective-permute-start | bytes 1179656 | tf_op jit(solution)/shard_map/ppermute | solution.py:811
  494.6 32.3 %collective-permute-start.21 = (bf16[2,1,128,768]{3,2,0,1:T(8,128)(2,1)S(1)}, bf16[2,1,128,768]{3,2,0,1:T(8,128)(2,1)}, u32[]{:S(2)}, u32[]{:S(2)}) collective-permute-start(bf16[2,1,128,768]{3,2,0,1:T(8,128)(2,1)S(1)} %constant_dynamic-slice_fusion.4), channel_id=1, source_target_pairs={{0,2},{1,3},{2,0},{3,1},{4,6},{5,7},{6,4},{7,5},{8,10},{9,11},{10,... | collective-permute-start | bytes 1179656 | tf_op jit(solution)/shard_map/ppermute | solution.py:811
  521.4 59.7 %all-to-all-start.6 = ((bf16[8,3,96,512]{3,2,1,0:T(8,128)(2,1)}), bf16[8,3,96,512]{3,2,1,0:T(8,128)(2,1)S(1)}, u32[]{:S(2)}, u32[]{:S(2)}) async-start(bf16[8,3,96,512]{3,2,1,0:T(8,128)(2,1)} %bitcast.268), calls=%async_computation.8 | async-start | bytes 4718592 | tf_op jit(solution)/shard_map/all_to_all | solution.py:836
  529.5 18.5 %collective-permute-start.22 = (bf16[1,2,128,768]{3,2,1,0:T(8,128)(2,1)S(1)}, bf16[1,2,128,768]{3,2,1,0:T(8,128)(2,1)S(1)}, u32[]{:S(2)}, u32[]{:S(2)}) collective-permute-start(bf16[1,2,128,768]{3,2,1,0:T(8,128)(2,1)S(1)} %get-tuple-element.210), channel_id=1, source_target_pairs={{0,2},{1,3},{2,0},{3,1},{4,6},{5,7},{6,4},{7,5},{8,10},{9,11},{10,... | collective-permute-start | bytes 1179656 | tf_op jit(solution)/shard_map/ppermute | solution.py:811
  (78 other events, 676.9 us)
Sparse Core Ops, SparseCore 0:
  21.4 69.9 all-gather.3
  93.5 63.3 all-gather.5
  229.6 52.8 all-gather.7
  340.0 85.3 reduce-scatter.2
  427.8 93.4 reduce-scatter.4
